TPU v7x, 512 devices: a whole 4x8x8 slice. The times are simulated.
512 devices in a mesh: rows: 128 (over y, z, core), cols: 4 (over x).
Axes of the slice: x: 4, y: 8, z: 8, core: 2. Of those that a mesh axis runs over, the one named last changes fastest.
Arguments:
- tile_values: float32 [1920, 256, 256], P('rows'), may hold values from -0.09375 to 0.09375, as said below
- tile_rows: int32 [1920], P('rows'), may hold values from 0 to 1
- tile_cols: int32 [1920], P('rows'), may hold values from -1 to 255, as said below
- start_vectors: float32 [128, 65536], P('cols', 'rows'), may hold values from -6 to 6
Outputs:
- vectors: float32 [128, 65536], P('cols', 'rows')
- images: float32 [128, 65536], P('cols', 'rows')
Inputs may be any that keep to these rules, and one draw needn't show every extreme that they name: tile_values lie within the stated bounds. `tile_cols`: if slot s of index p of rows is not empty, its column block lies on index p + s // 3 - 2 of rows, that is in 2 * (p + s // 3 - 2) up to 2 * (p + s // 3 - 1) - 1; slots whose index would fall off the mesh are empty.
All inputs are finite; a program needn't handle non-finite values.
Results may differ from a plain program's by a relative error of at most 0.0001.
Values sent between devices are 32-bit elements; how exact they have to be, the bound alone decides.
No kernel may reach another device: no remote copies, remote signals or barrier semaphores. Data moves between devices by JAX's collectives and lax.ppermute only.
A program may use at most 64 MiB of HBM per device.

v0:
```python
import functools

import jax
import jax.numpy as jnp
from jax import lax
from jax.experimental import pallas as pl
from jax.experimental.pallas import tpu as pltpu
from jax.sharding import Mesh, PartitionSpec as P

REACH = 2
GROUPS = 2 * REACH + 1
ITERS = 3
ROWS = ("y", "z", "core")
MIB = 1 << 20

precise = lax.Precision.HIGHEST


def halves(value):
    high = value.astype(jnp.bfloat16)
    low = (value - high.astype(jnp.float32)).astype(jnp.bfloat16)
    return high, low


def band_kernel(rows_ref, cols_ref, tiles_ref, high_ref, low_ref, total):
    group = pl.program_id(0)
    in_group, size, _ = tiles_ref.shape
    blocks = total.shape[0] // size
    total[...] = jnp.zeros_like(total)
    for s in range(in_group):
        row, col = rows_ref[group * in_group + s], cols_ref[group * in_group + s]

        @pl.when(col >= 0)
        def _():
            at = (
                pl.ds(pl.multiple_of(row * size, size), size),
                pl.ds(pl.multiple_of(lax.rem(col, blocks) * size, size), size),
            )
            total[at] += tiles_ref[s]

    high_ref[0], low_ref[0] = halves(total[...])


def operator_band(tile_values, tile_rows, tile_cols, width):
    slots, size, _ = tile_values.shape
    in_group = slots // GROUPS
    piece = jax.ShapeDtypeStruct((GROUPS, width, width), jnp.bfloat16)
    return pl.pallas_call(
        band_kernel,
        grid_spec=pltpu.PrefetchScalarGridSpec(
            num_scalar_prefetch=2,
            grid=(GROUPS,),
            in_specs=[pl.BlockSpec((in_group, size, size), lambda g, rows, cols: (g, 0, 0))],
            out_specs=[pl.BlockSpec((1, width, width), lambda g, rows, cols: (g, 0, 0))] * 2,
            scratch_shapes=[pltpu.VMEM((width, width), jnp.float32)],
        ),
        out_shape=[piece, piece],
        compiler_params=pltpu.CompilerParams(vmem_limit_bytes=20 * MIB),
        name="operator_band",
    )(tile_rows, tile_cols, tile_values)


def products(high, low, band_high, band_low, dims):
    count = high.shape[0]
    dot = functools.partial(
        lax.dot_general, dimension_numbers=(dims, ((), ())), preferred_element_type=jnp.float32
    )
    both = dot(jnp.concatenate([high, low], axis=0), band_high)
    return both[:count] + both[count:] + dot(high, band_low)


def apply_kernel(core_ref, below, above, own, got, high_hbm, low_hbm, images, kept, crossing, down, up, high, low, sems):
    core = core_ref[0]
    copies = []
    for g in range(GROUPS):
        pair = [
            pltpu.make_async_copy(high_hbm.at[g], high.at[g], sems.at[0, g]),
            pltpu.make_async_copy(low_hbm.at[g], low.at[g], sems.at[1, g]),
        ]
        for copy in pair:
            copy.start()
        copies.append(pair)
    near = [below[...], got[1 - core], own[...], got[core], above[...]]
    total = 0.0
    for g in range(GROUPS):
        for copy in copies[g]:
            copy.wait()
        total = total + products(*halves(near[g]), high[g], low[g], ((1,), (1,)))
    images[...] = total
    parts = halves(total)
    sent = [products(*parts, high[g], low[g], ((1,), (0,))) for g in range(GROUPS)]
    down[...] = sent[0]
    crossing[1 - core] = sent[1]
    kept[...] = sent[2]
    crossing[core] = sent[3]
    up[...] = sent[4]


def apply_operator(core, below, above, own, got, high, low):
    vmem, hbm = pl.BlockSpec(memory_space=pltpu.VMEM), pl.BlockSpec(memory_space=pl.ANY)
    one = jax.ShapeDtypeStruct(own.shape, jnp.float32)
    two = jax.ShapeDtypeStruct(got.shape, jnp.float32)
    return pl.pallas_call(
        apply_kernel,
        in_specs=[pl.BlockSpec(memory_space=pltpu.SMEM)] + [vmem] * 4 + [hbm] * 2,
        out_specs=[vmem] * 5,
        out_shape=[one, one, two, one, one],
        scratch_shapes=[
            pltpu.VMEM(high.shape, high.dtype),
            pltpu.VMEM(low.shape, low.dtype),
            pltpu.SemaphoreType.DMA((2, GROUPS)),
        ],
        compiler_params=pltpu.CompilerParams(vmem_limit_bytes=16 * MIB),
        name="apply_operator",
    )(core, below, above, own, got, high, low)


def gram_kernel(place_ref, all_ref, out_ref, whole):
    total = lax.dot_general(
        all_ref[...],
        all_ref[...],
        (((1,), (1,)), ((), ())),
        precision=precise,
        preferred_element_type=jnp.float32,
    )
    whole[...] = total.reshape(whole.shape)
    few = out_ref.shape[1]
    for k in range(whole.shape[1] // few):

        @pl.when(place_ref[0] == k)
        def _():
            out_ref[...] = whole[:, few * k : few * (k + 1), :]


def gram_share(place, all_vectors, runs, x_count):
    vmem = pl.BlockSpec(memory_space=pltpu.VMEM)
    size = all_vectors.shape[0]
    run = size // runs
    return pl.pallas_call(
        gram_kernel,
        in_specs=[pl.BlockSpec(memory_space=pltpu.SMEM), vmem],
        out_specs=vmem,
        out_shape=jax.ShapeDtypeStruct((runs, run // x_count, size), jnp.float32),
        scratch_shapes=[pltpu.VMEM((runs, run, size), jnp.float32)],
        compiler_params=pltpu.CompilerParams(vmem_limit_bytes=8 * MIB),
        name="gram_share",
    )(place, all_vectors)


def whiten_kernel(place_ref, gram_ref, all_ref, out_ref, zero_ref, inverse_ref, *, scale, panel):
    size = gram_ref.shape[0]
    tall = 8
    zero_ref[...] = jnp.zeros((tall, size), jnp.float32)
    zero = zero_ref[...]
    row = lax.broadcasted_iota(jnp.int32, (tall, size), 0)
    col = lax.broadcasted_iota(jnp.int32, (tall, size), 1)
    count = size // tall
    left = [gram_ref[tall * b : tall * (b + 1), :] for b in range(count)]
    right = [jnp.where(row + tall * b == col, 1.0, 0.0).astype(jnp.float32) for b in range(count)]

    def lane(value, j):
        return jnp.broadcast_to(value[:, j : j + 1], (tall, size))

    def line(value, i):
        return jnp.broadcast_to(value[i : i + 1, :], (tall, size))

    pivots = jnp.ones((tall, size), jnp.float32)
    for j in range(0, size, panel):
        jb, js = divmod(j, tall)
        low = jb if js + panel < tall else jb + 1
        a = [line(left[jb], js + k) for k in range(panel)]
        w = [line(right[jb], js + k) for k in range(panel)]
        c = [[lane(left[b], j + k) for b in range(low, count)] for k in range(panel)]
        s = {(k, i): lane(a[k] + zero, j + i) for k in range(panel) for i in range(k, panel)}
        factors = []
        for k in range(panel):
            inv = 1.0 / s[k, k]
            pivots = jnp.where(row == js + k, s[k, k], pivots)
            for i in range(k + 1, panel):
                f = s[k, i] * inv
                for i2 in range(i, panel):
                    s[i, i2] = s[i, i2] - f * s[k, i2]
                a[i] = a[i] - f * a[k]
                w[i] = w[i] - f * w[k]
            m = [value * inv for value in c[k]]
            factors.append(m)
            for k2 in range(k + 1, panel):
                c[k2] = [y - x * s[k, k2] for x, y in zip(m, c[k2])]
        for n, b in enumerate(range(low, count)):
            da = dw = 0.0
            for k in range(panel):
                m = factors[k][n]
                if b == jb:
                    m = jnp.where(row > js + panel - 1, m, 0.0)
                da = da + m * a[k]
                dw = dw + m * w[k]
            left[b] = left[b] - da
            right[b] = right[b] - dw
        for k in range(1, panel):
            left[jb] = jnp.where(row == js + k, a[k], left[jb])
            right[jb] = jnp.where(row == js + k, w[k], right[jb])
        if js + panel == tall:
            inverse_ref[tall * jb : tall * (jb + 1), :] = right[jb] * (1.0 / jnp.sqrt(pivots))
            pivots = jnp.ones((tall, size), jnp.float32)
    own = out_ref.shape[0]
    rows = inverse_ref[pl.ds(pl.multiple_of(place_ref[0] * own, own), own), :]
    out_ref[...] = scale * jnp.dot(rows, all_ref[...], precision=precise, preferred_element_type=jnp.float32)


def whiten(place, gram, all_vectors, own, scale):
    vmem = pl.BlockSpec(memory_space=pltpu.VMEM)
    size = gram.shape[0]
    return pl.pallas_call(
        functools.partial(whiten_kernel, scale=scale, panel=4),
        in_specs=[pl.BlockSpec(memory_space=pltpu.SMEM), vmem, vmem],
        out_specs=vmem,
        out_shape=jax.ShapeDtypeStruct((own, all_vectors.shape[1]), jnp.float32),
        scratch_shapes=[pltpu.VMEM((8, size), jnp.float32), pltpu.VMEM((size, size), jnp.float32)],
        compiler_params=pltpu.CompilerParams(vmem_limit_bytes=8 * MIB),
        name="whiten",
    )(place, gram, all_vectors)


def shifted(value, steps):
    count = lax.axis_size(ROWS)
    leading, last = (max(0, -steps), min(count, count - steps))
    return lax.ppermute(value, ROWS, [(source, source + steps) for source in range(leading, last)])


def swapped(value):
    return lax.ppermute(value, "core", [(0, 1), (1, 0)])


def spread(value, axes):
    count = lax.axis_size(axes)
    copies = jnp.broadcast_to(value[None], (count, *value.shape))
    return lax.all_to_all(copies, axes, 0, 0)


def summed_gram(place, all_vectors):
    line, x_count = lax.axis_size(("z", "core")), lax.axis_size("x")
    size = all_vectors.shape[0]
    share = gram_share(place, all_vectors, line, x_count)
    few = share.shape[1]
    share = lax.all_to_all(share, ("z", "core"), 0, 0).sum(axis=0)
    run = spread(share, ("y", "x")).reshape(-1, x_count * few, size).sum(axis=0)
    return spread(run, ("z", "core")).reshape(size, size)


def body(tile_values, tile_rows, tile_cols, start_vectors):
    local_cols, row_width = start_vectors.shape
    all_count = local_cols * lax.axis_size("x")
    scale = (row_width * lax.axis_size(ROWS)) ** 0.5
    core = lax.axis_index("core").astype(jnp.int32)
    first = core == 0
    place = lax.axis_index("x").astype(jnp.int32).reshape(1)
    core = core.reshape(1)
    high, low = operator_band(tile_values, tile_rows, tile_cols, row_width)
    vectors = start_vectors
    for iteration in range(ITERS):
        below, above = shifted(vectors, 2), shifted(vectors, -2)
        got = swapped(jnp.stack([vectors, jnp.where(first, above, below)]))
        images, kept, crossing, down, up = apply_operator(core, below, above, vectors, got, high, low)
        got = swapped(crossing)
        up = jnp.where(first, up + got[1], up)
        down = jnp.where(first, down, down + got[1])
        pulled = kept + got[0] + shifted(up, 2) + shifted(down, -2)
        all_vectors = spread(pulled, "x").reshape(all_count, row_width)
        gram = summed_gram(place, all_vectors)
        vectors = whiten(place, gram, all_vectors, local_cols, scale)
    return (vectors, images)


def solution(mesh):
    split = Mesh(mesh.devices.reshape(8, 8, 2, 4), ("y", "z", "core", "x"))
    return jax.shard_map(
        body,
        mesh=split,
        in_specs=(P(ROWS, None, None), P(ROWS), P(ROWS), P("x", ROWS)),
        out_specs=(P("x", ROWS), P("x", ROWS)),
        check_vma=False,
    )
```

profile of v0, /device:TPU:1, one launch (start us, length us, event | category | flops | bytes accessed | tf_op | source)
XLA Modules:
  0.0 279.4 jit_solution(2175652410813627572)
XLA Ops:
  2.1 5.5 %collective-permute-start = (f32[32,512]{1,0:T(8,128)}, f32[32,512]{1,0:T(8,128)S(1)}, u32[]{:S(2)}, u32[]{:S(2)}) collective-permute-start(f32[32,512]{1,0:T(8,128)} %own.1), channel_id=1, source_target_pairs={{0,8},{4,12},{8,16},{12,20},{16,24},{20,28},{24,32},{28,36},{32,40... | collective-permute-start | bytes 196616 | tf_op jit(solution)/shard_map/ppermute | solution.py:227
  10.0 8.4 %collective-permute-start.2 = (f32[2,32,512]{2,1,0:T(8,128)S(1)}, f32[2,32,512]{2,1,0:T(8,128)S(1)}, u32[]{:S(2)}, u32[]{:S(2)}) collective-permute-start(f32[2,32,512]{2,1,0:T(8,128)S(1)} %pad_maximum_fusion), channel_id=1, source_target_pairs={{0,4},{4,0},{1,5},{5,1},{2,6},{6,2},{3,7},{7,3},{8,12},{12,8},{9,1... | collective-permute-start | bytes 393224 | tf_op jit(solution)/shard_map/ppermute | solution.py:231
  24.0 3.1 %apply_operator.3 = (f32[32,512]{1,0:T(8,128)}, f32[32,512]{1,0:T(8,128)S(1)}, f32[2,32,512]{2,1,0:T(8,128)S(1)}, f32[32,512]{1,0:T(8,128)S(1)}, f32[32,512]{1,0:T(8,128)S(1)}) custom-call(s32[1]{0:T(128)} %bitcast.1.core_ref, f32[32,512]{1,0:T(8,128)S(1)} %collective-permute-done.below, f32[32,512]{1,0:T(8,128)S(1)} %collective-permute-done.1.above, ...), custom_call_target="tpu_custom_call" | custom-call | tf_op jit(solution)/shard_map/apply_operator/pallas_call | solution.py:103
  30.4 3.7 %collective-permute-start.4 = (f32[32,512]{1,0:T(8,128)S(1)}, f32[32,512]{1,0:T(8,128)S(1)}, u32[]{:S(2)}, u32[]{:S(2)}) collective-permute-start(f32[32,512]{1,0:T(8,128)S(1)} %get-tuple-element.36), channel_id=1, source_target_pairs={{0,8},{4,12},{8,16},{12,20},{16,24},{20,28},{24,32},{28,36},{32,40... | collective-permute-start | bytes 196616 | tf_op jit(solution)/shard_map/ppermute | solution.py:227
  35.5 3.7 %collective-permute-done.5 = f32[32,512]{1,0:T(8,128)S(1)} collective-permute-done((f32[32,512]{1,0:T(8,128)S(1)}, f32[32,512]{1,0:T(8,128)S(1)}, u32[]{:S(2)}, u32[]{:S(2)}) %collective-permute-start.5) | collective-permute-done | bytes 65568 | tf_op jit(solution)/shard_map/ppermute | solution.py:227
  40.0 3.4 %all-to-all-start = ((f32[4,32,512]{2,1,0:T(8,128)}), f32[4,32,512]{2,1,0:T(8,128)S(1)}, u32[]{:S(2)}, u32[]{:S(2)}) async-start(f32[4,32,512]{2,1,0:T(8,128)} %broadcast_in_dim.18), calls=%async_computation | async-start | bytes 524288 | tf_op jit(solution)/shard_map/all_to_all | solution.py:237
  43.4 5.5 %all-to-all-done = f32[4,32,512]{2,1,0:T(8,128)S(1)} async-done(((f32[4,32,512]{2,1,0:T(8,128)}), f32[4,32,512]{2,1,0:T(8,128)S(1)}, u32[]{:S(2)}, u32[]{:S(2)}) %all-to-all-start) | async-done | bytes 262176 | tf_op jit(solution)/shard_map/all_to_all | solution.py:237
  49.3 22.0 %all_to_all.60 = f32[16,2,128]{2,1,0:T(2,128)S(1)} all-to-all(f32[16,2,128]{2,1,0:T(2,128)S(1)} %gram_share.3), channel_id=1, replica_groups=mesh['y'=8,'z'=8,'core'=2,'x'=4] {'z','core'}, dimensions={0} | all-to-all | bytes 32768 | tf_op jit(solution)/shard_map/all_to_all | solution.py:245
  71.4 17.9 %all_to_all.61 = f32[32,2,128]{2,1,0:T(2,128)S(1)} all-to-all(f32[32,2,128]{2,1,0:T(2,128)S(1)} %broadcast_in_dim.19), channel_id=1, replica_groups=mesh['y'=8,'z'=8,'core'=2,'x'=4] {'y','x'}, dimensions={0} | all-to-all | bytes 65536 | tf_op jit(solution)/shard_map/all_to_all | solution.py:237
  89.3 12.0 %all_to_all.62 = f32[16,8,128]{2,1,0:T(8,128)S(1)} all-to-all(f32[16,8,128]{2,1,0:T(8,128)S(1)} %broadcast_in_dim.20), channel_id=1, replica_groups=mesh['y'=8,'z'=8,'core'=2,'x'=4] {'z','core'}, dimensions={0} | all-to-all | bytes 131072 | tf_op jit(solution)/shard_map/all_to_all | solution.py:237
  101.3 4.8 %whiten.3.own = f32[32,512]{1,0:T(8,128)S(1)} custom-call(s32[1]{0:T(128)} %bitcast.place_ref, f32[128,128]{1,0:T(8,128)S(1)} %bitcast.78, f32[128,512]{1,0:T(8,128)S(1)} %bitcast.69), custom_call_target="tpu_custom_call" | custom-call | tf_op jit(solution)/shard_map/whiten/pallas_call | solution.py:213
  107.4 4.0 %collective-permute-start.6 = (f32[32,512]{1,0:T(8,128)S(1)}, f32[32,512]{1,0:T(8,128)S(1)}, u32[]{:S(2)}, u32[]{:S(2)}) collective-permute-start(f32[32,512]{1,0:T(8,128)S(1)} %whiten.3.own), channel_id=1, source_target_pairs={{0,8},{4,12},{8,16},{12,20},{16,24},{20,28},{24,32},{28,36},{32,40... | collective-permute-start | bytes 196616 | tf_op jit(solution)/shard_map/ppermute | solution.py:227
  112.8 3.2 %collective-permute-start.8 = (f32[2,32,512]{2,1,0:T(8,128)S(1)}, f32[2,32,512]{2,1,0:T(8,128)S(1)}, u32[]{:S(2)}, u32[]{:S(2)}) collective-permute-start(f32[2,32,512]{2,1,0:T(8,128)S(1)} %pad_maximum_fusion.1), channel_id=1, source_target_pairs={{0,4},{4,0},{1,5},{5,1},{2,6},{6,2},{3,7},{7,3},{8,12},{12,8},{9,1... | collective-permute-start | bytes 393224 | tf_op jit(solution)/shard_map/ppermute | solution.py:231
  118.7 3.1 %apply_operator.4 = (f32[32,512]{1,0:T(8,128)}, f32[32,512]{1,0:T(8,128)S(1)}, f32[2,32,512]{2,1,0:T(8,128)S(1)}, f32[32,512]{1,0:T(8,128)S(1)}, f32[32,512]{1,0:T(8,128)S(1)}) custom-call(s32[1]{0:T(128)} %bitcast.1.core_ref, f32[32,512]{1,0:T(8,128)S(1)} %collective-permute-done.6.below, f32[32,512]{1,0:T(8,128)S(1)} %collective-permute-done.7.above, ...), custom_call_target="tpu_custom_call" | custom-call | tf_op jit(solution)/shard_map/apply_operator/pallas_call | solution.py:103
  121.8 2.3 collective-permute-start.9
  125.1 4.0 %collective-permute-start.10 = (f32[32,512]{1,0:T(8,128)S(1)}, f32[32,512]{1,0:T(8,128)S(1)}, u32[]{:S(2)}, u32[]{:S(2)}) collective-permute-start(f32[32,512]{1,0:T(8,128)S(1)} %get-tuple-element.34), channel_id=1, source_target_pairs={{0,8},{4,12},{8,16},{12,20},{16,24},{20,28},{24,32},{28,36},{32,40... | collective-permute-start | bytes 196616 | tf_op jit(solution)/shard_map/ppermute | solution.py:227
  130.4 3.7 %collective-permute-done.11 = f32[32,512]{1,0:T(8,128)S(1)} collective-permute-done((f32[32,512]{1,0:T(8,128)S(1)}, f32[32,512]{1,0:T(8,128)S(1)}, u32[]{:S(2)}, u32[]{:S(2)}) %collective-permute-start.11) | collective-permute-done | bytes 65568 | tf_op jit(solution)/shard_map/ppermute | solution.py:227
  134.2 7.9 %all_to_all.63 = f32[4,32,512]{2,1,0:T(8,128)S(1)} all-to-all(f32[4,32,512]{2,1,0:T(8,128)S(1)} %broadcast_in_dim.21), channel_id=1, replica_groups=mesh['y'=8,'z'=8,'core'=2,'x'=4] {'x'}, dimensions={0} | all-to-all | bytes 524288 | tf_op jit(solution)/shard_map/all_to_all | solution.py:237
  142.5 18.2 %all_to_all.64 = f32[16,2,128]{2,1,0:T(2,128)S(1)} all-to-all(f32[16,2,128]{2,1,0:T(2,128)S(1)} %gram_share.4), channel_id=1, replica_groups=mesh['y'=8,'z'=8,'core'=2,'x'=4] {'z','core'}, dimensions={0} | all-to-all | bytes 32768 | tf_op jit(solution)/shard_map/all_to_all | solution.py:245
  160.7 14.9 %all_to_all.65 = f32[32,2,128]{2,1,0:T(2,128)S(1)} all-to-all(f32[32,2,128]{2,1,0:T(2,128)S(1)} %broadcast_in_dim.22), channel_id=1, replica_groups=mesh['y'=8,'z'=8,'core'=2,'x'=4] {'y','x'}, dimensions={0} | all-to-all | bytes 65536 | tf_op jit(solution)/shard_map/all_to_all | solution.py:237
  175.6 12.0 %all_to_all.66 = f32[16,8,128]{2,1,0:T(8,128)S(1)} all-to-all(f32[16,8,128]{2,1,0:T(8,128)S(1)} %broadcast_in_dim.23), channel_id=1, replica_groups=mesh['y'=8,'z'=8,'core'=2,'x'=4] {'z','core'}, dimensions={0} | all-to-all | bytes 131072 | tf_op jit(solution)/shard_map/all_to_all | solution.py:237
  187.6 4.8 %whiten.4.own = f32[32,512]{1,0:T(8,128)S(1)} custom-call(s32[1]{0:T(128)} %bitcast.place_ref, f32[128,128]{1,0:T(8,128)S(1)} %bitcast.79, f32[128,512]{1,0:T(8,128)S(1)} %bitcast.73), custom_call_target="tpu_custom_call" | custom-call | tf_op jit(solution)/shard_map/whiten/pallas_call | solution.py:213
  193.8 4.0 %collective-permute-start.12 = (f32[32,512]{1,0:T(8,128)S(1)}, f32[32,512]{1,0:T(8,128)S(1)}, u32[]{:S(2)}, u32[]{:S(2)}) collective-permute-start(f32[32,512]{1,0:T(8,128)S(1)} %whiten.4.own), channel_id=1, source_target_pairs={{0,8},{4,12},{8,16},{12,20},{16,24},{20,28},{24,32},{28,36},{32,40... | collective-permute-start | bytes 196616 | tf_op jit(solution)/shard_map/ppermute | solution.py:227
  199.1 3.2 %collective-permute-start.14 = (f32[2,32,512]{2,1,0:T(8,128)S(1)}, f32[2,32,512]{2,1,0:T(8,128)S(1)}, u32[]{:S(2)}, u32[]{:S(2)}) collective-permute-start(f32[2,32,512]{2,1,0:T(8,128)S(1)} %pad_maximum_fusion.2), channel_id=1, source_target_pairs={{0,4},{4,0},{1,5},{5,1},{2,6},{6,2},{3,7},{7,3},{8,12},{12,8},{9,1... | collective-permute-start | bytes 393224 | tf_op jit(solution)/shard_map/ppermute | solution.py:231
  205.0 3.1 %apply_operator.5 = (f32[32,512]{1,0:T(8,128)}, f32[32,512]{1,0:T(8,128)S(1)}, f32[2,32,512]{2,1,0:T(8,128)S(1)}, f32[32,512]{1,0:T(8,128)S(1)}, f32[32,512]{1,0:T(8,128)S(1)}) custom-call(s32[1]{0:T(128)} %bitcast.1.core_ref, f32[32,512]{1,0:T(8,128)S(1)} %collective-permute-done.12.below, f32[32,512]{1,0:T(8,128)S(1)} %collective-permute-done.13.above, ...), custom_call_target="tpu_custom_call" | custom-call | tf_op jit(solution)/shard_map/apply_operator/pallas_call | solution.py:103
  211.4 4.0 %collective-permute-start.16 = (f32[32,512]{1,0:T(8,128)S(1)}, f32[32,512]{1,0:T(8,128)S(1)}, u32[]{:S(2)}, u32[]{:S(2)}) collective-permute-start(f32[32,512]{1,0:T(8,128)S(1)} %get-tuple-element.32), channel_id=1, source_target_pairs={{0,8},{4,12},{8,16},{12,20},{16,24},{20,28},{24,32},{28,36},{32,40... | collective-permute-start | bytes 196616 | tf_op jit(solution)/shard_map/ppermute | solution.py:227
  216.7 3.7 %collective-permute-done.17 = f32[32,512]{1,0:T(8,128)S(1)} collective-permute-done((f32[32,512]{1,0:T(8,128)S(1)}, f32[32,512]{1,0:T(8,128)S(1)}, u32[]{:S(2)}, u32[]{:S(2)}) %collective-permute-start.17) | collective-permute-done | bytes 65568 | tf_op jit(solution)/shard_map/ppermute | solution.py:227
  220.5 7.9 %all_to_all.67 = f32[4,32,512]{2,1,0:T(8,128)S(1)} all-to-all(f32[4,32,512]{2,1,0:T(8,128)S(1)} %broadcast_in_dim.24), channel_id=1, replica_groups=mesh['y'=8,'z'=8,'core'=2,'x'=4] {'x'}, dimensions={0} | all-to-all | bytes 524288 | tf_op jit(solution)/shard_map/all_to_all | solution.py:237
  228.8 18.2 %all_to_all.68 = f32[16,2,128]{2,1,0:T(2,128)S(1)} all-to-all(f32[16,2,128]{2,1,0:T(2,128)S(1)} %gram_share.5), channel_id=1, replica_groups=mesh['y'=8,'z'=8,'core'=2,'x'=4] {'z','core'}, dimensions={0} | all-to-all | bytes 32768 | tf_op jit(solution)/shard_map/all_to_all | solution.py:245
  247.0 14.9 %all_to_all.69 = f32[32,2,128]{2,1,0:T(2,128)S(1)} all-to-all(f32[32,2,128]{2,1,0:T(2,128)S(1)} %broadcast_in_dim.25), channel_id=1, replica_groups=mesh['y'=8,'z'=8,'core'=2,'x'=4] {'y','x'}, dimensions={0} | all-to-all | bytes 65536 | tf_op jit(solution)/shard_map/all_to_all | solution.py:237
  261.9 12.0 %all_to_all.70 = f32[16,8,128]{2,1,0:T(8,128)S(1)} all-to-all(f32[16,8,128]{2,1,0:T(8,128)S(1)} %broadcast_in_dim.26), channel_id=1, replica_groups=mesh['y'=8,'z'=8,'core'=2,'x'=4] {'z','core'}, dimensions={0} | all-to-all | bytes 131072 | tf_op jit(solution)/shard_map/all_to_all | solution.py:237
  273.9 5.5 %whiten.5 = f32[32,512]{1,0:T(8,128)} custom-call(s32[1]{0:T(128)} %bitcast.place_ref, f32[128,128]{1,0:T(8,128)S(1)} %bitcast.77, f32[128,512]{1,0:T(8,128)S(1)} %bitcast.71), custom_call_target="tpu_custom_call" | custom-call | tf_op jit(solution)/shard_map/whiten/pallas_call | solution.py:213
  (68 shorter events, 33.7 us)
Async XLA Ops:
  0.6 23.4 %copy-start.4 = (f32[32,512]{1,0:T(8,128)S(1)}, f32[32,512]{1,0:T(8,128)}, u32[]{:S(2)}) copy-start(f32[32,512]{1,0:T(8,128)} %own.1) | copy-start | bytes 196612
  0.6 6.9 %collective-permute-start.1 = (f32[32,512]{1,0:T(8,128)}, f32[32,512]{1,0:T(8,128)S(1)}, u32[]{:S(2)}, u32[]{:S(2)}) collective-permute-start(f32[32,512]{1,0:T(8,128)} %own.1), channel_id=1, source_target_pairs={{8,0},{12,4},{16,8},{20,12},{24,16},{28,20},{32,24},{36,28},{40,32... | collective-permute-start | bytes 196616 | tf_op jit(solution)/shard_map/ppermute | solution.py:227
  2.1 7.1 %collective-permute-start = (f32[32,512]{1,0:T(8,128)}, f32[32,512]{1,0:T(8,128)S(1)}, u32[]{:S(2)}, u32[]{:S(2)}) collective-permute-start(f32[32,512]{1,0:T(8,128)} %own.1), channel_id=1, source_target_pairs={{0,8},{4,12},{8,16},{12,20},{16,24},{20,28},{24,32},{28,36},{32,40... | collective-permute-start | bytes 196616 | tf_op jit(solution)/shard_map/ppermute | solution.py:227
  10.0 14.0 %collective-permute-start.2 = (f32[2,32,512]{2,1,0:T(8,128)S(1)}, f32[2,32,512]{2,1,0:T(8,128)S(1)}, u32[]{:S(2)}, u32[]{:S(2)}) collective-permute-start(f32[2,32,512]{2,1,0:T(8,128)S(1)} %pad_maximum_fusion), channel_id=1, source_target_pairs={{0,4},{4,0},{1,5},{5,1},{2,6},{6,2},{3,7},{7,3},{8,12},{12,8},{9,1... | collective-permute-start | bytes 393224 | tf_op jit(solution)/shard_map/ppermute | solution.py:231
  18.5 2.1 copy-start.3
  20.6 0.7 copy-start.5
  21.2 0.7 copy-start.6
  24.0 3.2 %copy-start = (bf16[5,512,512]{2,1,0:T(8,128)(2,1)}, bf16[5,512,512]{2,1,0:T(8,128)(2,1)S(1)}, u32[]{:S(2)}) copy-start(bf16[5,512,512]{2,1,0:T(8,128)(2,1)S(1)} %get-tuple-element.18.low_hbm) | copy-start | bytes 7864324
  27.2 3.2 %collective-permute-start.3 = (f32[2,32,512]{2,1,0:T(8,128)S(1)}, f32[2,32,512]{2,1,0:T(8,128)S(1)}, u32[]{:S(2)}, u32[]{:S(2)}) collective-permute-start(f32[2,32,512]{2,1,0:T(8,128)S(1)} %get-tuple-element.20), channel_id=1, source_target_pairs={{0,4},{4,0},{1,5},{5,1},{2,6},{6,2},{3,7},{7,3},{8,12},{12,8},{9,1... | collective-permute-start | bytes 393224 | tf_op jit(solution)/shard_map/ppermute | solution.py:231
  30.4 5.1 %collective-permute-start.4 = (f32[32,512]{1,0:T(8,128)S(1)}, f32[32,512]{1,0:T(8,128)S(1)}, u32[]{:S(2)}, u32[]{:S(2)}) collective-permute-start(f32[32,512]{1,0:T(8,128)S(1)} %get-tuple-element.36), channel_id=1, source_target_pairs={{0,8},{4,12},{8,16},{12,20},{16,24},{20,28},{24,32},{28,36},{32,40... | collective-permute-start | bytes 196616 | tf_op jit(solution)/shard_map/ppermute | solution.py:227
  34.2 5.0 %collective-permute-start.5 = (f32[32,512]{1,0:T(8,128)S(1)}, f32[32,512]{1,0:T(8,128)S(1)}, u32[]{:S(2)}, u32[]{:S(2)}) collective-permute-start(f32[32,512]{1,0:T(8,128)S(1)} %get-tuple-element.37), channel_id=1, source_target_pairs={{8,0},{12,4},{16,8},{20,12},{24,16},{28,20},{32,24},{36,28},{40,32... | collective-permute-start | bytes 196616 | tf_op jit(solution)/shard_map/ppermute | solution.py:227
  40.0 8.9 %all-to-all-start = ((f32[4,32,512]{2,1,0:T(8,128)}), f32[4,32,512]{2,1,0:T(8,128)S(1)}, u32[]{:S(2)}, u32[]{:S(2)}) async-start(f32[4,32,512]{2,1,0:T(8,128)} %broadcast_in_dim.18), calls=%async_computation | async-start | bytes 524288 | tf_op jit(solution)/shard_map/all_to_all | solution.py:237
  106.1 5.4 %collective-permute-start.7 = (f32[32,512]{1,0:T(8,128)S(1)}, f32[32,512]{1,0:T(8,128)S(1)}, u32[]{:S(2)}, u32[]{:S(2)}) collective-permute-start(f32[32,512]{1,0:T(8,128)S(1)} %whiten.3.own), channel_id=1, source_target_pairs={{8,0},{12,4},{16,8},{20,12},{24,16},{28,20},{32,24},{36,28},{40,32... | collective-permute-start | bytes 196616 | tf_op jit(solution)/shard_map/ppermute | solution.py:227
  107.4 5.3 %collective-permute-start.6 = (f32[32,512]{1,0:T(8,128)S(1)}, f32[32,512]{1,0:T(8,128)S(1)}, u32[]{:S(2)}, u32[]{:S(2)}) collective-permute-start(f32[32,512]{1,0:T(8,128)S(1)} %whiten.3.own), channel_id=1, source_target_pairs={{0,8},{4,12},{8,16},{12,20},{16,24},{20,28},{24,32},{28,36},{32,40... | collective-permute-start | bytes 196616 | tf_op jit(solution)/shard_map/ppermute | solution.py:227
  112.8 4.2 %collective-permute-start.8 = (f32[2,32,512]{2,1,0:T(8,128)S(1)}, f32[2,32,512]{2,1,0:T(8,128)S(1)}, u32[]{:S(2)}, u32[]{:S(2)}) collective-permute-start(f32[2,32,512]{2,1,0:T(8,128)S(1)} %pad_maximum_fusion.1), channel_id=1, source_target_pairs={{0,4},{4,0},{1,5},{5,1},{2,6},{6,2},{3,7},{7,3},{8,12},{12,8},{9,1... | collective-permute-start | bytes 393224 | tf_op jit(solution)/shard_map/ppermute | solution.py:231
  117.0 1.7 copy-start.1
  121.8 3.2 %collective-permute-start.9 = (f32[2,32,512]{2,1,0:T(8,128)S(1)}, f32[2,32,512]{2,1,0:T(8,128)S(1)}, u32[]{:S(2)}, u32[]{:S(2)}) collective-permute-start(f32[2,32,512]{2,1,0:T(8,128)S(1)} %get-tuple-element.24), channel_id=1, source_target_pairs={{0,4},{4,0},{1,5},{5,1},{2,6},{6,2},{3,7},{7,3},{8,12},{12,8},{9,1... | collective-permute-start | bytes 393224 | tf_op jit(solution)/shard_map/ppermute | solution.py:231
  125.1 5.3 %collective-permute-start.10 = (f32[32,512]{1,0:T(8,128)S(1)}, f32[32,512]{1,0:T(8,128)S(1)}, u32[]{:S(2)}, u32[]{:S(2)}) collective-permute-start(f32[32,512]{1,0:T(8,128)S(1)} %get-tuple-element.34), channel_id=1, source_target_pairs={{0,8},{4,12},{8,16},{12,20},{16,24},{20,28},{24,32},{28,36},{32,40... | collective-permute-start | bytes 196616 | tf_op jit(solution)/shard_map/ppermute | solution.py:227
  129.1 5.0 %collective-permute-start.11 = (f32[32,512]{1,0:T(8,128)S(1)}, f32[32,512]{1,0:T(8,128)S(1)}, u32[]{:S(2)}, u32[]{:S(2)}) collective-permute-start(f32[32,512]{1,0:T(8,128)S(1)} %get-tuple-element.35), channel_id=1, source_target_pairs={{8,0},{12,4},{16,8},{20,12},{24,16},{28,20},{32,24},{36,28},{40,32... | collective-permute-start | bytes 196616 | tf_op jit(solution)/shard_map/ppermute | solution.py:227
  192.5 5.4 %collective-permute-start.13 = (f32[32,512]{1,0:T(8,128)S(1)}, f32[32,512]{1,0:T(8,128)S(1)}, u32[]{:S(2)}, u32[]{:S(2)}) collective-permute-start(f32[32,512]{1,0:T(8,128)S(1)} %whiten.4.own), channel_id=1, source_target_pairs={{8,0},{12,4},{16,8},{20,12},{24,16},{28,20},{32,24},{36,28},{40,32... | collective-permute-start | bytes 196616 | tf_op jit(solution)/shard_map/ppermute | solution.py:227
  193.8 5.3 %collective-permute-start.12 = (f32[32,512]{1,0:T(8,128)S(1)}, f32[32,512]{1,0:T(8,128)S(1)}, u32[]{:S(2)}, u32[]{:S(2)}) collective-permute-start(f32[32,512]{1,0:T(8,128)S(1)} %whiten.4.own), channel_id=1, source_target_pairs={{0,8},{4,12},{8,16},{12,20},{16,24},{20,28},{24,32},{28,36},{32,40... | collective-permute-start | bytes 196616 | tf_op jit(solution)/shard_map/ppermute | solution.py:227
  199.1 4.2 %collective-permute-start.14 = (f32[2,32,512]{2,1,0:T(8,128)S(1)}, f32[2,32,512]{2,1,0:T(8,128)S(1)}, u32[]{:S(2)}, u32[]{:S(2)}) collective-permute-start(f32[2,32,512]{2,1,0:T(8,128)S(1)} %pad_maximum_fusion.2), channel_id=1, source_target_pairs={{0,4},{4,0},{1,5},{5,1},{2,6},{6,2},{3,7},{7,3},{8,12},{12,8},{9,1... | collective-permute-start | bytes 393224 | tf_op jit(solution)/shard_map/ppermute | solution.py:231
  203.3 1.7 copy-start.2
  208.2 3.2 %collective-permute-start.15 = (f32[2,32,512]{2,1,0:T(8,128)S(1)}, f32[2,32,512]{2,1,0:T(8,128)S(1)}, u32[]{:S(2)}, u32[]{:S(2)}) collective-permute-start(f32[2,32,512]{2,1,0:T(8,128)S(1)} %get-tuple-element.28), channel_id=1, source_target_pairs={{0,4},{4,0},{1,5},{5,1},{2,6},{6,2},{3,7},{7,3},{8,12},{12,8},{9,1... | collective-permute-start | bytes 393224 | tf_op jit(solution)/shard_map/ppermute | solution.py:231
  211.4 5.3 %collective-permute-start.16 = (f32[32,512]{1,0:T(8,128)S(1)}, f32[32,512]{1,0:T(8,128)S(1)}, u32[]{:S(2)}, u32[]{:S(2)}) collective-permute-start(f32[32,512]{1,0:T(8,128)S(1)} %get-tuple-element.32), channel_id=1, source_target_pairs={{0,8},{4,12},{8,16},{12,20},{16,24},{20,28},{24,32},{28,36},{32,40... | collective-permute-start | bytes 196616 | tf_op jit(solution)/shard_map/ppermute | solution.py:227
  215.4 5.0 %collective-permute-start.17 = (f32[32,512]{1,0:T(8,128)S(1)}, f32[32,512]{1,0:T(8,128)S(1)}, u32[]{:S(2)}, u32[]{:S(2)}) collective-permute-start(f32[32,512]{1,0:T(8,128)S(1)} %get-tuple-element.33), channel_id=1, source_target_pairs={{8,0},{12,4},{16,8},{20,12},{24,16},{28,20},{32,24},{36,28},{40,32... | collective-permute-start | bytes 196616 | tf_op jit(solution)/shard_map/ppermute | solution.py:227
where the time goes:
time: 281 us; the launch traced here: 279 us
  blocking collectives  158 us (56%)
  starting transfers between devices  57.7 us (21%)
  Pallas kernels  27.9 us (10%)
  waiting for transfers between devices  26 us (9%)
  local copies, waits for them, and re-layouts  7.77 us (3%)
    all_to_all x8, blocking collectives, spread(): return lax.all_to_all(copies, axes, 0, 0)  99.4 us
    all_to_all x3, blocking collectives, summed_gram(): share = lax.all_to_all(share, ('z', 'core'), 0, 0).sum(axis=0)  58.4 us
    ppermute x12, starting transfers between devices, shifted(): lax.ppermute(value, ROWS, [(source, source + steps) for source in range(l...  33 us
    ppermute x6, starting transfers between devices, swapped(): return lax.ppermute(value, 'core', [(0, 1), (1, 0)])  21.3 us
    ppermute x12, waiting for transfers between devices, shifted(): lax.ppermute(value, ROWS, [(source, source + steps) for source in range(l...  15.4 us
    pallas_call x3, Pallas kernels, whiten(): pl.pallas_call(functools.partial(whiten_kernel, scale=scale, panel=4), in...  15.2 us
    pallas_call x3, Pallas kernels, apply_operator(): pl.pallas_call(apply_kernel, in_specs=[pl.BlockSpec(memory_space=pltpu.SM...  9.42 us
    unnamed x14, local copies, waits for them, and re-layouts  6.91 us
  transfers between devices with their start and end apart: 19, of which 14 were waited for; matrix products, arithmetic and copies ran while one was open for 0% of the time, Pallas kernels for 1%

commit v1 on v0

--- a/solution.py
+++ b/solution.py
@@ -55,7 +55,6 @@
             scratch_shapes=[pltpu.VMEM((width, width), jnp.float32)],
         ),
         out_shape=[piece, piece],
-        compiler_params=pltpu.CompilerParams(vmem_limit_bytes=20 * MIB),
         name="operator_band",
     )(tile_rows, tile_cols, tile_values)
 
@@ -97,7 +96,7 @@
 
 
 def apply_operator(core, below, above, own, got, high, low):
-    vmem, hbm = pl.BlockSpec(memory_space=pltpu.VMEM), pl.BlockSpec(memory_space=pl.ANY)
+    vmem, hbm = pl.BlockSpec(memory_space=pltpu.VMEM), pl.BlockSpec(memory_space=pltpu.HBM)
     one = jax.ShapeDtypeStruct(own.shape, jnp.float32)
     two = jax.ShapeDtypeStruct(got.shape, jnp.float32)
     return pl.pallas_call(
@@ -115,39 +114,62 @@
     )(core, below, above, own, got, high, low)
 
 
-def gram_kernel(place_ref, all_ref, out_ref, whole):
-    total = lax.dot_general(
-        all_ref[...],
-        all_ref[...],
-        (((1,), (1,)), ((), ())),
-        precision=precise,
-        preferred_element_type=jnp.float32,
+def gram_of(value):
+    return lax.dot_general(
+        value, value, (((1,), (1,)), ((), ())), precision=precise, preferred_element_type=jnp.float32
     )
-    whole[...] = total.reshape(whole.shape)
-    few = out_ref.shape[1]
-    for k in range(whole.shape[1] // few):
-
-        @pl.when(place_ref[0] == k)
-        def _():
-            out_ref[...] = whole[:, few * k : few * (k + 1), :]
-
-
-def gram_share(place, all_vectors, runs, x_count):
+
+
+def gram_kernel(all_ref, out_ref):
+    out_ref[...] = gram_of(all_ref[...])
+
+
+def gram_share(all_vectors):
     vmem = pl.BlockSpec(memory_space=pltpu.VMEM)
     size = all_vectors.shape[0]
-    run = size // runs
     return pl.pallas_call(
         gram_kernel,
-        in_specs=[pl.BlockSpec(memory_space=pltpu.SMEM), vmem],
+        in_specs=[vmem],
         out_specs=vmem,
-        out_shape=jax.ShapeDtypeStruct((runs, run // x_count, size), jnp.float32),
-        scratch_shapes=[pltpu.VMEM((runs, run, size), jnp.float32)],
+        out_shape=jax.ShapeDtypeStruct((size, size), jnp.float32),
         compiler_params=pltpu.CompilerParams(vmem_limit_bytes=8 * MIB),
         name="gram_share",
-    )(place, all_vectors)
-
-
-def whiten_kernel(place_ref, gram_ref, all_ref, out_ref, zero_ref, inverse_ref, *, scale, panel):
+    )(all_vectors)
+
+
+def advance_kernel(place_ref, inverse_ref, raw_ref, all_ref, own_ref, gram_ref, *, scale):
+    members, parts, own, width = raw_ref.shape
+    dot = functools.partial(jnp.dot, precision=precise, preferred_element_type=jnp.float32)
+    current = scale * dot(inverse_ref[...], raw_ref[:, 0].reshape(members * own, width))
+    all_ref[...] = current
+    gram_ref[...] = gram_of(current)
+    rows = pl.ds(pl.multiple_of(place_ref[0] * own, own), own)
+    if parts == 1:
+        own_ref[...] = all_ref[rows, :]
+    else:
+        last = raw_ref[:, parts - 1].reshape(members * own, width)
+        own_ref[...] = scale * dot(inverse_ref[rows, :], last)
+
+
+def advance(place, inverse, raw, scale):
+    vmem = pl.BlockSpec(memory_space=pltpu.VMEM)
+    members, _, own, width = raw.shape
+    size = members * own
+    return pl.pallas_call(
+        functools.partial(advance_kernel, scale=scale),
+        in_specs=[pl.BlockSpec(memory_space=pltpu.SMEM), vmem, vmem],
+        out_specs=[vmem] * 3,
+        out_shape=[
+            jax.ShapeDtypeStruct((size, width), jnp.float32),
+            jax.ShapeDtypeStruct((own, width), jnp.float32),
+            jax.ShapeDtypeStruct((size, size), jnp.float32),
+        ],
+        compiler_params=pltpu.CompilerParams(vmem_limit_bytes=8 * MIB),
+        name="advance",
+    )(place, inverse, raw)
+
+
+def invert(gram_ref, inverse_ref, zero_ref, panel):
     size = gram_ref.shape[0]
     tall = 8
     zero_ref[...] = jnp.zeros((tall, size), jnp.float32)
@@ -202,6 +224,27 @@
         if js + panel == tall:
             inverse_ref[tall * jb : tall * (jb + 1), :] = right[jb] * (1.0 / jnp.sqrt(pivots))
             pivots = jnp.ones((tall, size), jnp.float32)
+
+
+def inverse_kernel(gram_ref, inverse_ref, zero_ref, *, panel):
+    invert(gram_ref, inverse_ref, zero_ref, panel)
+
+
+def cholesky_inverse(gram):
+    vmem = pl.BlockSpec(memory_space=pltpu.VMEM)
+    return pl.pallas_call(
+        functools.partial(inverse_kernel, panel=4),
+        in_specs=[vmem],
+        out_specs=vmem,
+        out_shape=jax.ShapeDtypeStruct(gram.shape, jnp.float32),
+        scratch_shapes=[pltpu.VMEM((8, gram.shape[0]), jnp.float32)],
+        compiler_params=pltpu.CompilerParams(vmem_limit_bytes=8 * MIB),
+        name="cholesky_inverse",
+    )(gram)
+
+
+def whiten_kernel(place_ref, gram_ref, all_ref, out_ref, zero_ref, inverse_ref, *, scale, panel):
+    invert(gram_ref, inverse_ref, zero_ref, panel)
     own = out_ref.shape[0]
     rows = inverse_ref[pl.ds(pl.multiple_of(place_ref[0] * own, own), own), :]
     out_ref[...] = scale * jnp.dot(rows, all_ref[...], precision=precise, preferred_element_type=jnp.float32)
@@ -237,37 +280,44 @@
     return lax.all_to_all(copies, axes, 0, 0)
 
 
-def summed_gram(place, all_vectors):
-    line, x_count = lax.axis_size(("z", "core")), lax.axis_size("x")
-    size = all_vectors.shape[0]
-    share = gram_share(place, all_vectors, line, x_count)
-    few = share.shape[1]
-    share = lax.all_to_all(share, ("z", "core"), 0, 0).sum(axis=0)
-    run = spread(share, ("y", "x")).reshape(-1, x_count * few, size).sum(axis=0)
+def summed(share):
+    size = share.shape[0]
+    line = lax.axis_size(("z", "core"))
+    share = lax.all_to_all(share.reshape(line, size // line, size), ("z", "core"), 0, 0).sum(axis=0)
+    run = spread(share, "y").sum(axis=0)
     return spread(run, ("z", "core")).reshape(size, size)
 
 
 def body(tile_values, tile_rows, tile_cols, start_vectors):
-    local_cols, row_width = start_vectors.shape
-    all_count = local_cols * lax.axis_size("x")
+    own, row_width = start_vectors.shape
+    all_count = own * lax.axis_size("x")
     scale = (row_width * lax.axis_size(ROWS)) ** 0.5
     core = lax.axis_index("core").astype(jnp.int32)
     first = core == 0
     place = lax.axis_index("x").astype(jnp.int32).reshape(1)
     core = core.reshape(1)
     high, low = operator_band(tile_values, tile_rows, tile_cols, row_width)
-    vectors = start_vectors
-    for iteration in range(ITERS):
+
+    def operator_pass(vectors):
         below, above = shifted(vectors, 2), shifted(vectors, -2)
         got = swapped(jnp.stack([vectors, jnp.where(first, above, below)]))
         images, kept, crossing, down, up = apply_operator(core, below, above, vectors, got, high, low)
         got = swapped(crossing)
         up = jnp.where(first, up + got[1], up)
         down = jnp.where(first, down, down + got[1])
-        pulled = kept + got[0] + shifted(up, 2) + shifted(down, -2)
-        all_vectors = spread(pulled, "x").reshape(all_count, row_width)
-        gram = summed_gram(place, all_vectors)
-        vectors = whiten(place, gram, all_vectors, local_cols, scale)
+        return images, kept + got[0] + shifted(up, 2) + shifted(down, -2)
+
+    images, pulled = operator_pass(start_vectors)
+    all_vectors = spread(pulled, "x").reshape(all_count, row_width)
+    gram = gram_share(all_vectors)
+    for iteration in range(1, ITERS):
+        images, ahead = operator_pass(pulled)
+        inverse = cholesky_inverse(summed(gram))
+        parts = [ahead, images] if iteration == ITERS - 1 else [ahead]
+        raw = spread(jnp.stack(parts), "x")
+        all_vectors, pulled, gram = advance(place, inverse, raw, scale)
+    images = pulled
+    vectors = whiten(place, summed(gram), all_vectors, own, scale)
     return (vectors, images)
 
 

time: 281 us -> 249 us (0.89)
  blocking collectives: 158 us -> 59 us
  starting transfers between devices: 57.7 us -> 96.7 us
  waiting for transfers between devices: 26 us -> 43.5 us
  Pallas kernels: 27.9 us -> 35.1 us
  local copies, waits for them, and re-layouts: 7.77 us -> 10.6 us
    all_to_all x8 -> x4, blocking collectives: 99.4 us -> 47.8 us  [spread(): return lax.all_to_all(copies, axes, 0, 0)]
    all_to_all x3 -> x1, blocking collectives: 58.4 us -> 11.2 us  [summed(): lax.all_to_all(share.reshape(line, size // line, size), ('z', 'core'), 0, 0)]
    all_to_all x1 -> x5, starting transfers between devices: 3.4 us -> 24.8 us  [spread(): return lax.all_to_all(copies, axes, 0, 0)]
    all_to_all x0 -> x2, starting transfers between devices: none -> 20.1 us  [summed(): lax.all_to_all(share.reshape(line, size // line, size), ('z', 'core'), 0, 0)]
    all_to_all x1 -> x5, waiting for transfers between devices: 5.49 us -> 21.5 us  [spread(): return lax.all_to_all(copies, axes, 0, 0)]
    pallas_call x3 -> x5, Pallas kernels: 1.23 us -> 13.2 us  [the longest x2 9.4 us: cholesky_inverse(): pl.pallas_call(functools.partial(inverse_kernel, panel=4), in_specs=[vmem...]
    pallas_call x3 -> x1, Pallas kernels: 15.2 us -> 5.48 us  [whiten(): pl.pallas_call(functools.partial(whiten_kernel, scale=scale, panel=4), in...]
    pallas_call x1, Pallas kernels: 2.07 us -> 7.04 us  [operator_band(): pl.pallas_call(band_kernel, grid_spec=pltpu.PrefetchScalarGridSpec(num_sc...]
  transfers between devices with their start and end apart: 19 -> 25, of which waited for: 14 -> 14; matrix products, arithmetic and copies ran while one was open for 0% -> 1% of each run, Pallas kernels for 1% -> 8%
where the time goes in v1:
time: 249 us; the launch traced here: 247 us
  starting transfers between devices  96.7 us (39%)
  blocking collectives  59 us (24%)
  waiting for transfers between devices  43.5 us (17%)
  Pallas kernels  35.1 us (14%)
  local copies, waits for them, and re-layouts  10.6 us (4%)
    all_to_all x4, blocking collectives, spread(): return lax.all_to_all(copies, axes, 0, 0)  47.8 us
    ppermute x12, starting transfers between devices, shifted(): lax.ppermute(value, ROWS, [(source, source + steps) for source in range(l...  30.5 us
    all_to_all x5, starting transfers between devices, spread(): return lax.all_to_all(copies, axes, 0, 0)  24.8 us
    all_to_all x5, waiting for transfers between devices, spread(): return lax.all_to_all(copies, axes, 0, 0)  21.5 us
    ppermute x6, starting transfers between devices, swapped(): return lax.ppermute(value, 'core', [(0, 1), (1, 0)])  21.3 us
    all_to_all x2, starting transfers between devices, summed(): lax.all_to_all(share.reshape(line, size // line, size), ('z', 'core'), 0, 0)  20.1 us
    ppermute x12, waiting for transfers between devices, shifted(): lax.ppermute(value, ROWS, [(source, source + steps) for source in range(l...  14.8 us
    all_to_all x1, blocking collectives, summed(): lax.all_to_all(share.reshape(line, size // line, size), ('z', 'core'), 0, 0)  11.2 us
  transfers between devices with their start and end apart: 25, of which 14 were waited for; matrix products, arithmetic and copies ran while one was open for 1% of the time, Pallas kernels for 8%

profile of v1, /device:TPU:1, one launch (start us, length us, event | category | flops | bytes accessed | tf_op | source)
XLA Modules:
  0.0 247.0 jit_solution(15818123227853256608)
XLA Ops:
  0.6 5.0 %collective-permute-start = (f32[32,512]{1,0:T(8,128)}, f32[32,512]{1,0:T(8,128)S(1)}, u32[]{:S(2)}, u32[]{:S(2)}) collective-permute-start(f32[32,512]{1,0:T(8,128)} %own.1), channel_id=1, source_target_pairs={{0,8},{4,12},{8,16},{12,20},{16,24},{20,28},{24,32},{28,36},{32,40... | collective-permute-start | bytes 196616 | tf_op jit(solution)/shard_map/ppermute | solution.py:270
  7.2 4.2 %collective-permute-done.1.above = f32[32,512]{1,0:T(8,128)S(1)} collective-permute-done((f32[32,512]{1,0:T(8,128)}, f32[32,512]{1,0:T(8,128)S(1)}, u32[]{:S(2)}, u32[]{:S(2)}) %collective-permute-start.1) | collective-permute-done | bytes 65568 | tf_op jit(solution)/shard_map/ppermute | solution.py:270
  12.3 5.7 %collective-permute-start.2 = (f32[2,32,512]{2,1,0:T(8,128)S(1)}, f32[2,32,512]{2,1,0:T(8,128)S(1)}, u32[]{:S(2)}, u32[]{:S(2)}) collective-permute-start(f32[2,32,512]{2,1,0:T(8,128)S(1)} %pad_maximum_fusion), channel_id=1, source_target_pairs={{0,4},{4,0},{1,5},{5,1},{2,6},{6,2},{3,7},{7,3},{8,12},{12,8},{9,1... | collective-permute-start | bytes 393224 | tf_op jit(solution)/shard_map/ppermute | solution.py:274
  18.1 7.0 %operator_band.1 = (bf16[5,512,512]{2,1,0:T(8,128)(2,1)}, bf16[5,512,512]{2,1,0:T(8,128)(2,1)}) custom-call(s32[15]{0:T(128)} %rows_ref.1, s32[15]{0:T(128)} %cols_ref.1, f32[15,256,256]{2,1,0:T(8,128)} %tiles_ref.1), custom_call_target="tpu_custom_call" | custom-call | tf_op jit(solution)/shard_map/operator_band/pallas_call | solution.py:48
  28.6 3.1 %apply_operator.3 = (f32[32,512]{1,0:T(8,128)}, f32[32,512]{1,0:T(8,128)S(1)}, f32[2,32,512]{2,1,0:T(8,128)S(1)}, f32[32,512]{1,0:T(8,128)S(1)}, f32[32,512]{1,0:T(8,128)S(1)}) custom-call(s32[1]{0:T(128)} %bitcast.1.core_ref, f32[32,512]{1,0:T(8,128)S(1)} %collective-permute-done.below, f32[32,512]{1,0:T(8,128)S(1)} %collective-permute-done.1.above, ...), custom_call_target="tpu_custom_call" | custom-call | tf_op jit(solution)/shard_map/apply_operator/pallas_call | solution.py:102
  36.3 4.0 %collective-permute-start.4 = (f32[32,512]{1,0:T(8,128)S(1)}, f32[32,512]{1,0:T(8,128)S(1)}, u32[]{:S(2)}, u32[]{:S(2)}) collective-permute-start(f32[32,512]{1,0:T(8,128)S(1)} %get-tuple-element.46), channel_id=1, source_target_pairs={{0,8},{4,12},{8,16},{12,20},{16,24},{20,28},{24,32},{28,36},{32,40... | collective-permute-start | bytes 196616 | tf_op jit(solution)/shard_map/ppermute | solution.py:270
  41.6 3.9 %collective-permute-start.6 = (f32[32,512]{1,0:T(8,128)S(1)}, f32[32,512]{1,0:T(8,128)S(1)}, u32[]{:S(2)}, u32[]{:S(2)}) collective-permute-start(f32[32,512]{1,0:T(8,128)S(1)} %fusion.9.own), channel_id=1, source_target_pairs={{0,8},{4,12},{8,16},{12,20},{16,24},{20,28},{24,32},{28,36},{32,40... | collective-permute-start | bytes 196616 | tf_op jit(solution)/shard_map/ppermute | solution.py:270
  46.9 5.2 %collective-permute-done.7.above = f32[32,512]{1,0:T(8,128)S(1)} collective-permute-done((f32[32,512]{1,0:T(8,128)S(1)}, f32[32,512]{1,0:T(8,128)S(1)}, u32[]{:S(2)}, u32[]{:S(2)}) %collective-permute-start.7) | collective-permute-done | bytes 65568 | tf_op jit(solution)/shard_map/ppermute | solution.py:270
  52.1 4.1 %collective-permute-start.8 = (f32[2,32,512]{2,1,0:T(8,128)S(1)}, f32[2,32,512]{2,1,0:T(8,128)S(1)}, u32[]{:S(2)}, u32[]{:S(2)}) collective-permute-start(f32[2,32,512]{2,1,0:T(8,128)S(1)} %pad_maximum_fusion.1), channel_id=1, source_target_pairs={{0,4},{4,0},{1,5},{5,1},{2,6},{6,2},{3,7},{7,3},{8,12},{12,8},{9,1... | collective-permute-start | bytes 393224 | tf_op jit(solution)/shard_map/ppermute | solution.py:274
  56.9 4.0 %all-to-all-start = ((f32[4,32,512]{2,1,0:T(8,128)}), f32[4,32,512]{2,1,0:T(8,128)S(1)}, u32[]{:S(2)}, u32[]{:S(2)}) async-start(f32[4,32,512]{2,1,0:T(8,128)} %broadcast_in_dim.20), calls=%async_computation | async-start | bytes 524288 | tf_op jit(solution)/shard_map/all_to_all | solution.py:280
  62.7 3.1 %apply_operator.4 = (f32[32,512]{1,0:T(8,128)}, f32[32,512]{1,0:T(8,128)S(1)}, f32[2,32,512]{2,1,0:T(8,128)S(1)}, f32[32,512]{1,0:T(8,128)S(1)}, f32[32,512]{1,0:T(8,128)S(1)}) custom-call(s32[1]{0:T(128)} %bitcast.1.core_ref, f32[32,512]{1,0:T(8,128)S(1)} %collective-permute-done.6.below, f32[32,512]{1,0:T(8,128)S(1)} %collective-permute-done.7.above, ...), custom_call_target="tpu_custom_call" | custom-call | tf_op jit(solution)/shard_map/apply_operator/pallas_call | solution.py:102
  69.1 13.7 %all-to-all-start.1 = ((f32[16,8,128]{2,1,0:T(8,128)}), f32[16,8,128]{2,1,0:T(8,128)S(1)}, u32[]{:S(2)}, u32[]{:S(2)}) async-start(f32[16,8,128]{2,1,0:T(8,128)} %bitcast.7), calls=%async_computation.1 | async-start | bytes 131072 | tf_op jit(solution)/shard_map/all_to_all | solution.py:286
  84.1 4.0 %collective-permute-start.10 = (f32[32,512]{1,0:T(8,128)S(1)}, f32[32,512]{1,0:T(8,128)S(1)}, u32[]{:S(2)}, u32[]{:S(2)}) collective-permute-start(f32[32,512]{1,0:T(8,128)S(1)} %get-tuple-element.44), channel_id=1, source_target_pairs={{0,8},{4,12},{8,16},{12,20},{16,24},{20,28},{24,32},{28,36},{32,40... | collective-permute-start | bytes 196616 | tf_op jit(solution)/shard_map/ppermute | solution.py:270
  90.6 16.8 %all_to_all.60 = f32[8,8,128]{2,1,0:T(8,128)S(1)} all-to-all(f32[8,8,128]{2,1,0:T(8,128)S(1)} %broadcast_in_dim.21), channel_id=1, replica_groups=mesh['y'=8,'z'=8,'core'=2,'x'=4] {'y'}, dimensions={0} | all-to-all | bytes 65536 | tf_op jit(solution)/shard_map/all_to_all | solution.py:280
  108.1 6.6 %all-to-all-start.3 = ((f32[16,8,128]{2,1,0:T(8,128)}), f32[16,8,128]{2,1,0:T(8,128)S(1)}, u32[]{:S(2)}, u32[]{:S(2)}) async-start(f32[16,8,128]{2,1,0:T(8,128)} %broadcast_in_dim.22), calls=%async_computation.3 | async-start | bytes 131072 | tf_op jit(solution)/shard_map/all_to_all | solution.py:280
  114.7 7.7 %all-to-all-done.3 = f32[16,8,128]{2,1,0:T(8,128)S(1)} async-done(((f32[16,8,128]{2,1,0:T(8,128)}), f32[16,8,128]{2,1,0:T(8,128)S(1)}, u32[]{:S(2)}, u32[]{:S(2)}) %all-to-all-start.3) | async-done | bytes 65568 | tf_op jit(solution)/shard_map/all_to_all | solution.py:280
  123.2 4.1 %all-to-all-start.4 = ((f32[4,1,32,512]{3,2,1,0:T(8,128)}), f32[4,1,32,512]{3,2,1,0:T(8,128)S(1)}, u32[]{:S(2)}, u32[]{:S(2)}) async-start(f32[4,1,32,512]{3,2,1,0:T(8,128)} %broadcast_in_dim.24), calls=%async_computation.4 | async-start | bytes 524288 | tf_op jit(solution)/shard_map/all_to_all | solution.py:280
  127.3 4.7 %cholesky_inverse.2.inverse_ref = f32[128,128]{1,0:T(8,128)S(1)} custom-call(f32[128,128]{1,0:T(8,128)S(1)} %bitcast.69), custom_call_target="tpu_custom_call" | custom-call | tf_op jit(solution)/shard_map/cholesky_inverse/pallas_call | solution.py:235
  138.2 3.7 %collective-permute-done.13.above = f32[32,512]{1,0:T(8,128)S(1)} collective-permute-done((f32[32,512]{1,0:T(8,128)S(1)}, f32[32,512]{1,0:T(8,128)S(1)}, u32[]{:S(2)}, u32[]{:S(2)}) %collective-permute-start.13) | collective-permute-done | bytes 65568 | tf_op jit(solution)/shard_map/ppermute | solution.py:270
  141.9 5.0 %collective-permute-start.14 = (f32[2,32,512]{2,1,0:T(8,128)S(1)}, f32[2,32,512]{2,1,0:T(8,128)S(1)}, u32[]{:S(2)}, u32[]{:S(2)}) collective-permute-start(f32[2,32,512]{2,1,0:T(8,128)S(1)} %pad_maximum_fusion.2), channel_id=1, source_target_pairs={{0,4},{4,0},{1,5},{5,1},{2,6},{6,2},{3,7},{7,3},{8,12},{12,8},{9,1... | collective-permute-start | bytes 393224 | tf_op jit(solution)/shard_map/ppermute | solution.py:274
  155.1 6.3 %all-to-all-start.5 = ((f32[16,8,128]{2,1,0:T(8,128)}), f32[16,8,128]{2,1,0:T(8,128)S(1)}, u32[]{:S(2)}, u32[]{:S(2)}) async-start(f32[16,8,128]{2,1,0:T(8,128)} %bitcast.13), calls=%async_computation.5 | async-start | bytes 131072 | tf_op jit(solution)/shard_map/all_to_all | solution.py:286
  162.7 4.0 %collective-permute-start.16 = (f32[32,512]{1,0:T(8,128)S(1)}, f32[32,512]{1,0:T(8,128)S(1)}, u32[]{:S(2)}, u32[]{:S(2)}) collective-permute-start(f32[32,512]{1,0:T(8,128)S(1)} %get-tuple-element.42), channel_id=1, source_target_pairs={{0,8},{4,12},{8,16},{12,20},{16,24},{20,28},{24,32},{28,36},{32,40... | collective-permute-start | bytes 196616 | tf_op jit(solution)/shard_map/ppermute | solution.py:270
  169.2 10.2 %all_to_all.61 = f32[8,8,128]{2,1,0:T(8,128)S(1)} all-to-all(f32[8,8,128]{2,1,0:T(8,128)S(1)} %broadcast_in_dim.25), channel_id=1, replica_groups=mesh['y'=8,'z'=8,'core'=2,'x'=4] {'y'}, dimensions={0} | all-to-all | bytes 65536 | tf_op jit(solution)/shard_map/all_to_all | solution.py:280
  180.0 6.6 %all-to-all-start.7 = ((f32[16,8,128]{2,1,0:T(8,128)}), f32[16,8,128]{2,1,0:T(8,128)S(1)}, u32[]{:S(2)}, u32[]{:S(2)}) async-start(f32[16,8,128]{2,1,0:T(8,128)} %broadcast_in_dim.26), calls=%async_computation.7 | async-start | bytes 131072 | tf_op jit(solution)/shard_map/all_to_all | solution.py:280
  186.7 7.7 %all-to-all-done.7 = f32[16,8,128]{2,1,0:T(8,128)S(1)} async-done(((f32[16,8,128]{2,1,0:T(8,128)}), f32[16,8,128]{2,1,0:T(8,128)S(1)}, u32[]{:S(2)}, u32[]{:S(2)}) %all-to-all-start.7) | async-done | bytes 65568 | tf_op jit(solution)/shard_map/all_to_all | solution.py:280
  195.3 3.5 %all-to-all-start.8 = ((f32[4,2,32,512]{3,2,1,0:T(8,128)}), f32[4,2,32,512]{3,2,1,0:T(8,128)S(1)}, u32[]{:S(2)}, u32[]{:S(2)}) async-start(f32[4,2,32,512]{3,2,1,0:T(8,128)} %broadcast_in_dim.27), calls=%async_computation.8 | async-start | bytes 1048576 | tf_op jit(solution)/shard_map/all_to_all | solution.py:280
  198.8 4.7 %cholesky_inverse.3.inverse_ref = f32[128,128]{1,0:T(8,128)S(1)} custom-call(f32[128,128]{1,0:T(8,128)S(1)} %bitcast.70), custom_call_target="tpu_custom_call" | custom-call | tf_op jit(solution)/shard_map/cholesky_inverse/pallas_call | solution.py:235
  203.5 4.7 %all-to-all-done.8.raw_ref = f32[4,2,32,512]{3,2,1,0:T(8,128)S(1)} async-done(((f32[4,2,32,512]{3,2,1,0:T(8,128)}), f32[4,2,32,512]{3,2,1,0:T(8,128)S(1)}, u32[]{:S(2)}, u32[]{:S(2)}) %all-to-all-start.8) | async-done | bytes 524320 | tf_op jit(solution)/shard_map/all_to_all | solution.py:280
  209.5 11.2 %all_to_all.62 = f32[16,8,128]{2,1,0:T(8,128)S(1)} all-to-all(f32[16,8,128]{2,1,0:T(8,128)S(1)} %bitcast.72), channel_id=1, replica_groups=mesh['y'=8,'z'=8,'core'=2,'x'=4] {'z','core'}, dimensions={0} | all-to-all | bytes 131072 | tf_op jit(solution)/shard_map/all_to_all | solution.py:286
  220.7 9.2 %all_to_all.63 = f32[8,8,128]{2,1,0:T(8,128)S(1)} all-to-all(f32[8,8,128]{2,1,0:T(8,128)S(1)} %broadcast_in_dim.28), channel_id=1, replica_groups=mesh['y'=8,'z'=8,'core'=2,'x'=4] {'y'}, dimensions={0} | all-to-all | bytes 65536 | tf_op jit(solution)/shard_map/all_to_all | solution.py:280
  230.0 11.5 %all_to_all.64 = f32[16,8,128]{2,1,0:T(8,128)S(1)} all-to-all(f32[16,8,128]{2,1,0:T(8,128)S(1)} %broadcast_in_dim.29), channel_id=1, replica_groups=mesh['y'=8,'z'=8,'core'=2,'x'=4] {'z','core'}, dimensions={0} | all-to-all | bytes 131072 | tf_op jit(solution)/shard_map/all_to_all | solution.py:280
  241.5 5.5 %whiten.1 = f32[32,512]{1,0:T(8,128)} custom-call(s32[1]{0:T(128)} %bitcast.place_ref, f32[128,128]{1,0:T(8,128)S(1)} %bitcast.71, f32[128,512]{1,0:T(8,128)S(1)} %get-tuple-element.40.all_ref), custom_call_target="tpu_custom_call" | custom-call | tf_op jit(solution)/shard_map/whiten/pallas_call | solution.py:256
  (73 shorter events, 45.0 us)
Async XLA Ops:
  0.6 24.5 %copy-start.5 = (f32[32,512]{1,0:T(8,128)S(1)}, f32[32,512]{1,0:T(8,128)}, u32[]{:S(2)}) copy-start(f32[32,512]{1,0:T(8,128)} %own.1) | copy-start | bytes 196612
  0.6 6.6 %collective-permute-start = (f32[32,512]{1,0:T(8,128)}, f32[32,512]{1,0:T(8,128)S(1)}, u32[]{:S(2)}, u32[]{:S(2)}) collective-permute-start(f32[32,512]{1,0:T(8,128)} %own.1), channel_id=1, source_target_pairs={{0,8},{4,12},{8,16},{12,20},{16,24},{20,28},{24,32},{28,36},{32,40... | collective-permute-start | bytes 196616 | tf_op jit(solution)/shard_map/ppermute | solution.py:270
  5.6 5.9 %collective-permute-start.1 = (f32[32,512]{1,0:T(8,128)}, f32[32,512]{1,0:T(8,128)S(1)}, u32[]{:S(2)}, u32[]{:S(2)}) collective-permute-start(f32[32,512]{1,0:T(8,128)} %own.1), channel_id=1, source_target_pairs={{8,0},{12,4},{16,8},{20,12},{24,16},{28,20},{32,24},{36,28},{40,32... | collective-permute-start | bytes 196616 | tf_op jit(solution)/shard_map/ppermute | solution.py:270
  12.3 12.8 %collective-permute-start.2 = (f32[2,32,512]{2,1,0:T(8,128)S(1)}, f32[2,32,512]{2,1,0:T(8,128)S(1)}, u32[]{:S(2)}, u32[]{:S(2)}) collective-permute-start(f32[2,32,512]{2,1,0:T(8,128)S(1)} %pad_maximum_fusion), channel_id=1, source_target_pairs={{0,4},{4,0},{1,5},{5,1},{2,6},{6,2},{3,7},{7,3},{8,12},{12,8},{9,1... | collective-permute-start | bytes 393224 | tf_op jit(solution)/shard_map/ppermute | solution.py:274
  25.1 1.7 copy-start
  26.9 1.7 copy-start.2
  28.6 32.3 %copy-start.1 = (bf16[5,512,512]{2,1,0:T(8,128)(2,1)S(1)}, bf16[5,512,512]{2,1,0:T(8,128)(2,1)}, u32[]{:S(2)}) copy-start(bf16[5,512,512]{2,1,0:T(8,128)(2,1)} %get-tuple-element.22.high_hbm) | copy-start | bytes 7864324
  31.7 3.2 %collective-permute-start.3 = (f32[2,32,512]{2,1,0:T(8,128)S(1)}, f32[2,32,512]{2,1,0:T(8,128)S(1)}, u32[]{:S(2)}, u32[]{:S(2)}) collective-permute-start(f32[2,32,512]{2,1,0:T(8,128)S(1)} %get-tuple-element.25), channel_id=1, source_target_pairs={{0,4},{4,0},{1,5},{5,1},{2,6},{6,2},{3,7},{7,3},{8,12},{12,8},{9,1... | collective-permute-start | bytes 393224 | tf_op jit(solution)/shard_map/ppermute | solution.py:274
  35.0 5.4 %collective-permute-start.5 = (f32[32,512]{1,0:T(8,128)S(1)}, f32[32,512]{1,0:T(8,128)S(1)}, u32[]{:S(2)}, u32[]{:S(2)}) collective-permute-start(f32[32,512]{1,0:T(8,128)S(1)} %get-tuple-element.47), channel_id=1, source_target_pairs={{8,0},{12,4},{16,8},{20,12},{24,16},{28,20},{32,24},{36,28},{40,32... | collective-permute-start | bytes 196616 | tf_op jit(solution)/shard_map/ppermute | solution.py:270
  36.3 5.3 %collective-permute-start.4 = (f32[32,512]{1,0:T(8,128)S(1)}, f32[32,512]{1,0:T(8,128)S(1)}, u32[]{:S(2)}, u32[]{:S(2)}) collective-permute-start(f32[32,512]{1,0:T(8,128)S(1)} %get-tuple-element.46), channel_id=1, source_target_pairs={{0,8},{4,12},{8,16},{12,20},{16,24},{20,28},{24,32},{28,36},{32,40... | collective-permute-start | bytes 196616 | tf_op jit(solution)/shard_map/ppermute | solution.py:270
  41.6 5.2 %collective-permute-start.6 = (f32[32,512]{1,0:T(8,128)S(1)}, f32[32,512]{1,0:T(8,128)S(1)}, u32[]{:S(2)}, u32[]{:S(2)}) collective-permute-start(f32[32,512]{1,0:T(8,128)S(1)} %fusion.9.own), channel_id=1, source_target_pairs={{0,8},{4,12},{8,16},{12,20},{16,24},{20,28},{24,32},{28,36},{32,40... | collective-permute-start | bytes 196616 | tf_op jit(solution)/shard_map/ppermute | solution.py:270
  45.5 6.5 %collective-permute-start.7 = (f32[32,512]{1,0:T(8,128)S(1)}, f32[32,512]{1,0:T(8,128)S(1)}, u32[]{:S(2)}, u32[]{:S(2)}) collective-permute-start(f32[32,512]{1,0:T(8,128)S(1)} %fusion.9.own), channel_id=1, source_target_pairs={{8,0},{12,4},{16,8},{20,12},{24,16},{28,20},{32,24},{36,28},{40,32... | collective-permute-start | bytes 196616 | tf_op jit(solution)/shard_map/ppermute | solution.py:270
  52.1 8.8 %collective-permute-start.8 = (f32[2,32,512]{2,1,0:T(8,128)S(1)}, f32[2,32,512]{2,1,0:T(8,128)S(1)}, u32[]{:S(2)}, u32[]{:S(2)}) collective-permute-start(f32[2,32,512]{2,1,0:T(8,128)S(1)} %pad_maximum_fusion.1), channel_id=1, source_target_pairs={{0,4},{4,0},{1,5},{5,1},{2,6},{6,2},{3,7},{7,3},{8,12},{12,8},{9,1... | collective-permute-start | bytes 393224 | tf_op jit(solution)/shard_map/ppermute | solution.py:274
  56.9 11.1 %all-to-all-start = ((f32[4,32,512]{2,1,0:T(8,128)}), f32[4,32,512]{2,1,0:T(8,128)S(1)}, u32[]{:S(2)}, u32[]{:S(2)}) async-start(f32[4,32,512]{2,1,0:T(8,128)} %broadcast_in_dim.20), calls=%async_computation | async-start | bytes 524288 | tf_op jit(solution)/shard_map/all_to_all | solution.py:280
  60.9 1.7 copy-start.3
  65.8 17.0 %collective-permute-start.9 = (f32[2,32,512]{2,1,0:T(8,128)S(1)}, f32[2,32,512]{2,1,0:T(8,128)S(1)}, u32[]{:S(2)}, u32[]{:S(2)}) collective-permute-start(f32[2,32,512]{2,1,0:T(8,128)S(1)} %get-tuple-element.29), channel_id=1, source_target_pairs={{0,4},{4,0},{1,5},{5,1},{2,6},{6,2},{3,7},{7,3},{8,12},{12,8},{9,1... | collective-permute-start | bytes 393224 | tf_op jit(solution)/shard_map/ppermute | solution.py:274
  69.1 21.5 %all-to-all-start.1 = ((f32[16,8,128]{2,1,0:T(8,128)}), f32[16,8,128]{2,1,0:T(8,128)S(1)}, u32[]{:S(2)}, u32[]{:S(2)}) async-start(f32[16,8,128]{2,1,0:T(8,128)} %bitcast.7), calls=%async_computation.1 | async-start | bytes 131072 | tf_op jit(solution)/shard_map/all_to_all | solution.py:286
  82.8 31.9 %collective-permute-start.11 = (f32[32,512]{1,0:T(8,128)S(1)}, f32[32,512]{1,0:T(8,128)S(1)}, u32[]{:S(2)}, u32[]{:S(2)}) collective-permute-start(f32[32,512]{1,0:T(8,128)S(1)} %get-tuple-element.45), channel_id=1, source_target_pairs={{8,0},{12,4},{16,8},{20,12},{24,16},{28,20},{32,24},{36,28},{40,32... | collective-permute-start | bytes 196616 | tf_op jit(solution)/shard_map/ppermute | solution.py:270
  84.1 30.6 %collective-permute-start.10 = (f32[32,512]{1,0:T(8,128)S(1)}, f32[32,512]{1,0:T(8,128)S(1)}, u32[]{:S(2)}, u32[]{:S(2)}) collective-permute-start(f32[32,512]{1,0:T(8,128)S(1)} %get-tuple-element.44), channel_id=1, source_target_pairs={{0,8},{4,12},{8,16},{12,20},{16,24},{20,28},{24,32},{28,36},{32,40... | collective-permute-start | bytes 196616 | tf_op jit(solution)/shard_map/ppermute | solution.py:270
  108.1 14.4 %all-to-all-start.3 = ((f32[16,8,128]{2,1,0:T(8,128)}), f32[16,8,128]{2,1,0:T(8,128)S(1)}, u32[]{:S(2)}, u32[]{:S(2)}) async-start(f32[16,8,128]{2,1,0:T(8,128)} %broadcast_in_dim.22), calls=%async_computation.3 | async-start | bytes 131072 | tf_op jit(solution)/shard_map/all_to_all | solution.py:280
  123.2 10.2 %all-to-all-start.4 = ((f32[4,1,32,512]{3,2,1,0:T(8,128)}), f32[4,1,32,512]{3,2,1,0:T(8,128)S(1)}, u32[]{:S(2)}, u32[]{:S(2)}) async-start(f32[4,1,32,512]{3,2,1,0:T(8,128)} %broadcast_in_dim.24), calls=%async_computation.4 | async-start | bytes 524288 | tf_op jit(solution)/shard_map/all_to_all | solution.py:280
  134.9 3.3 %collective-permute-start.12 = (f32[32,512]{1,0:T(8,128)S(1)}, f32[32,512]{1,0:T(8,128)S(1)}, u32[]{:S(2)}, u32[]{:S(2)}) collective-permute-start(f32[32,512]{1,0:T(8,128)S(1)} %get-tuple-element.33.own), channel_id=1, source_target_pairs={{0,8},{4,12},{8,16},{12,20},{16,24},{20,28},{24,32},{28,36},{32,40... | collective-permute-start | bytes 196616 | tf_op jit(solution)/shard_map/ppermute | solution.py:270
  136.8 5.0 %collective-permute-start.13 = (f32[32,512]{1,0:T(8,128)S(1)}, f32[32,512]{1,0:T(8,128)S(1)}, u32[]{:S(2)}, u32[]{:S(2)}) collective-permute-start(f32[32,512]{1,0:T(8,128)S(1)} %get-tuple-element.33.own), channel_id=1, source_target_pairs={{8,0},{12,4},{16,8},{20,12},{24,16},{28,20},{32,24},{36,28},{40,32... | collective-permute-start | bytes 196616 | tf_op jit(solution)/shard_map/ppermute | solution.py:270
  141.9 6.0 %collective-permute-start.14 = (f32[2,32,512]{2,1,0:T(8,128)S(1)}, f32[2,32,512]{2,1,0:T(8,128)S(1)}, u32[]{:S(2)}, u32[]{:S(2)}) collective-permute-start(f32[2,32,512]{2,1,0:T(8,128)S(1)} %pad_maximum_fusion.2), channel_id=1, source_target_pairs={{0,4},{4,0},{1,5},{5,1},{2,6},{6,2},{3,7},{7,3},{8,12},{12,8},{9,1... | collective-permute-start | bytes 393224 | tf_op jit(solution)/shard_map/ppermute | solution.py:274
  147.9 1.7 copy-start.4
  152.8 8.6 %collective-permute-start.15 = (f32[2,32,512]{2,1,0:T(8,128)S(1)}, f32[2,32,512]{2,1,0:T(8,128)S(1)}, u32[]{:S(2)}, u32[]{:S(2)}) collective-permute-start(f32[2,32,512]{2,1,0:T(8,128)S(1)} %get-tuple-element.35), channel_id=1, source_target_pairs={{0,4},{4,0},{1,5},{5,1},{2,6},{6,2},{3,7},{7,3},{8,12},{12,8},{9,1... | collective-permute-start | bytes 393224 | tf_op jit(solution)/shard_map/ppermute | solution.py:274
  155.1 14.1 %all-to-all-start.5 = ((f32[16,8,128]{2,1,0:T(8,128)}), f32[16,8,128]{2,1,0:T(8,128)S(1)}, u32[]{:S(2)}, u32[]{:S(2)}) async-start(f32[16,8,128]{2,1,0:T(8,128)} %bitcast.13), calls=%async_computation.5 | async-start | bytes 131072 | tf_op jit(solution)/shard_map/all_to_all | solution.py:286
  161.4 25.2 %collective-permute-start.17 = (f32[32,512]{1,0:T(8,128)S(1)}, f32[32,512]{1,0:T(8,128)S(1)}, u32[]{:S(2)}, u32[]{:S(2)}) collective-permute-start(f32[32,512]{1,0:T(8,128)S(1)} %get-tuple-element.43), channel_id=1, source_target_pairs={{8,0},{12,4},{16,8},{20,12},{24,16},{28,20},{32,24},{36,28},{40,32... | collective-permute-start | bytes 196616 | tf_op jit(solution)/shard_map/ppermute | solution.py:270
  162.7 23.9 %collective-permute-start.16 = (f32[32,512]{1,0:T(8,128)S(1)}, f32[32,512]{1,0:T(8,128)S(1)}, u32[]{:S(2)}, u32[]{:S(2)}) collective-permute-start(f32[32,512]{1,0:T(8,128)S(1)} %get-tuple-element.42), channel_id=1, source_target_pairs={{0,8},{4,12},{8,16},{12,20},{16,24},{20,28},{24,32},{28,36},{32,40... | collective-permute-start | bytes 196616 | tf_op jit(solution)/shard_map/ppermute | solution.py:270
  180.0 14.4 %all-to-all-start.7 = ((f32[16,8,128]{2,1,0:T(8,128)}), f32[16,8,128]{2,1,0:T(8,128)S(1)}, u32[]{:S(2)}, u32[]{:S(2)}) async-start(f32[16,8,128]{2,1,0:T(8,128)} %broadcast_in_dim.26), calls=%async_computation.7 | async-start | bytes 131072 | tf_op jit(solution)/shard_map/all_to_all | solution.py:280
  195.3 12.9 %all-to-all-start.8 = ((f32[4,2,32,512]{3,2,1,0:T(8,128)}), f32[4,2,32,512]{3,2,1,0:T(8,128)S(1)}, u32[]{:S(2)}, u32[]{:S(2)}) async-start(f32[4,2,32,512]{3,2,1,0:T(8,128)} %broadcast_in_dim.27), calls=%async_computation.8 | async-start | bytes 1048576 | tf_op jit(solution)/shard_map/all_to_all | solution.py:280

commit v2 on v1

--- a/solution.py
+++ b/solution.py
@@ -22,39 +22,58 @@
     return high, low
 
 
-def band_kernel(rows_ref, cols_ref, tiles_ref, high_ref, low_ref, total):
-    group = pl.program_id(0)
-    in_group, size, _ = tiles_ref.shape
-    blocks = total.shape[0] // size
-    total[...] = jnp.zeros_like(total)
-    for s in range(in_group):
-        row, col = rows_ref[group * in_group + s], cols_ref[group * in_group + s]
-
-        @pl.when(col >= 0)
-        def _():
-            at = (
-                pl.ds(pl.multiple_of(row * size, size), size),
-                pl.ds(pl.multiple_of(lax.rem(col, blocks) * size, size), size),
-            )
-            total[at] += tiles_ref[s]
-
-    high_ref[0], low_ref[0] = halves(total[...])
+def band_kernel(rows_ref, cols_ref, tiles_hbm, high_hbm, low_hbm, tiles, total, high, low, sems):
+    groups, width, _ = high.shape
+    slots, size, _ = tiles.shape
+    in_group, blocks = slots // groups, width // size
+    arrive = []
+    for g in range(groups):
+        part = pl.ds(g * in_group, in_group)
+        arrive.append(pltpu.make_async_copy(tiles_hbm.at[part], tiles.at[part], sems.at[0, g]))
+        arrive[-1].start()
+    leave = []
+    for g in range(groups):
+        arrive[g].wait()
+        total[...] = jnp.zeros_like(total)
+        for s in range(in_group):
+            slot = g * in_group + s
+            row, col = rows_ref[slot], cols_ref[slot]
+
+            @pl.when(col >= 0)
+            def _():
+                at = (
+                    pl.ds(pl.multiple_of(row * size, size), size),
+                    pl.ds(pl.multiple_of(lax.rem(col, blocks) * size, size), size),
+                )
+                total[at] += tiles[slot]
+
+        high[g], low[g] = halves(total[...])
+        leave += [
+            pltpu.make_async_copy(high.at[g], high_hbm.at[g], sems.at[1, g]),
+            pltpu.make_async_copy(low.at[g], low_hbm.at[g], sems.at[2, g]),
+        ]
+        leave[-2].start()
+        leave[-1].start()
+    for copy in leave:
+        copy.wait()
 
 
 def operator_band(tile_values, tile_rows, tile_cols, width):
-    slots, size, _ = tile_values.shape
-    in_group = slots // GROUPS
+    smem, hbm = pl.BlockSpec(memory_space=pltpu.SMEM), pl.BlockSpec(memory_space=pl.ANY)
     piece = jax.ShapeDtypeStruct((GROUPS, width, width), jnp.bfloat16)
     return pl.pallas_call(
         band_kernel,
-        grid_spec=pltpu.PrefetchScalarGridSpec(
-            num_scalar_prefetch=2,
-            grid=(GROUPS,),
-            in_specs=[pl.BlockSpec((in_group, size, size), lambda g, rows, cols: (g, 0, 0))],
-            out_specs=[pl.BlockSpec((1, width, width), lambda g, rows, cols: (g, 0, 0))] * 2,
-            scratch_shapes=[pltpu.VMEM((width, width), jnp.float32)],
-        ),
+        in_specs=[smem, smem, hbm],
+        out_specs=[hbm, hbm],
         out_shape=[piece, piece],
+        scratch_shapes=[
+            pltpu.VMEM(tile_values.shape, jnp.float32),
+            pltpu.VMEM((width, width), jnp.float32),
+            pltpu.VMEM(piece.shape, piece.dtype),
+            pltpu.VMEM(piece.shape, piece.dtype),
+            pltpu.SemaphoreType.DMA((3, GROUPS)),
+        ],
+        compiler_params=pltpu.CompilerParams(vmem_limit_bytes=63 * MIB),
         name="operator_band",
     )(tile_rows, tile_cols, tile_values)
 
@@ -96,7 +115,7 @@
 
 
 def apply_operator(core, below, above, own, got, high, low):
-    vmem, hbm = pl.BlockSpec(memory_space=pltpu.VMEM), pl.BlockSpec(memory_space=pltpu.HBM)
+    vmem, hbm = pl.BlockSpec(memory_space=pltpu.VMEM), pl.BlockSpec(memory_space=pl.ANY)
     one = jax.ShapeDtypeStruct(own.shape, jnp.float32)
     two = jax.ShapeDtypeStruct(got.shape, jnp.float32)
     return pl.pallas_call(
@@ -109,7 +128,7 @@
             pltpu.VMEM(low.shape, low.dtype),
             pltpu.SemaphoreType.DMA((2, GROUPS)),
         ],
-        compiler_params=pltpu.CompilerParams(vmem_limit_bytes=16 * MIB),
+        compiler_params=pltpu.CompilerParams(vmem_limit_bytes=32 * MIB),
         name="apply_operator",
     )(core, below, above, own, got, high, low)
 
@@ -280,10 +299,14 @@
     return lax.all_to_all(copies, axes, 0, 0)
 
 
-def summed(share):
-    size = share.shape[0]
+def scattered(whole):
+    size = whole.shape[0]
     line = lax.axis_size(("z", "core"))
-    share = lax.all_to_all(share.reshape(line, size // line, size), ("z", "core"), 0, 0).sum(axis=0)
+    return lax.all_to_all(whole.reshape(line, size // line, size), ("z", "core"), 0, 0).sum(axis=0)
+
+
+def gathered(share):
+    size = share.shape[1]
     run = spread(share, "y").sum(axis=0)
     return spread(run, ("z", "core")).reshape(size, size)
 
@@ -296,28 +319,30 @@
     first = core == 0
     place = lax.axis_index("x").astype(jnp.int32).reshape(1)
     core = core.reshape(1)
-    high, low = operator_band(tile_values, tile_rows, tile_cols, row_width)
-
-    def operator_pass(vectors):
+    bands = operator_band(tile_values, tile_rows, tile_cols, row_width)
+
+    def operator_pass(vectors, beside=()):
         below, above = shifted(vectors, 2), shifted(vectors, -2)
+        below, above, *beside = lax.optimization_barrier((below, above, *beside))
         got = swapped(jnp.stack([vectors, jnp.where(first, above, below)]))
-        images, kept, crossing, down, up = apply_operator(core, below, above, vectors, got, high, low)
+        images, kept, crossing, down, up = apply_operator(core, below, above, vectors, got, *bands)
         got = swapped(crossing)
         up = jnp.where(first, up + got[1], up)
         down = jnp.where(first, down, down + got[1])
-        return images, kept + got[0] + shifted(up, 2) + shifted(down, -2)
-
-    images, pulled = operator_pass(start_vectors)
+        return images, kept + got[0] + shifted(up, 2) + shifted(down, -2), beside
+
+    images, pulled, bands = operator_pass(start_vectors, bands)
     all_vectors = spread(pulled, "x").reshape(all_count, row_width)
-    gram = gram_share(all_vectors)
+    share = scattered(gram_share(all_vectors))
     for iteration in range(1, ITERS):
-        images, ahead = operator_pass(pulled)
-        inverse = cholesky_inverse(summed(gram))
-        parts = [ahead, images] if iteration == ITERS - 1 else [ahead]
-        raw = spread(jnp.stack(parts), "x")
+        last = iteration == ITERS - 1
+        images, ahead, taken = operator_pass(pulled, [share] if last else [])
+        inverse = cholesky_inverse(gathered(*(taken or [share])))
+        raw = spread(jnp.stack([ahead, images] if last else [ahead]), "x")
         all_vectors, pulled, gram = advance(place, inverse, raw, scale)
+        share = scattered(gram)
     images = pulled
-    vectors = whiten(place, summed(gram), all_vectors, own, scale)
+    vectors = whiten(place, gathered(share), all_vectors, own, scale)
     return (vectors, images)
 
 

time: 249 us -> 242 us (0.972)
  waiting for transfers between devices: 43.5 us -> 37.8 us
  blocking collectives: 59 us -> 62.2 us
  Pallas kernels: 35.1 us -> 32.5 us
    ppermute x12, waiting for transfers between devices: 14.8 us -> 6.82 us  [shifted(): lax.ppermute(value, ROWS, [(source, source + steps) for source in range(l...]
    all_to_all x4, blocking collectives: 47.8 us -> 51 us  [spread(): return lax.all_to_all(copies, axes, 0, 0)]
    pallas_call x1, Pallas kernels: 7.04 us -> 4.42 us  [operator_band(): pl.pallas_call(band_kernel, in_specs=[smem, smem, hbm], out_specs=[hbm, h...]
  transfers between devices with their start and end apart: 25 -> 25, of which waited for: 14 -> 15; matrix products, arithmetic and copies ran while one was open for 1% -> 1% of each run, Pallas kernels for 8% -> 7%
where the time goes in v2:
time: 242 us; the launch traced here: 240 us
  starting transfers between devices  96 us (40%)
  blocking collectives  62.2 us (26%)
  waiting for transfers between devices  37.8 us (16%)
  Pallas kernels  32.5 us (13%)
  local copies, waits for them, and re-layouts  10.6 us (4%)
    all_to_all x4, blocking collectives, spread(): return lax.all_to_all(copies, axes, 0, 0)  51 us
    ppermute x12, starting transfers between devices, shifted(): lax.ppermute(value, ROWS, [(source, source + steps) for source in range(l...  32 us
    all_to_all x5, starting transfers between devices, spread(): return lax.all_to_all(copies, axes, 0, 0)  24.8 us
    all_to_all x5, waiting for transfers between devices, spread(): return lax.all_to_all(copies, axes, 0, 0)  21.5 us
    ppermute x6, starting transfers between devices, swapped(): return lax.ppermute(value, 'core', [(0, 1), (1, 0)])  20.6 us
    all_to_all x2, starting transfers between devices, scattered(): lax.all_to_all(whole.reshape(line, size // line, size), ('z', 'core'), 0, 0)  18.6 us
    all_to_all x1, blocking collectives, scattered(): lax.all_to_all(whole.reshape(line, size // line, size), ('z', 'core'), 0, 0)  11.2 us
    pallas_call x3, Pallas kernels, apply_operator(): pl.pallas_call(apply_kernel, in_specs=[pl.BlockSpec(memory_space=pltpu.SM...  9.41 us
  transfers between devices with their start and end apart: 25, of which 15 were waited for; matrix products, arithmetic and copies ran while one was open for 1% of the time, Pallas kernels for 7%

profile of v2, /device:TPU:1, one launch (start us, length us, event | category | flops | bytes accessed | tf_op | source)
XLA Modules:
  0.0 240.4 jit_solution(6174467660383604908)
XLA Ops:
  0.6 4.9 %collective-permute-start = (f32[32,512]{1,0:T(8,128)}, f32[32,512]{1,0:T(8,128)S(1)}, u32[]{:S(2)}, u32[]{:S(2)}) collective-permute-start(f32[32,512]{1,0:T(8,128)} %own.1), channel_id=1, source_target_pairs={{0,8},{4,12},{8,16},{12,20},{16,24},{20,28},{24,32},{28,36},{32,40... | collective-permute-start | bytes 196616 | tf_op jit(solution)/shard_map/ppermute | solution.py:289
  6.9 4.4 %operator_band.1 = (bf16[5,512,512]{2,1,0:T(8,128)(2,1)}, bf16[5,512,512]{2,1,0:T(8,128)(2,1)}) custom-call(s32[15]{0:T(128)} %rows_ref.1, s32[15]{0:T(128)} %cols_ref.1, f32[15,256,256]{2,1,0:T(8,128)} %tiles_hbm.1), custom_call_target="tpu_custom_call" | custom-call | tf_op jit(solution)/shard_map/operator_band/pallas_call | solution.py:64
  11.5 5.7 %collective-permute-start.2 = (f32[2,32,512]{2,1,0:T(8,128)S(1)}, f32[2,32,512]{2,1,0:T(8,128)S(1)}, u32[]{:S(2)}, u32[]{:S(2)}) collective-permute-start(f32[2,32,512]{2,1,0:T(8,128)S(1)} %pad_maximum_fusion), channel_id=1, source_target_pairs={{0,4},{4,0},{1,5},{5,1},{2,6},{6,2},{3,7},{7,3},{8,12},{12,8},{9,1... | collective-permute-start | bytes 393224 | tf_op jit(solution)/shard_map/ppermute | solution.py:293
  21.7 3.1 %apply_operator.3 = (f32[32,512]{1,0:T(8,128)}, f32[32,512]{1,0:T(8,128)S(1)}, f32[2,32,512]{2,1,0:T(8,128)S(1)}, f32[32,512]{1,0:T(8,128)S(1)}, f32[32,512]{1,0:T(8,128)S(1)}) custom-call(s32[1]{0:T(128)} %bitcast.1.core_ref, f32[32,512]{1,0:T(8,128)S(1)} %collective-permute-done.below, f32[32,512]{1,0:T(8,128)S(1)} %collective-permute-done.1.above, ...), custom_call_target="tpu_custom_call" | custom-call | tf_op jit(solution)/shard_map/apply_operator/pallas_call | solution.py:121
  29.4 4.3 %collective-permute-start.4 = (f32[32,512]{1,0:T(8,128)S(1)}, f32[32,512]{1,0:T(8,128)S(1)}, u32[]{:S(2)}, u32[]{:S(2)}) collective-permute-start(f32[32,512]{1,0:T(8,128)S(1)} %get-tuple-element.64), channel_id=1, source_target_pairs={{0,8},{4,12},{8,16},{12,20},{16,24},{20,28},{24,32},{28,36},{32,40... | collective-permute-start | bytes 196616 | tf_op jit(solution)/shard_map/ppermute | solution.py:289
  35.1 3.7 %collective-permute-start.6 = (f32[32,512]{1,0:T(8,128)S(1)}, f32[32,512]{1,0:T(8,128)S(1)}, u32[]{:S(2)}, u32[]{:S(2)}) collective-permute-start(f32[32,512]{1,0:T(8,128)S(1)} %fusion.9.own), channel_id=1, source_target_pairs={{0,8},{4,12},{8,16},{12,20},{16,24},{20,28},{24,32},{28,36},{32,40... | collective-permute-start | bytes 196616 | tf_op jit(solution)/shard_map/ppermute | solution.py:289
  40.1 5.0 %collective-permute-done.7.above = f32[32,512]{1,0:T(8,128)S(1)} collective-permute-done((f32[32,512]{1,0:T(8,128)S(1)}, f32[32,512]{1,0:T(8,128)S(1)}, u32[]{:S(2)}, u32[]{:S(2)}) %collective-permute-start.7) | collective-permute-done | bytes 65568 | tf_op jit(solution)/shard_map/ppermute | solution.py:289
  45.1 4.3 %collective-permute-start.8 = (f32[2,32,512]{2,1,0:T(8,128)S(1)}, f32[2,32,512]{2,1,0:T(8,128)S(1)}, u32[]{:S(2)}, u32[]{:S(2)}) collective-permute-start(f32[2,32,512]{2,1,0:T(8,128)S(1)} %pad_maximum_fusion.1), channel_id=1, source_target_pairs={{0,4},{4,0},{1,5},{5,1},{2,6},{6,2},{3,7},{7,3},{8,12},{12,8},{9,1... | collective-permute-start | bytes 393224 | tf_op jit(solution)/shard_map/ppermute | solution.py:293
  50.1 4.0 %all-to-all-start = ((f32[4,32,512]{2,1,0:T(8,128)}), f32[4,32,512]{2,1,0:T(8,128)S(1)}, u32[]{:S(2)}, u32[]{:S(2)}) async-start(f32[4,32,512]{2,1,0:T(8,128)} %broadcast_in_dim.20), calls=%async_computation | async-start | bytes 524288 | tf_op jit(solution)/shard_map/all_to_all | solution.py:299
  55.9 3.1 %apply_operator.4 = (f32[32,512]{1,0:T(8,128)}, f32[32,512]{1,0:T(8,128)S(1)}, f32[2,32,512]{2,1,0:T(8,128)S(1)}, f32[32,512]{1,0:T(8,128)S(1)}, f32[32,512]{1,0:T(8,128)S(1)}) custom-call(s32[1]{0:T(128)} %bitcast.1.core_ref, f32[32,512]{1,0:T(8,128)S(1)} %collective-permute-done.6.below, f32[32,512]{1,0:T(8,128)S(1)} %collective-permute-done.7.above, ...), custom_call_target="tpu_custom_call" | custom-call | tf_op jit(solution)/shard_map/apply_operator/pallas_call | solution.py:121
  62.3 13.8 %all-to-all-start.1 = ((f32[16,8,128]{2,1,0:T(8,128)}), f32[16,8,128]{2,1,0:T(8,128)S(1)}, u32[]{:S(2)}, u32[]{:S(2)}) async-start(f32[16,8,128]{2,1,0:T(8,128)} %bitcast.7), calls=%async_computation.1 | async-start | bytes 131072 | tf_op jit(solution)/shard_map/all_to_all | solution.py:305
  77.4 4.0 %collective-permute-start.10 = (f32[32,512]{1,0:T(8,128)S(1)}, f32[32,512]{1,0:T(8,128)S(1)}, u32[]{:S(2)}, u32[]{:S(2)}) collective-permute-start(f32[32,512]{1,0:T(8,128)S(1)} %get-tuple-element.62), channel_id=1, source_target_pairs={{0,8},{4,12},{8,16},{12,20},{16,24},{20,28},{24,32},{28,36},{32,40... | collective-permute-start | bytes 196616 | tf_op jit(solution)/shard_map/ppermute | solution.py:289
  83.8 16.9 %all_to_all.60 = f32[8,8,128]{2,1,0:T(8,128)S(1)} all-to-all(f32[8,8,128]{2,1,0:T(8,128)S(1)} %broadcast_in_dim.21), channel_id=1, replica_groups=mesh['y'=8,'z'=8,'core'=2,'x'=4] {'y'}, dimensions={0} | all-to-all | bytes 65536 | tf_op jit(solution)/shard_map/all_to_all | solution.py:299
  101.4 6.6 %all-to-all-start.3 = ((f32[16,8,128]{2,1,0:T(8,128)}), f32[16,8,128]{2,1,0:T(8,128)S(1)}, u32[]{:S(2)}, u32[]{:S(2)}) async-start(f32[16,8,128]{2,1,0:T(8,128)} %broadcast_in_dim.22), calls=%async_computation.3 | async-start | bytes 131072 | tf_op jit(solution)/shard_map/all_to_all | solution.py:299
  108.1 7.7 %all-to-all-done.3 = f32[16,8,128]{2,1,0:T(8,128)S(1)} async-done(((f32[16,8,128]{2,1,0:T(8,128)}), f32[16,8,128]{2,1,0:T(8,128)S(1)}, u32[]{:S(2)}, u32[]{:S(2)}) %all-to-all-start.3) | async-done | bytes 65568 | tf_op jit(solution)/shard_map/all_to_all | solution.py:299
  116.5 4.1 %all-to-all-start.4 = ((f32[4,1,32,512]{3,2,1,0:T(8,128)}), f32[4,1,32,512]{3,2,1,0:T(8,128)S(1)}, u32[]{:S(2)}, u32[]{:S(2)}) async-start(f32[4,1,32,512]{3,2,1,0:T(8,128)} %broadcast_in_dim.24), calls=%async_computation.4 | async-start | bytes 524288 | tf_op jit(solution)/shard_map/all_to_all | solution.py:299
  120.7 4.7 %cholesky_inverse.2.inverse_ref = f32[128,128]{1,0:T(8,128)S(1)} custom-call(f32[128,128]{1,0:T(8,128)S(1)} %bitcast.69), custom_call_target="tpu_custom_call" | custom-call | tf_op jit(solution)/shard_map/cholesky_inverse/pallas_call | solution.py:254
  128.2 4.8 %all-to-all-start.5 = ((f32[16,8,128]{2,1,0:T(8,128)}), f32[16,8,128]{2,1,0:T(8,128)S(1)}, u32[]{:S(2)}, u32[]{:S(2)}) async-start(f32[16,8,128]{2,1,0:T(8,128)} %bitcast.13), calls=%async_computation.5 | async-start | bytes 131072 | tf_op jit(solution)/shard_map/all_to_all | solution.py:305
  133.1 3.3 %collective-permute-start.12 = (f32[32,512]{1,0:T(8,128)S(1)}, f32[32,512]{1,0:T(8,128)S(1)}, u32[]{:S(2)}, u32[]{:S(2)}) collective-permute-start(f32[32,512]{1,0:T(8,128)S(1)} %get-tuple-element.47.own), channel_id=1, source_target_pairs={{0,8},{4,12},{8,16},{12,20},{16,24},{20,28},{24,32},{28,36},{32,40... | collective-permute-start | bytes 196616 | tf_op jit(solution)/shard_map/ppermute | solution.py:289
  137.6 3.3 %all-to-all-done.5 = f32[16,8,128]{2,1,0:T(8,128)S(1)} async-done(((f32[16,8,128]{2,1,0:T(8,128)}), f32[16,8,128]{2,1,0:T(8,128)S(1)}, u32[]{:S(2)}, u32[]{:S(2)}) %all-to-all-start.5) | async-done | bytes 65568 | tf_op jit(solution)/shard_map/all_to_all | solution.py:305
  141.4 3.9 %collective-permute-start.14 = (f32[2,32,512]{2,1,0:T(8,128)S(1)}, f32[2,32,512]{2,1,0:T(8,128)S(1)}, u32[]{:S(2)}, u32[]{:S(2)}) collective-permute-start(f32[2,32,512]{2,1,0:T(8,128)S(1)} %pad_maximum_fusion.2), channel_id=1, source_target_pairs={{0,4},{4,0},{1,5},{5,1},{2,6},{6,2},{3,7},{7,3},{8,12},{12,8},{9,1... | collective-permute-start | bytes 393224 | tf_op jit(solution)/shard_map/ppermute | solution.py:293
  155.5 4.0 %collective-permute-start.16 = (f32[32,512]{1,0:T(8,128)S(1)}, f32[32,512]{1,0:T(8,128)S(1)}, u32[]{:S(2)}, u32[]{:S(2)}) collective-permute-start(f32[32,512]{1,0:T(8,128)S(1)} %get-tuple-element.60), channel_id=1, source_target_pairs={{0,8},{4,12},{8,16},{12,20},{16,24},{20,28},{24,32},{28,36},{32,40... | collective-permute-start | bytes 196616 | tf_op jit(solution)/shard_map/ppermute | solution.py:289
  159.5 13.3 %all_to_all.61 = f32[8,8,128]{2,1,0:T(8,128)S(1)} all-to-all(f32[8,8,128]{2,1,0:T(8,128)S(1)} %broadcast_in_dim.25), channel_id=1, replica_groups=mesh['y'=8,'z'=8,'core'=2,'x'=4] {'y'}, dimensions={0} | all-to-all | bytes 65536 | tf_op jit(solution)/shard_map/all_to_all | solution.py:299
  173.5 6.6 %all-to-all-start.7 = ((f32[16,8,128]{2,1,0:T(8,128)}), f32[16,8,128]{2,1,0:T(8,128)S(1)}, u32[]{:S(2)}, u32[]{:S(2)}) async-start(f32[16,8,128]{2,1,0:T(8,128)} %broadcast_in_dim.26), calls=%async_computation.7 | async-start | bytes 131072 | tf_op jit(solution)/shard_map/all_to_all | solution.py:299
  180.1 7.7 %all-to-all-done.7 = f32[16,8,128]{2,1,0:T(8,128)S(1)} async-done(((f32[16,8,128]{2,1,0:T(8,128)}), f32[16,8,128]{2,1,0:T(8,128)S(1)}, u32[]{:S(2)}, u32[]{:S(2)}) %all-to-all-start.7) | async-done | bytes 65568 | tf_op jit(solution)/shard_map/all_to_all | solution.py:299
  188.7 3.5 %all-to-all-start.8 = ((f32[4,2,32,512]{3,2,1,0:T(8,128)}), f32[4,2,32,512]{3,2,1,0:T(8,128)S(1)}, u32[]{:S(2)}, u32[]{:S(2)}) async-start(f32[4,2,32,512]{3,2,1,0:T(8,128)} %broadcast_in_dim.27), calls=%async_computation.8 | async-start | bytes 1048576 | tf_op jit(solution)/shard_map/all_to_all | solution.py:299
  192.2 4.7 %cholesky_inverse.3.inverse_ref = f32[128,128]{1,0:T(8,128)S(1)} custom-call(f32[128,128]{1,0:T(8,128)S(1)} %bitcast.70), custom_call_target="tpu_custom_call" | custom-call | tf_op jit(solution)/shard_map/cholesky_inverse/pallas_call | solution.py:254
  196.9 4.7 %all-to-all-done.8.raw_ref = f32[4,2,32,512]{3,2,1,0:T(8,128)S(1)} async-done(((f32[4,2,32,512]{3,2,1,0:T(8,128)}), f32[4,2,32,512]{3,2,1,0:T(8,128)S(1)}, u32[]{:S(2)}, u32[]{:S(2)}) %all-to-all-start.8) | async-done | bytes 524320 | tf_op jit(solution)/shard_map/all_to_all | solution.py:299
  202.9 11.2 %all_to_all.62 = f32[16,8,128]{2,1,0:T(8,128)S(1)} all-to-all(f32[16,8,128]{2,1,0:T(8,128)S(1)} %bitcast.72), channel_id=1, replica_groups=mesh['y'=8,'z'=8,'core'=2,'x'=4] {'z','core'}, dimensions={0} | all-to-all | bytes 131072 | tf_op jit(solution)/shard_map/all_to_all | solution.py:305
  214.1 9.2 %all_to_all.63 = f32[8,8,128]{2,1,0:T(8,128)S(1)} all-to-all(f32[8,8,128]{2,1,0:T(8,128)S(1)} %broadcast_in_dim.28), channel_id=1, replica_groups=mesh['y'=8,'z'=8,'core'=2,'x'=4] {'y'}, dimensions={0} | all-to-all | bytes 65536 | tf_op jit(solution)/shard_map/all_to_all | solution.py:299
  223.4 11.5 %all_to_all.64 = f32[16,8,128]{2,1,0:T(8,128)S(1)} all-to-all(f32[16,8,128]{2,1,0:T(8,128)S(1)} %broadcast_in_dim.29), channel_id=1, replica_groups=mesh['y'=8,'z'=8,'core'=2,'x'=4] {'z','core'}, dimensions={0} | all-to-all | bytes 131072 | tf_op jit(solution)/shard_map/all_to_all | solution.py:299
  234.9 5.5 %whiten.1 = f32[32,512]{1,0:T(8,128)} custom-call(s32[1]{0:T(128)} %bitcast.place_ref, f32[128,128]{1,0:T(8,128)S(1)} %bitcast.71, f32[128,512]{1,0:T(8,128)S(1)} %get-tuple-element.58.all_ref), custom_call_target="tpu_custom_call" | custom-call | tf_op jit(solution)/shard_map/whiten/pallas_call | solution.py:275
  (73 shorter events, 41.6 us)
Async XLA Ops:
  0.6 10.8 %copy-start.5 = (f32[32,512]{1,0:T(8,128)S(1)}, f32[32,512]{1,0:T(8,128)}, u32[]{:S(2)}) copy-start(f32[32,512]{1,0:T(8,128)} %own.1) | copy-start | bytes 196612
  0.6 10.7 %collective-permute-start = (f32[32,512]{1,0:T(8,128)}, f32[32,512]{1,0:T(8,128)S(1)}, u32[]{:S(2)}, u32[]{:S(2)}) collective-permute-start(f32[32,512]{1,0:T(8,128)} %own.1), channel_id=1, source_target_pairs={{0,8},{4,12},{8,16},{12,20},{16,24},{20,28},{24,32},{28,36},{32,40... | collective-permute-start | bytes 196616 | tf_op jit(solution)/shard_map/ppermute | solution.py:289
  5.6 5.9 %collective-permute-start.1 = (f32[32,512]{1,0:T(8,128)}, f32[32,512]{1,0:T(8,128)S(1)}, u32[]{:S(2)}, u32[]{:S(2)}) collective-permute-start(f32[32,512]{1,0:T(8,128)} %own.1), channel_id=1, source_target_pairs={{8,0},{12,4},{16,8},{20,12},{24,16},{28,20},{32,24},{36,28},{40,32... | collective-permute-start | bytes 196616 | tf_op jit(solution)/shard_map/ppermute | solution.py:289
  11.5 6.7 %collective-permute-start.2 = (f32[2,32,512]{2,1,0:T(8,128)S(1)}, f32[2,32,512]{2,1,0:T(8,128)S(1)}, u32[]{:S(2)}, u32[]{:S(2)}) collective-permute-start(f32[2,32,512]{2,1,0:T(8,128)S(1)} %pad_maximum_fusion), channel_id=1, source_target_pairs={{0,4},{4,0},{1,5},{5,1},{2,6},{6,2},{3,7},{7,3},{8,12},{12,8},{9,1... | collective-permute-start | bytes 393224 | tf_op jit(solution)/shard_map/ppermute | solution.py:293
  18.2 1.7 copy-start
  19.9 1.7 copy-start.2
  21.7 32.5 %copy-start.1 = (bf16[5,512,512]{2,1,0:T(8,128)(2,1)S(1)}, bf16[5,512,512]{2,1,0:T(8,128)(2,1)}, u32[]{:S(2)}) copy-start(bf16[5,512,512]{2,1,0:T(8,128)(2,1)} %get-tuple-element.41.high_hbm) | copy-start | bytes 7864324
  24.8 3.2 %collective-permute-start.3 = (f32[2,32,512]{2,1,0:T(8,128)S(1)}, f32[2,32,512]{2,1,0:T(8,128)S(1)}, u32[]{:S(2)}, u32[]{:S(2)}) collective-permute-start(f32[2,32,512]{2,1,0:T(8,128)S(1)} %get-tuple-element.36), channel_id=1, source_target_pairs={{0,4},{4,0},{1,5},{5,1},{2,6},{6,2},{3,7},{7,3},{8,12},{12,8},{9,1... | collective-permute-start | bytes 393224 | tf_op jit(solution)/shard_map/ppermute | solution.py:293
  28.1 5.8 %collective-permute-start.5 = (f32[32,512]{1,0:T(8,128)S(1)}, f32[32,512]{1,0:T(8,128)S(1)}, u32[]{:S(2)}, u32[]{:S(2)}) collective-permute-start(f32[32,512]{1,0:T(8,128)S(1)} %get-tuple-element.65), channel_id=1, source_target_pairs={{8,0},{12,4},{16,8},{20,12},{24,16},{28,20},{32,24},{36,28},{40,32... | collective-permute-start | bytes 196616 | tf_op jit(solution)/shard_map/ppermute | solution.py:289
  29.4 5.7 %collective-permute-start.4 = (f32[32,512]{1,0:T(8,128)S(1)}, f32[32,512]{1,0:T(8,128)S(1)}, u32[]{:S(2)}, u32[]{:S(2)}) collective-permute-start(f32[32,512]{1,0:T(8,128)S(1)} %get-tuple-element.64), channel_id=1, source_target_pairs={{0,8},{4,12},{8,16},{12,20},{16,24},{20,28},{24,32},{28,36},{32,40... | collective-permute-start | bytes 196616 | tf_op jit(solution)/shard_map/ppermute | solution.py:289
  35.1 5.0 %collective-permute-start.6 = (f32[32,512]{1,0:T(8,128)S(1)}, f32[32,512]{1,0:T(8,128)S(1)}, u32[]{:S(2)}, u32[]{:S(2)}) collective-permute-start(f32[32,512]{1,0:T(8,128)S(1)} %fusion.9.own), channel_id=1, source_target_pairs={{0,8},{4,12},{8,16},{12,20},{16,24},{20,28},{24,32},{28,36},{32,40... | collective-permute-start | bytes 196616 | tf_op jit(solution)/shard_map/ppermute | solution.py:289
  38.8 6.3 %collective-permute-start.7 = (f32[32,512]{1,0:T(8,128)S(1)}, f32[32,512]{1,0:T(8,128)S(1)}, u32[]{:S(2)}, u32[]{:S(2)}) collective-permute-start(f32[32,512]{1,0:T(8,128)S(1)} %fusion.9.own), channel_id=1, source_target_pairs={{8,0},{12,4},{16,8},{20,12},{24,16},{28,20},{32,24},{36,28},{40,32... | collective-permute-start | bytes 196616 | tf_op jit(solution)/shard_map/ppermute | solution.py:289
  45.1 9.0 %collective-permute-start.8 = (f32[2,32,512]{2,1,0:T(8,128)S(1)}, f32[2,32,512]{2,1,0:T(8,128)S(1)}, u32[]{:S(2)}, u32[]{:S(2)}) collective-permute-start(f32[2,32,512]{2,1,0:T(8,128)S(1)} %pad_maximum_fusion.1), channel_id=1, source_target_pairs={{0,4},{4,0},{1,5},{5,1},{2,6},{6,2},{3,7},{7,3},{8,12},{12,8},{9,1... | collective-permute-start | bytes 393224 | tf_op jit(solution)/shard_map/ppermute | solution.py:293
  50.1 11.1 %all-to-all-start = ((f32[4,32,512]{2,1,0:T(8,128)}), f32[4,32,512]{2,1,0:T(8,128)S(1)}, u32[]{:S(2)}, u32[]{:S(2)}) async-start(f32[4,32,512]{2,1,0:T(8,128)} %broadcast_in_dim.20), calls=%async_computation | async-start | bytes 524288 | tf_op jit(solution)/shard_map/all_to_all | solution.py:299
  54.2 1.7 copy-start.3
  59.1 17.0 %collective-permute-start.9 = (f32[2,32,512]{2,1,0:T(8,128)S(1)}, f32[2,32,512]{2,1,0:T(8,128)S(1)}, u32[]{:S(2)}, u32[]{:S(2)}) collective-permute-start(f32[2,32,512]{2,1,0:T(8,128)S(1)} %get-tuple-element.44), channel_id=1, source_target_pairs={{0,4},{4,0},{1,5},{5,1},{2,6},{6,2},{3,7},{7,3},{8,12},{12,8},{9,1... | collective-permute-start | bytes 393224 | tf_op jit(solution)/shard_map/ppermute | solution.py:293
  62.3 21.5 %all-to-all-start.1 = ((f32[16,8,128]{2,1,0:T(8,128)}), f32[16,8,128]{2,1,0:T(8,128)S(1)}, u32[]{:S(2)}, u32[]{:S(2)}) async-start(f32[16,8,128]{2,1,0:T(8,128)} %bitcast.7), calls=%async_computation.1 | async-start | bytes 131072 | tf_op jit(solution)/shard_map/all_to_all | solution.py:305
  76.1 32.0 %collective-permute-start.11 = (f32[32,512]{1,0:T(8,128)S(1)}, f32[32,512]{1,0:T(8,128)S(1)}, u32[]{:S(2)}, u32[]{:S(2)}) collective-permute-start(f32[32,512]{1,0:T(8,128)S(1)} %get-tuple-element.63), channel_id=1, source_target_pairs={{8,0},{12,4},{16,8},{20,12},{24,16},{28,20},{32,24},{36,28},{40,32... | collective-permute-start | bytes 196616 | tf_op jit(solution)/shard_map/ppermute | solution.py:289
  77.4 30.7 %collective-permute-start.10 = (f32[32,512]{1,0:T(8,128)S(1)}, f32[32,512]{1,0:T(8,128)S(1)}, u32[]{:S(2)}, u32[]{:S(2)}) collective-permute-start(f32[32,512]{1,0:T(8,128)S(1)} %get-tuple-element.62), channel_id=1, source_target_pairs={{0,8},{4,12},{8,16},{12,20},{16,24},{20,28},{24,32},{28,36},{32,40... | collective-permute-start | bytes 196616 | tf_op jit(solution)/shard_map/ppermute | solution.py:289
  101.4 14.4 %all-to-all-start.3 = ((f32[16,8,128]{2,1,0:T(8,128)}), f32[16,8,128]{2,1,0:T(8,128)S(1)}, u32[]{:S(2)}, u32[]{:S(2)}) async-start(f32[16,8,128]{2,1,0:T(8,128)} %broadcast_in_dim.22), calls=%async_computation.3 | async-start | bytes 131072 | tf_op jit(solution)/shard_map/all_to_all | solution.py:299
  116.5 10.2 %all-to-all-start.4 = ((f32[4,1,32,512]{3,2,1,0:T(8,128)}), f32[4,1,32,512]{3,2,1,0:T(8,128)S(1)}, u32[]{:S(2)}, u32[]{:S(2)}) async-start(f32[4,1,32,512]{3,2,1,0:T(8,128)} %broadcast_in_dim.24), calls=%async_computation.4 | async-start | bytes 524288 | tf_op jit(solution)/shard_map/all_to_all | solution.py:299
  128.2 12.7 %all-to-all-start.5 = ((f32[16,8,128]{2,1,0:T(8,128)}), f32[16,8,128]{2,1,0:T(8,128)S(1)}, u32[]{:S(2)}, u32[]{:S(2)}) async-start(f32[16,8,128]{2,1,0:T(8,128)} %bitcast.13), calls=%async_computation.5 | async-start | bytes 131072 | tf_op jit(solution)/shard_map/all_to_all | solution.py:305
  133.1 7.9 %collective-permute-start.12 = (f32[32,512]{1,0:T(8,128)S(1)}, f32[32,512]{1,0:T(8,128)S(1)}, u32[]{:S(2)}, u32[]{:S(2)}) collective-permute-start(f32[32,512]{1,0:T(8,128)S(1)} %get-tuple-element.47.own), channel_id=1, source_target_pairs={{0,8},{4,12},{8,16},{12,20},{16,24},{20,28},{24,32},{28,36},{32,40... | collective-permute-start | bytes 196616 | tf_op jit(solution)/shard_map/ppermute | solution.py:289
  136.3 5.0 %collective-permute-start.13 = (f32[32,512]{1,0:T(8,128)S(1)}, f32[32,512]{1,0:T(8,128)S(1)}, u32[]{:S(2)}, u32[]{:S(2)}) collective-permute-start(f32[32,512]{1,0:T(8,128)S(1)} %get-tuple-element.47.own), channel_id=1, source_target_pairs={{8,0},{12,4},{16,8},{20,12},{24,16},{28,20},{32,24},{36,28},{40,32... | collective-permute-start | bytes 196616 | tf_op jit(solution)/shard_map/ppermute | solution.py:289
  141.4 4.7 %collective-permute-start.14 = (f32[2,32,512]{2,1,0:T(8,128)S(1)}, f32[2,32,512]{2,1,0:T(8,128)S(1)}, u32[]{:S(2)}, u32[]{:S(2)}) collective-permute-start(f32[2,32,512]{2,1,0:T(8,128)S(1)} %pad_maximum_fusion.2), channel_id=1, source_target_pairs={{0,4},{4,0},{1,5},{5,1},{2,6},{6,2},{3,7},{7,3},{8,12},{12,8},{9,1... | collective-permute-start | bytes 393224 | tf_op jit(solution)/shard_map/ppermute | solution.py:293
  146.1 1.7 copy-start.4
  150.9 3.2 %collective-permute-start.15 = (f32[2,32,512]{2,1,0:T(8,128)S(1)}, f32[2,32,512]{2,1,0:T(8,128)S(1)}, u32[]{:S(2)}, u32[]{:S(2)}) collective-permute-start(f32[2,32,512]{2,1,0:T(8,128)S(1)} %get-tuple-element.53), channel_id=1, source_target_pairs={{0,4},{4,0},{1,5},{5,1},{2,6},{6,2},{3,7},{7,3},{8,12},{12,8},{9,1... | collective-permute-start | bytes 393224 | tf_op jit(solution)/shard_map/ppermute | solution.py:293
  154.2 25.9 %collective-permute-start.17 = (f32[32,512]{1,0:T(8,128)S(1)}, f32[32,512]{1,0:T(8,128)S(1)}, u32[]{:S(2)}, u32[]{:S(2)}) collective-permute-start(f32[32,512]{1,0:T(8,128)S(1)} %get-tuple-element.61), channel_id=1, source_target_pairs={{8,0},{12,4},{16,8},{20,12},{24,16},{28,20},{32,24},{36,28},{40,32... | collective-permute-start | bytes 196616 | tf_op jit(solution)/shard_map/ppermute | solution.py:289
  155.5 24.6 %collective-permute-start.16 = (f32[32,512]{1,0:T(8,128)S(1)}, f32[32,512]{1,0:T(8,128)S(1)}, u32[]{:S(2)}, u32[]{:S(2)}) collective-permute-start(f32[32,512]{1,0:T(8,128)S(1)} %get-tuple-element.60), channel_id=1, source_target_pairs={{0,8},{4,12},{8,16},{12,20},{16,24},{20,28},{24,32},{28,36},{32,40... | collective-permute-start | bytes 196616 | tf_op jit(solution)/shard_map/ppermute | solution.py:289
  173.5 14.4 %all-to-all-start.7 = ((f32[16,8,128]{2,1,0:T(8,128)}), f32[16,8,128]{2,1,0:T(8,128)S(1)}, u32[]{:S(2)}, u32[]{:S(2)}) async-start(f32[16,8,128]{2,1,0:T(8,128)} %broadcast_in_dim.26), calls=%async_computation.7 | async-start | bytes 131072 | tf_op jit(solution)/shard_map/all_to_all | solution.py:299
  188.7 12.9 %all-to-all-start.8 = ((f32[4,2,32,512]{3,2,1,0:T(8,128)}), f32[4,2,32,512]{3,2,1,0:T(8,128)S(1)}, u32[]{:S(2)}, u32[]{:S(2)}) async-start(f32[4,2,32,512]{3,2,1,0:T(8,128)} %broadcast_in_dim.27), calls=%async_computation.8 | async-start | bytes 1048576 | tf_op jit(solution)/shard_map/all_to_all | solution.py:299

commit v3 on v2

--- a/solution.py
+++ b/solution.py
@@ -22,16 +22,15 @@
     return high, low
 
 
-def band_kernel(rows_ref, cols_ref, tiles_hbm, high_hbm, low_hbm, tiles, total, high, low, sems):
+def band_kernel(rows_ref, cols_ref, tiles_hbm, high, low, tiles, total, sems):
     groups, width, _ = high.shape
     slots, size, _ = tiles.shape
     in_group, blocks = slots // groups, width // size
     arrive = []
     for g in range(groups):
         part = pl.ds(g * in_group, in_group)
-        arrive.append(pltpu.make_async_copy(tiles_hbm.at[part], tiles.at[part], sems.at[0, g]))
+        arrive.append(pltpu.make_async_copy(tiles_hbm.at[part], tiles.at[part], sems.at[g]))
         arrive[-1].start()
-    leave = []
     for g in range(groups):
         arrive[g].wait()
         total[...] = jnp.zeros_like(total)
@@ -48,32 +47,22 @@
                 total[at] += tiles[slot]
 
         high[g], low[g] = halves(total[...])
-        leave += [
-            pltpu.make_async_copy(high.at[g], high_hbm.at[g], sems.at[1, g]),
-            pltpu.make_async_copy(low.at[g], low_hbm.at[g], sems.at[2, g]),
-        ]
-        leave[-2].start()
-        leave[-1].start()
-    for copy in leave:
-        copy.wait()
 
 
 def operator_band(tile_values, tile_rows, tile_cols, width):
-    smem, hbm = pl.BlockSpec(memory_space=pltpu.SMEM), pl.BlockSpec(memory_space=pl.ANY)
+    smem, vmem = pl.BlockSpec(memory_space=pltpu.SMEM), pl.BlockSpec(memory_space=pltpu.VMEM)
     piece = jax.ShapeDtypeStruct((GROUPS, width, width), jnp.bfloat16)
     return pl.pallas_call(
         band_kernel,
-        in_specs=[smem, smem, hbm],
-        out_specs=[hbm, hbm],
+        in_specs=[smem, smem, pl.BlockSpec(memory_space=pl.ANY)],
+        out_specs=[vmem, vmem],
         out_shape=[piece, piece],
         scratch_shapes=[
             pltpu.VMEM(tile_values.shape, jnp.float32),
             pltpu.VMEM((width, width), jnp.float32),
-            pltpu.VMEM(piece.shape, piece.dtype),
-            pltpu.VMEM(piece.shape, piece.dtype),
-            pltpu.SemaphoreType.DMA((3, GROUPS)),
+            pltpu.SemaphoreType.DMA((GROUPS,)),
         ],
-        compiler_params=pltpu.CompilerParams(vmem_limit_bytes=63 * MIB),
+        compiler_params=pltpu.CompilerParams(vmem_limit_bytes=48 * MIB),
         name="operator_band",
     )(tile_rows, tile_cols, tile_values)
 
@@ -87,22 +76,11 @@
     return both[:count] + both[count:] + dot(high, band_low)
 
 
-def apply_kernel(core_ref, below, above, own, got, high_hbm, low_hbm, images, kept, crossing, down, up, high, low, sems):
+def apply_kernel(core_ref, below, above, own, got, high, low, images, kept, crossing, down, up):
     core = core_ref[0]
-    copies = []
-    for g in range(GROUPS):
-        pair = [
-            pltpu.make_async_copy(high_hbm.at[g], high.at[g], sems.at[0, g]),
-            pltpu.make_async_copy(low_hbm.at[g], low.at[g], sems.at[1, g]),
-        ]
-        for copy in pair:
-            copy.start()
-        copies.append(pair)
     near = [below[...], got[1 - core], own[...], got[core], above[...]]
     total = 0.0
     for g in range(GROUPS):
-        for copy in copies[g]:
-            copy.wait()
         total = total + products(*halves(near[g]), high[g], low[g], ((1,), (1,)))
     images[...] = total
     parts = halves(total)
@@ -115,20 +93,15 @@
 
 
 def apply_operator(core, below, above, own, got, high, low):
-    vmem, hbm = pl.BlockSpec(memory_space=pltpu.VMEM), pl.BlockSpec(memory_space=pl.ANY)
+    vmem = pl.BlockSpec(memory_space=pltpu.VMEM)
     one = jax.ShapeDtypeStruct(own.shape, jnp.float32)
     two = jax.ShapeDtypeStruct(got.shape, jnp.float32)
     return pl.pallas_call(
         apply_kernel,
-        in_specs=[pl.BlockSpec(memory_space=pltpu.SMEM)] + [vmem] * 4 + [hbm] * 2,
+        in_specs=[pl.BlockSpec(memory_space=pltpu.SMEM)] + [vmem] * 6,
         out_specs=[vmem] * 5,
         out_shape=[one, one, two, one, one],
-        scratch_shapes=[
-            pltpu.VMEM(high.shape, high.dtype),
-            pltpu.VMEM(low.shape, low.dtype),
-            pltpu.SemaphoreType.DMA((2, GROUPS)),
-        ],
-        compiler_params=pltpu.CompilerParams(vmem_limit_bytes=32 * MIB),
+        compiler_params=pltpu.CompilerParams(vmem_limit_bytes=16 * MIB),
         name="apply_operator",
     )(core, below, above, own, got, high, low)
 
@@ -336,8 +309,8 @@
     share = scattered(gram_share(all_vectors))
     for iteration in range(1, ITERS):
         last = iteration == ITERS - 1
-        images, ahead, taken = operator_pass(pulled, [share] if last else [])
-        inverse = cholesky_inverse(gathered(*(taken or [share])))
+        images, ahead, taken = operator_pass(pulled, [share])
+        inverse = cholesky_inverse(gathered(*taken))
         raw = spread(jnp.stack([ahead, images] if last else [ahead]), "x")
         all_vectors, pulled, gram = advance(place, inverse, raw, scale)
         share = scattered(gram)

time: 242 us -> 240 us (level)
  blocking collectives: 62.2 us -> 75.3 us
  starting transfers between devices: 96 us -> 84.3 us
  local copies, waits for them, and re-layouts: 10.6 us -> 7.73 us
    all_to_all x4 -> x5, blocking collectives: 51 us -> 64.1 us  [spread(): return lax.all_to_all(copies, axes, 0, 0)]
    all_to_all x5 -> x4, starting transfers between devices: 24.8 us -> 17.9 us  [spread(): return lax.all_to_all(copies, axes, 0, 0)]
    ppermute x12, starting transfers between devices: 32 us -> 29.1 us  [shifted(): lax.ppermute(value, ROWS, [(source, source + steps) for source in range(l...]
    all_to_all x5 -> x4, waiting for transfers between devices: 21.5 us -> 22.1 us  [spread(): return lax.all_to_all(copies, axes, 0, 0)]
  transfers between devices with their start and end apart: 25 -> 24, of which waited for: 15 -> 16; matrix products, arithmetic and copies ran while one was open for 1% -> 1% of each run, Pallas kernels for 7% -> 5%
where the time goes in v3:
time: 240 us; the launch traced here: 238 us
  starting transfers between devices  84.3 us (35%)
  blocking collectives  75.3 us (31%)
  waiting for transfers between devices  39.1 us (16%)
  Pallas kernels  30.6 us (13%)
  local copies, waits for them, and re-layouts  7.73 us (3%)
    all_to_all x5, blocking collectives, spread(): return lax.all_to_all(copies, axes, 0, 0)  64.1 us
    ppermute x12, starting transfers between devices, shifted(): lax.ppermute(value, ROWS, [(source, source + steps) for source in range(l...  29.1 us
    all_to_all x4, waiting for transfers between devices, spread(): return lax.all_to_all(copies, axes, 0, 0)  22.1 us
    ppermute x6, starting transfers between devices, swapped(): return lax.ppermute(value, 'core', [(0, 1), (1, 0)])  20.2 us
    all_to_all x4, starting transfers between devices, spread(): return lax.all_to_all(copies, axes, 0, 0)  17.9 us
    all_to_all x2, starting transfers between devices, scattered(): lax.all_to_all(whole.reshape(line, size // line, size), ('z', 'core'), 0, 0)  17.1 us
    all_to_all x1, blocking collectives, scattered(): lax.all_to_all(whole.reshape(line, size // line, size), ('z', 'core'), 0, 0)  11.2 us
    pallas_call x2, Pallas kernels, cholesky_inverse(): pl.pallas_call(functools.partial(inverse_kernel, panel=4), in_specs=[vmem...  9.4 us
  transfers between devices with their start and end apart: 24, of which 16 were waited for; matrix products, arithmetic and copies ran while one was open for 1% of the time, Pallas kernels for 5%

profile of v3, /device:TPU:1, one launch (start us, length us, event | category | flops | bytes accessed | tf_op | source)
XLA Modules:
  0.0 238.2 jit_solution(5270723921006007885)
XLA Ops:
  0.6 4.9 %collective-permute-start = (f32[32,512]{1,0:T(8,128)}, f32[32,512]{1,0:T(8,128)S(1)}, u32[]{:S(2)}, u32[]{:S(2)}) collective-permute-start(f32[32,512]{1,0:T(8,128)} %own.1), channel_id=1, source_target_pairs={{0,8},{4,12},{8,16},{12,20},{16,24},{20,28},{24,32},{28,36},{32,40... | collective-permute-start | bytes 196616 | tf_op jit(solution)/shard_map/ppermute | solution.py:262
  11.5 5.7 %collective-permute-start.2 = (f32[2,32,512]{2,1,0:T(8,128)S(1)}, f32[2,32,512]{2,1,0:T(8,128)S(1)}, u32[]{:S(2)}, u32[]{:S(2)}) collective-permute-start(f32[2,32,512]{2,1,0:T(8,128)S(1)} %pad_maximum_fusion), channel_id=1, source_target_pairs={{0,4},{4,0},{1,5},{5,1},{2,6},{6,2},{3,7},{7,3},{8,12},{12,8},{9,1... | collective-permute-start | bytes 393224 | tf_op jit(solution)/shard_map/ppermute | solution.py:266
  18.2 3.1 %apply_operator.3 = (f32[32,512]{1,0:T(8,128)}, f32[32,512]{1,0:T(8,128)S(1)}, f32[2,32,512]{2,1,0:T(8,128)S(1)}, f32[32,512]{1,0:T(8,128)S(1)}, f32[32,512]{1,0:T(8,128)S(1)}) custom-call(s32[1]{0:T(128)} %bitcast.1.core_ref, f32[32,512]{1,0:T(8,128)S(1)} %collective-permute-done.below, f32[32,512]{1,0:T(8,128)S(1)} %collective-permute-done.1.above, ...), custom_call_target="tpu_custom_call" | custom-call | tf_op jit(solution)/shard_map/apply_operator/pallas_call | solution.py:99
  24.6 3.7 %collective-permute-start.4 = (f32[32,512]{1,0:T(8,128)S(1)}, f32[32,512]{1,0:T(8,128)S(1)}, u32[]{:S(2)}, u32[]{:S(2)}) collective-permute-start(f32[32,512]{1,0:T(8,128)S(1)} %get-tuple-element.66), channel_id=1, source_target_pairs={{0,8},{4,12},{8,16},{12,20},{16,24},{20,28},{24,32},{28,36},{32,40... | collective-permute-start | bytes 196616 | tf_op jit(solution)/shard_map/ppermute | solution.py:262
  29.6 3.9 %collective-permute-done.5 = f32[32,512]{1,0:T(8,128)S(1)} collective-permute-done((f32[32,512]{1,0:T(8,128)S(1)}, f32[32,512]{1,0:T(8,128)S(1)}, u32[]{:S(2)}, u32[]{:S(2)}) %collective-permute-start.5) | collective-permute-done | bytes 65568 | tf_op jit(solution)/shard_map/ppermute | solution.py:262
  33.5 9.3 %all_to_all.60 = f32[4,32,512]{2,1,0:T(8,128)S(1)} all-to-all(f32[4,32,512]{2,1,0:T(8,128)S(1)} %broadcast_in_dim.20), channel_id=1, replica_groups=mesh['y'=8,'z'=8,'core'=2,'x'=4] {'x'}, dimensions={0} | all-to-all | bytes 524288 | tf_op jit(solution)/shard_map/all_to_all | solution.py:272
  43.9 12.8 %all-to-all-start.1 = ((f32[16,8,128]{2,1,0:T(8,128)}), f32[16,8,128]{2,1,0:T(8,128)S(1)}, u32[]{:S(2)}, u32[]{:S(2)}) async-start(f32[16,8,128]{2,1,0:T(8,128)} %bitcast.7), calls=%async_computation.1 | async-start | bytes 131072 | tf_op jit(solution)/shard_map/all_to_all | solution.py:278
  56.7 3.2 %collective-permute-start.6 = (f32[32,512]{1,0:T(8,128)S(1)}, f32[32,512]{1,0:T(8,128)S(1)}, u32[]{:S(2)}, u32[]{:S(2)}) collective-permute-start(f32[32,512]{1,0:T(8,128)S(1)} %fusion.9.own), channel_id=1, source_target_pairs={{0,8},{4,12},{8,16},{12,20},{16,24},{20,28},{24,32},{28,36},{32,40... | collective-permute-start | bytes 196616 | tf_op jit(solution)/shard_map/ppermute | solution.py:262
  61.2 3.2 %all-to-all-done.1 = f32[16,8,128]{2,1,0:T(8,128)S(1)} async-done(((f32[16,8,128]{2,1,0:T(8,128)}), f32[16,8,128]{2,1,0:T(8,128)S(1)}, u32[]{:S(2)}, u32[]{:S(2)}) %all-to-all-start.1) | async-done | bytes 65568 | tf_op jit(solution)/shard_map/all_to_all | solution.py:278
  65.0 3.7 %collective-permute-start.8 = (f32[2,32,512]{2,1,0:T(8,128)S(1)}, f32[2,32,512]{2,1,0:T(8,128)S(1)}, u32[]{:S(2)}, u32[]{:S(2)}) collective-permute-start(f32[2,32,512]{2,1,0:T(8,128)S(1)} %pad_maximum_fusion.1), channel_id=1, source_target_pairs={{0,4},{4,0},{1,5},{5,1},{2,6},{6,2},{3,7},{7,3},{8,12},{12,8},{9,1... | collective-permute-start | bytes 393224 | tf_op jit(solution)/shard_map/ppermute | solution.py:266
  71.4 3.1 %apply_operator.4 = (f32[32,512]{1,0:T(8,128)}, f32[32,512]{1,0:T(8,128)S(1)}, f32[2,32,512]{2,1,0:T(8,128)S(1)}, f32[32,512]{1,0:T(8,128)S(1)}, f32[32,512]{1,0:T(8,128)S(1)}) custom-call(s32[1]{0:T(128)} %bitcast.1.core_ref, f32[32,512]{1,0:T(8,128)S(1)} %collective-permute-done.6.below, f32[32,512]{1,0:T(8,128)S(1)} %collective-permute-done.7.above, ...), custom_call_target="tpu_custom_call" | custom-call | tf_op jit(solution)/shard_map/apply_operator/pallas_call | solution.py:99
  77.8 3.1 %collective-permute-start.10 = (f32[32,512]{1,0:T(8,128)S(1)}, f32[32,512]{1,0:T(8,128)S(1)}, u32[]{:S(2)}, u32[]{:S(2)}) collective-permute-start(f32[32,512]{1,0:T(8,128)S(1)} %get-tuple-element.64), channel_id=1, source_target_pairs={{0,8},{4,12},{8,16},{12,20},{16,24},{20,28},{24,32},{28,36},{32,40... | collective-permute-start | bytes 196616 | tf_op jit(solution)/shard_map/ppermute | solution.py:262
  82.2 19.7 %all_to_all.61 = f32[8,8,128]{2,1,0:T(8,128)S(1)} all-to-all(f32[8,8,128]{2,1,0:T(8,128)S(1)} %broadcast_in_dim.21), channel_id=1, replica_groups=mesh['y'=8,'z'=8,'core'=2,'x'=4] {'y'}, dimensions={0} | all-to-all | bytes 65536 | tf_op jit(solution)/shard_map/all_to_all | solution.py:272
  102.6 5.4 %all-to-all-start.3 = ((f32[16,8,128]{2,1,0:T(8,128)}), f32[16,8,128]{2,1,0:T(8,128)S(1)}, u32[]{:S(2)}, u32[]{:S(2)}) async-start(f32[16,8,128]{2,1,0:T(8,128)} %broadcast_in_dim.22), calls=%async_computation.3 | async-start | bytes 131072 | tf_op jit(solution)/shard_map/all_to_all | solution.py:272
  108.0 7.8 %all-to-all-done.3 = f32[16,8,128]{2,1,0:T(8,128)S(1)} async-done(((f32[16,8,128]{2,1,0:T(8,128)}), f32[16,8,128]{2,1,0:T(8,128)S(1)}, u32[]{:S(2)}, u32[]{:S(2)}) %all-to-all-start.3) | async-done | bytes 65568 | tf_op jit(solution)/shard_map/all_to_all | solution.py:272
  116.5 3.4 %all-to-all-start.4 = ((f32[4,1,32,512]{3,2,1,0:T(8,128)}), f32[4,1,32,512]{3,2,1,0:T(8,128)S(1)}, u32[]{:S(2)}, u32[]{:S(2)}) async-start(f32[4,1,32,512]{3,2,1,0:T(8,128)} %broadcast_in_dim.24), calls=%async_computation.4 | async-start | bytes 524288 | tf_op jit(solution)/shard_map/all_to_all | solution.py:272
  119.9 4.7 %cholesky_inverse.2.inverse_ref = f32[128,128]{1,0:T(8,128)S(1)} custom-call(f32[128,128]{1,0:T(8,128)S(1)} %bitcast.69), custom_call_target="tpu_custom_call" | custom-call | tf_op jit(solution)/shard_map/cholesky_inverse/pallas_call | solution.py:227
  128.0 4.3 %all-to-all-start.5 = ((f32[16,8,128]{2,1,0:T(8,128)}), f32[16,8,128]{2,1,0:T(8,128)S(1)}, u32[]{:S(2)}, u32[]{:S(2)}) async-start(f32[16,8,128]{2,1,0:T(8,128)} %bitcast.13), calls=%async_computation.5 | async-start | bytes 131072 | tf_op jit(solution)/shard_map/all_to_all | solution.py:278
  132.3 3.3 %collective-permute-start.12 = (f32[32,512]{1,0:T(8,128)S(1)}, f32[32,512]{1,0:T(8,128)S(1)}, u32[]{:S(2)}, u32[]{:S(2)}) collective-permute-start(f32[32,512]{1,0:T(8,128)S(1)} %get-tuple-element.49.own), channel_id=1, source_target_pairs={{0,8},{4,12},{8,16},{12,20},{16,24},{20,28},{24,32},{28,36},{32,40... | collective-permute-start | bytes 196616 | tf_op jit(solution)/shard_map/ppermute | solution.py:262
  136.9 3.3 %all-to-all-done.5 = f32[16,8,128]{2,1,0:T(8,128)S(1)} async-done(((f32[16,8,128]{2,1,0:T(8,128)}), f32[16,8,128]{2,1,0:T(8,128)S(1)}, u32[]{:S(2)}, u32[]{:S(2)}) %all-to-all-start.5) | async-done | bytes 65568 | tf_op jit(solution)/shard_map/all_to_all | solution.py:278
  140.6 3.9 %collective-permute-start.14 = (f32[2,32,512]{2,1,0:T(8,128)S(1)}, f32[2,32,512]{2,1,0:T(8,128)S(1)}, u32[]{:S(2)}, u32[]{:S(2)}) collective-permute-start(f32[2,32,512]{2,1,0:T(8,128)S(1)} %pad_maximum_fusion.2), channel_id=1, source_target_pairs={{0,4},{4,0},{1,5},{5,1},{2,6},{6,2},{3,7},{7,3},{8,12},{12,8},{9,1... | collective-permute-start | bytes 393224 | tf_op jit(solution)/shard_map/ppermute | solution.py:266
  152.9 3.1 %collective-permute-start.16 = (f32[32,512]{1,0:T(8,128)S(1)}, f32[32,512]{1,0:T(8,128)S(1)}, u32[]{:S(2)}, u32[]{:S(2)}) collective-permute-start(f32[32,512]{1,0:T(8,128)S(1)} %get-tuple-element.62), channel_id=1, source_target_pairs={{0,8},{4,12},{8,16},{12,20},{16,24},{20,28},{24,32},{28,36},{32,40... | collective-permute-start | bytes 196616 | tf_op jit(solution)/shard_map/ppermute | solution.py:262
  157.3 14.2 %all_to_all.62 = f32[8,8,128]{2,1,0:T(8,128)S(1)} all-to-all(f32[8,8,128]{2,1,0:T(8,128)S(1)} %broadcast_in_dim.25), channel_id=1, replica_groups=mesh['y'=8,'z'=8,'core'=2,'x'=4] {'y'}, dimensions={0} | all-to-all | bytes 65536 | tf_op jit(solution)/shard_map/all_to_all | solution.py:272
  172.2 5.7 %all-to-all-start.7 = ((f32[16,8,128]{2,1,0:T(8,128)}), f32[16,8,128]{2,1,0:T(8,128)S(1)}, u32[]{:S(2)}, u32[]{:S(2)}) async-start(f32[16,8,128]{2,1,0:T(8,128)} %broadcast_in_dim.26), calls=%async_computation.7 | async-start | bytes 131072 | tf_op jit(solution)/shard_map/all_to_all | solution.py:272
  177.9 7.7 %all-to-all-done.7 = f32[16,8,128]{2,1,0:T(8,128)S(1)} async-done(((f32[16,8,128]{2,1,0:T(8,128)}), f32[16,8,128]{2,1,0:T(8,128)S(1)}, u32[]{:S(2)}, u32[]{:S(2)}) %all-to-all-start.7) | async-done | bytes 65568 | tf_op jit(solution)/shard_map/all_to_all | solution.py:272
  186.5 3.5 %all-to-all-start.8 = ((f32[4,2,32,512]{3,2,1,0:T(8,128)}), f32[4,2,32,512]{3,2,1,0:T(8,128)S(1)}, u32[]{:S(2)}, u32[]{:S(2)}) async-start(f32[4,2,32,512]{3,2,1,0:T(8,128)} %broadcast_in_dim.27), calls=%async_computation.8 | async-start | bytes 1048576 | tf_op jit(solution)/shard_map/all_to_all | solution.py:272
  190.0 4.7 %cholesky_inverse.3.inverse_ref = f32[128,128]{1,0:T(8,128)S(1)} custom-call(f32[128,128]{1,0:T(8,128)S(1)} %bitcast.70), custom_call_target="tpu_custom_call" | custom-call | tf_op jit(solution)/shard_map/cholesky_inverse/pallas_call | solution.py:227
  194.7 4.7 %all-to-all-done.8.raw_ref = f32[4,2,32,512]{3,2,1,0:T(8,128)S(1)} async-done(((f32[4,2,32,512]{3,2,1,0:T(8,128)}), f32[4,2,32,512]{3,2,1,0:T(8,128)S(1)}, u32[]{:S(2)}, u32[]{:S(2)}) %all-to-all-start.8) | async-done | bytes 524320 | tf_op jit(solution)/shard_map/all_to_all | solution.py:272
  200.7 11.2 %all_to_all.63 = f32[16,8,128]{2,1,0:T(8,128)S(1)} all-to-all(f32[16,8,128]{2,1,0:T(8,128)S(1)} %bitcast.72), channel_id=1, replica_groups=mesh['y'=8,'z'=8,'core'=2,'x'=4] {'z','core'}, dimensions={0} | all-to-all | bytes 131072 | tf_op jit(solution)/shard_map/all_to_all | solution.py:278
  211.9 9.2 %all_to_all.64 = f32[8,8,128]{2,1,0:T(8,128)S(1)} all-to-all(f32[8,8,128]{2,1,0:T(8,128)S(1)} %broadcast_in_dim.28), channel_id=1, replica_groups=mesh['y'=8,'z'=8,'core'=2,'x'=4] {'y'}, dimensions={0} | all-to-all | bytes 65536 | tf_op jit(solution)/shard_map/all_to_all | solution.py:272
  221.2 11.5 %all_to_all.65 = f32[16,8,128]{2,1,0:T(8,128)S(1)} all-to-all(f32[16,8,128]{2,1,0:T(8,128)S(1)} %broadcast_in_dim.29), channel_id=1, replica_groups=mesh['y'=8,'z'=8,'core'=2,'x'=4] {'z','core'}, dimensions={0} | all-to-all | bytes 131072 | tf_op jit(solution)/shard_map/all_to_all | solution.py:272
  232.7 5.5 %whiten.1 = f32[32,512]{1,0:T(8,128)} custom-call(s32[1]{0:T(128)} %bitcast.place_ref, f32[128,128]{1,0:T(8,128)S(1)} %bitcast.71, f32[128,512]{1,0:T(8,128)S(1)} %get-tuple-element.60.all_ref), custom_call_target="tpu_custom_call" | custom-call | tf_op jit(solution)/shard_map/whiten/pallas_call | solution.py:248
  (72 shorter events, 40.5 us)
Async XLA Ops:
  0.6 10.8 %copy-start.3 = (f32[32,512]{1,0:T(8,128)S(1)}, f32[32,512]{1,0:T(8,128)}, u32[]{:S(2)}) copy-start(f32[32,512]{1,0:T(8,128)} %own.1) | copy-start | bytes 196612
  0.6 10.6 %collective-permute-start = (f32[32,512]{1,0:T(8,128)}, f32[32,512]{1,0:T(8,128)S(1)}, u32[]{:S(2)}, u32[]{:S(2)}) collective-permute-start(f32[32,512]{1,0:T(8,128)} %own.1), channel_id=1, source_target_pairs={{0,8},{4,12},{8,16},{12,20},{16,24},{20,28},{24,32},{28,36},{32,40... | collective-permute-start | bytes 196616 | tf_op jit(solution)/shard_map/ppermute | solution.py:262
  5.6 5.9 %collective-permute-start.1 = (f32[32,512]{1,0:T(8,128)}, f32[32,512]{1,0:T(8,128)S(1)}, u32[]{:S(2)}, u32[]{:S(2)}) collective-permute-start(f32[32,512]{1,0:T(8,128)} %own.1), channel_id=1, source_target_pairs={{8,0},{12,4},{16,8},{20,12},{24,16},{28,20},{32,24},{36,28},{40,32... | collective-permute-start | bytes 196616 | tf_op jit(solution)/shard_map/ppermute | solution.py:262
  6.9 0.7 copy-start.4
  7.6 0.7 copy-start.5
  11.3 10.1 %copy-start = (bf16[5,512,512]{2,1,0:T(8,128)(2,1)}, bf16[5,512,512]{2,1,0:T(8,128)(2,1)S(1)}, u32[]{:S(2)}) copy-start(bf16[5,512,512]{2,1,0:T(8,128)(2,1)S(1)} %get-tuple-element.44.low) | copy-start | bytes 7864324
  11.5 6.7 %collective-permute-start.2 = (f32[2,32,512]{2,1,0:T(8,128)S(1)}, f32[2,32,512]{2,1,0:T(8,128)S(1)}, u32[]{:S(2)}, u32[]{:S(2)}) collective-permute-start(f32[2,32,512]{2,1,0:T(8,128)S(1)} %pad_maximum_fusion), channel_id=1, source_target_pairs={{0,4},{4,0},{1,5},{5,1},{2,6},{6,2},{3,7},{7,3},{8,12},{12,8},{9,1... | collective-permute-start | bytes 393224 | tf_op jit(solution)/shard_map/ppermute | solution.py:266
  21.3 3.2 %collective-permute-start.3 = (f32[2,32,512]{2,1,0:T(8,128)S(1)}, f32[2,32,512]{2,1,0:T(8,128)S(1)}, u32[]{:S(2)}, u32[]{:S(2)}) collective-permute-start(f32[2,32,512]{2,1,0:T(8,128)S(1)} %get-tuple-element.37), channel_id=1, source_target_pairs={{0,4},{4,0},{1,5},{5,1},{2,6},{6,2},{3,7},{7,3},{8,12},{12,8},{9,1... | collective-permute-start | bytes 393224 | tf_op jit(solution)/shard_map/ppermute | solution.py:266
  24.6 5.0 %collective-permute-start.4 = (f32[32,512]{1,0:T(8,128)S(1)}, f32[32,512]{1,0:T(8,128)S(1)}, u32[]{:S(2)}, u32[]{:S(2)}) collective-permute-start(f32[32,512]{1,0:T(8,128)S(1)} %get-tuple-element.66), channel_id=1, source_target_pairs={{0,8},{4,12},{8,16},{12,20},{16,24},{20,28},{24,32},{28,36},{32,40... | collective-permute-start | bytes 196616 | tf_op jit(solution)/shard_map/ppermute | solution.py:262
  28.3 5.2 %collective-permute-start.5 = (f32[32,512]{1,0:T(8,128)S(1)}, f32[32,512]{1,0:T(8,128)S(1)}, u32[]{:S(2)}, u32[]{:S(2)}) collective-permute-start(f32[32,512]{1,0:T(8,128)S(1)} %get-tuple-element.67), channel_id=1, source_target_pairs={{8,0},{12,4},{16,8},{20,12},{24,16},{28,20},{32,24},{36,28},{40,32... | collective-permute-start | bytes 196616 | tf_op jit(solution)/shard_map/ppermute | solution.py:262
  43.9 20.6 %all-to-all-start.1 = ((f32[16,8,128]{2,1,0:T(8,128)}), f32[16,8,128]{2,1,0:T(8,128)S(1)}, u32[]{:S(2)}, u32[]{:S(2)}) async-start(f32[16,8,128]{2,1,0:T(8,128)} %bitcast.7), calls=%async_computation.1 | async-start | bytes 131072 | tf_op jit(solution)/shard_map/all_to_all | solution.py:278
  56.7 7.8 %collective-permute-start.6 = (f32[32,512]{1,0:T(8,128)S(1)}, f32[32,512]{1,0:T(8,128)S(1)}, u32[]{:S(2)}, u32[]{:S(2)}) collective-permute-start(f32[32,512]{1,0:T(8,128)S(1)} %fusion.9.own), channel_id=1, source_target_pairs={{0,8},{4,12},{8,16},{12,20},{16,24},{20,28},{24,32},{28,36},{32,40... | collective-permute-start | bytes 196616 | tf_op jit(solution)/shard_map/ppermute | solution.py:262
  59.9 5.0 %collective-permute-start.7 = (f32[32,512]{1,0:T(8,128)S(1)}, f32[32,512]{1,0:T(8,128)S(1)}, u32[]{:S(2)}, u32[]{:S(2)}) collective-permute-start(f32[32,512]{1,0:T(8,128)S(1)} %fusion.9.own), channel_id=1, source_target_pairs={{8,0},{12,4},{16,8},{20,12},{24,16},{28,20},{32,24},{36,28},{40,32... | collective-permute-start | bytes 196616 | tf_op jit(solution)/shard_map/ppermute | solution.py:262
  65.0 4.7 %collective-permute-start.8 = (f32[2,32,512]{2,1,0:T(8,128)S(1)}, f32[2,32,512]{2,1,0:T(8,128)S(1)}, u32[]{:S(2)}, u32[]{:S(2)}) collective-permute-start(f32[2,32,512]{2,1,0:T(8,128)S(1)} %pad_maximum_fusion.1), channel_id=1, source_target_pairs={{0,4},{4,0},{1,5},{5,1},{2,6},{6,2},{3,7},{7,3},{8,12},{12,8},{9,1... | collective-permute-start | bytes 393224 | tf_op jit(solution)/shard_map/ppermute | solution.py:266
  69.7 1.7 copy-start.1
  74.5 3.2 %collective-permute-start.9 = (f32[2,32,512]{2,1,0:T(8,128)S(1)}, f32[2,32,512]{2,1,0:T(8,128)S(1)}, u32[]{:S(2)}, u32[]{:S(2)}) collective-permute-start(f32[2,32,512]{2,1,0:T(8,128)S(1)} %get-tuple-element.46), channel_id=1, source_target_pairs={{0,4},{4,0},{1,5},{5,1},{2,6},{6,2},{3,7},{7,3},{8,12},{12,8},{9,1... | collective-permute-start | bytes 393224 | tf_op jit(solution)/shard_map/ppermute | solution.py:266
  77.8 30.2 %collective-permute-start.10 = (f32[32,512]{1,0:T(8,128)S(1)}, f32[32,512]{1,0:T(8,128)S(1)}, u32[]{:S(2)}, u32[]{:S(2)}) collective-permute-start(f32[32,512]{1,0:T(8,128)S(1)} %get-tuple-element.64), channel_id=1, source_target_pairs={{0,8},{4,12},{8,16},{12,20},{16,24},{20,28},{24,32},{28,36},{32,40... | collective-permute-start | bytes 196616 | tf_op jit(solution)/shard_map/ppermute | solution.py:262
  80.9 27.1 %collective-permute-start.11 = (f32[32,512]{1,0:T(8,128)S(1)}, f32[32,512]{1,0:T(8,128)S(1)}, u32[]{:S(2)}, u32[]{:S(2)}) collective-permute-start(f32[32,512]{1,0:T(8,128)S(1)} %get-tuple-element.65), channel_id=1, source_target_pairs={{8,0},{12,4},{16,8},{20,12},{24,16},{28,20},{32,24},{36,28},{40,32... | collective-permute-start | bytes 196616 | tf_op jit(solution)/shard_map/ppermute | solution.py:262
  102.6 13.2 %all-to-all-start.3 = ((f32[16,8,128]{2,1,0:T(8,128)}), f32[16,8,128]{2,1,0:T(8,128)S(1)}, u32[]{:S(2)}, u32[]{:S(2)}) async-start(f32[16,8,128]{2,1,0:T(8,128)} %broadcast_in_dim.22), calls=%async_computation.3 | async-start | bytes 131072 | tf_op jit(solution)/shard_map/all_to_all | solution.py:272
  116.5 10.0 %all-to-all-start.4 = ((f32[4,1,32,512]{3,2,1,0:T(8,128)}), f32[4,1,32,512]{3,2,1,0:T(8,128)S(1)}, u32[]{:S(2)}, u32[]{:S(2)}) async-start(f32[4,1,32,512]{3,2,1,0:T(8,128)} %broadcast_in_dim.24), calls=%async_computation.4 | async-start | bytes 524288 | tf_op jit(solution)/shard_map/all_to_all | solution.py:272
  128.0 12.2 %all-to-all-start.5 = ((f32[16,8,128]{2,1,0:T(8,128)}), f32[16,8,128]{2,1,0:T(8,128)S(1)}, u32[]{:S(2)}, u32[]{:S(2)}) async-start(f32[16,8,128]{2,1,0:T(8,128)} %bitcast.13), calls=%async_computation.5 | async-start | bytes 131072 | tf_op jit(solution)/shard_map/all_to_all | solution.py:278
  132.3 7.9 %collective-permute-start.12 = (f32[32,512]{1,0:T(8,128)S(1)}, f32[32,512]{1,0:T(8,128)S(1)}, u32[]{:S(2)}, u32[]{:S(2)}) collective-permute-start(f32[32,512]{1,0:T(8,128)S(1)} %get-tuple-element.49.own), channel_id=1, source_target_pairs={{0,8},{4,12},{8,16},{12,20},{16,24},{20,28},{24,32},{28,36},{32,40... | collective-permute-start | bytes 196616 | tf_op jit(solution)/shard_map/ppermute | solution.py:262
  135.6 5.0 %collective-permute-start.13 = (f32[32,512]{1,0:T(8,128)S(1)}, f32[32,512]{1,0:T(8,128)S(1)}, u32[]{:S(2)}, u32[]{:S(2)}) collective-permute-start(f32[32,512]{1,0:T(8,128)S(1)} %get-tuple-element.49.own), channel_id=1, source_target_pairs={{8,0},{12,4},{16,8},{20,12},{24,16},{28,20},{32,24},{36,28},{40,32... | collective-permute-start | bytes 196616 | tf_op jit(solution)/shard_map/ppermute | solution.py:262
  140.6 4.7 %collective-permute-start.14 = (f32[2,32,512]{2,1,0:T(8,128)S(1)}, f32[2,32,512]{2,1,0:T(8,128)S(1)}, u32[]{:S(2)}, u32[]{:S(2)}) collective-permute-start(f32[2,32,512]{2,1,0:T(8,128)S(1)} %pad_maximum_fusion.2), channel_id=1, source_target_pairs={{0,4},{4,0},{1,5},{5,1},{2,6},{6,2},{3,7},{7,3},{8,12},{12,8},{9,1... | collective-permute-start | bytes 393224 | tf_op jit(solution)/shard_map/ppermute | solution.py:266
  145.3 1.7 copy-start.2
  149.7 3.2 %collective-permute-start.15 = (f32[2,32,512]{2,1,0:T(8,128)S(1)}, f32[2,32,512]{2,1,0:T(8,128)S(1)}, u32[]{:S(2)}, u32[]{:S(2)}) collective-permute-start(f32[2,32,512]{2,1,0:T(8,128)S(1)} %get-tuple-element.55), channel_id=1, source_target_pairs={{0,4},{4,0},{1,5},{5,1},{2,6},{6,2},{3,7},{7,3},{8,12},{12,8},{9,1... | collective-permute-start | bytes 393224 | tf_op jit(solution)/shard_map/ppermute | solution.py:266
  152.9 25.0 %collective-permute-start.16 = (f32[32,512]{1,0:T(8,128)S(1)}, f32[32,512]{1,0:T(8,128)S(1)}, u32[]{:S(2)}, u32[]{:S(2)}) collective-permute-start(f32[32,512]{1,0:T(8,128)S(1)} %get-tuple-element.62), channel_id=1, source_target_pairs={{0,8},{4,12},{8,16},{12,20},{16,24},{20,28},{24,32},{28,36},{32,40... | collective-permute-start | bytes 196616 | tf_op jit(solution)/shard_map/ppermute | solution.py:262
  156.0 21.8 %collective-permute-start.17 = (f32[32,512]{1,0:T(8,128)S(1)}, f32[32,512]{1,0:T(8,128)S(1)}, u32[]{:S(2)}, u32[]{:S(2)}) collective-permute-start(f32[32,512]{1,0:T(8,128)S(1)} %get-tuple-element.63), channel_id=1, source_target_pairs={{8,0},{12,4},{16,8},{20,12},{24,16},{28,20},{32,24},{36,28},{40,32... | collective-permute-start | bytes 196616 | tf_op jit(solution)/shard_map/ppermute | solution.py:262
  172.2 13.4 %all-to-all-start.7 = ((f32[16,8,128]{2,1,0:T(8,128)}), f32[16,8,128]{2,1,0:T(8,128)S(1)}, u32[]{:S(2)}, u32[]{:S(2)}) async-start(f32[16,8,128]{2,1,0:T(8,128)} %broadcast_in_dim.26), calls=%async_computation.7 | async-start | bytes 131072 | tf_op jit(solution)/shard_map/all_to_all | solution.py:272
  186.5 12.9 %all-to-all-start.8 = ((f32[4,2,32,512]{3,2,1,0:T(8,128)}), f32[4,2,32,512]{3,2,1,0:T(8,128)S(1)}, u32[]{:S(2)}, u32[]{:S(2)}) async-start(f32[4,2,32,512]{3,2,1,0:T(8,128)} %broadcast_in_dim.27), calls=%async_computation.8 | async-start | bytes 1048576 | tf_op jit(solution)/shard_map/all_to_all | solution.py:272

commit v4 on v3

--- a/solution.py
+++ b/solution.py
@@ -6,6 +6,7 @@
 from jax.experimental import pallas as pl
 from jax.experimental.pallas import tpu as pltpu
 from jax.sharding import Mesh, PartitionSpec as P
+
 
 REACH = 2
 GROUPS = 2 * REACH + 1
@@ -295,7 +296,8 @@
     bands = operator_band(tile_values, tile_rows, tile_cols, row_width)
 
     def operator_pass(vectors, beside=()):
-        below, above = shifted(vectors, 2), shifted(vectors, -2)
+        below = shifted(vectors, 2)
+        above = shifted(vectors, -2)
         below, above, *beside = lax.optimization_barrier((below, above, *beside))
         got = swapped(jnp.stack([vectors, jnp.where(first, above, below)]))
         images, kept, crossing, down, up = apply_operator(core, below, above, vectors, got, *bands)
@@ -305,15 +307,17 @@
         return images, kept + got[0] + shifted(up, 2) + shifted(down, -2), beside
 
     images, pulled, bands = operator_pass(start_vectors, bands)
-    all_vectors = spread(pulled, "x").reshape(all_count, row_width)
-    share = scattered(gram_share(all_vectors))
+    gram = None
     for iteration in range(1, ITERS):
         last = iteration == ITERS - 1
+        if gram is None:
+            gram = gram_share(spread(pulled, "x").reshape(all_count, row_width))
+        share = scattered(gram)
         images, ahead, taken = operator_pass(pulled, [share])
         inverse = cholesky_inverse(gathered(*taken))
         raw = spread(jnp.stack([ahead, images] if last else [ahead]), "x")
         all_vectors, pulled, gram = advance(place, inverse, raw, scale)
-        share = scattered(gram)
+    share = scattered(gram)
     images = pulled
     vectors = whiten(place, gathered(share), all_vectors, own, scale)
     return (vectors, images)

time: 240 us -> 239 us (level)
  no operation moved by 1% of the time
where the time goes in v4:
time: 239 us; the launch traced here: 238 us
  starting transfers between devices  84.4 us (35%)
  blocking collectives  75 us (31%)
  waiting for transfers between devices  39 us (16%)
  Pallas kernels  30.7 us (13%)
  local copies, waits for them, and re-layouts  7.73 us (3%)
    all_to_all x5, blocking collectives, spread(): return lax.all_to_all(copies, axes, 0, 0)  63.8 us
    ppermute x12, starting transfers between devices, shifted(): lax.ppermute(value, ROWS, [(source, source + steps) for source in range(l...  29.1 us
    all_to_all x4, waiting for transfers between devices, spread(): return lax.all_to_all(copies, axes, 0, 0)  22.1 us
    ppermute x6, starting transfers between devices, swapped(): return lax.ppermute(value, 'core', [(0, 1), (1, 0)])  20.2 us
    all_to_all x4, starting transfers between devices, spread(): return lax.all_to_all(copies, axes, 0, 0)  17.9 us
    all_to_all x2, starting transfers between devices, scattered(): lax.all_to_all(whole.reshape(line, size // line, size), ('z', 'core'), 0, 0)  17.2 us
    all_to_all x1, blocking collectives, scattered(): lax.all_to_all(whole.reshape(line, size // line, size), ('z', 'core'), 0, 0)  11.2 us
    pallas_call x2, Pallas kernels, cholesky_inverse(): pl.pallas_call(functools.partial(inverse_kernel, panel=4), in_specs=[vmem...  9.4 us
  transfers between devices with their start and end apart: 24, of which 16 were waited for; matrix products, arithmetic and copies ran while one was open for 1% of the time, Pallas kernels for 5%

profile of v4, /device:TPU:1, one launch (start us, length us, event | category | flops | bytes accessed | tf_op | source)
XLA Modules:
  0.0 238.1 jit_solution(5270723921006007885)
XLA Ops:
  0.6 4.9 %collective-permute-start = (f32[32,512]{1,0:T(8,128)}, f32[32,512]{1,0:T(8,128)S(1)}, u32[]{:S(2)}, u32[]{:S(2)}) collective-permute-start(f32[32,512]{1,0:T(8,128)} %own.1), channel_id=1, source_target_pairs={{0,8},{4,12},{8,16},{12,20},{16,24},{20,28},{24,32},{28,36},{32,40... | collective-permute-start | bytes 196616 | tf_op jit(solution)/shard_map/ppermute | solution.py:263
  8.2 3.1 %operator_band.1 = (bf16[5,512,512]{2,1,0:T(8,128)(2,1)S(1)}, bf16[5,512,512]{2,1,0:T(8,128)(2,1)S(1)}) custom-call(s32[15]{0:T(128)S(1)} %copy-done.4, s32[15]{0:T(128)S(1)} %copy-done.5, f32[15,256,256]{2,1,0:T(8,128)} %tiles_hbm.1), custom_call_target="tpu_custom_call" | custom-call | tf_op jit(solution)/shard_map/operator_band/pallas_call | solution.py:56
  11.5 5.7 %collective-permute-start.2 = (f32[2,32,512]{2,1,0:T(8,128)S(1)}, f32[2,32,512]{2,1,0:T(8,128)S(1)}, u32[]{:S(2)}, u32[]{:S(2)}) collective-permute-start(f32[2,32,512]{2,1,0:T(8,128)S(1)} %pad_maximum_fusion), channel_id=1, source_target_pairs={{0,4},{4,0},{1,5},{5,1},{2,6},{6,2},{3,7},{7,3},{8,12},{12,8},{9,1... | collective-permute-start | bytes 393224 | tf_op jit(solution)/shard_map/ppermute | solution.py:267
  18.2 3.1 %apply_operator.3 = (f32[32,512]{1,0:T(8,128)}, f32[32,512]{1,0:T(8,128)S(1)}, f32[2,32,512]{2,1,0:T(8,128)S(1)}, f32[32,512]{1,0:T(8,128)S(1)}, f32[32,512]{1,0:T(8,128)S(1)}) custom-call(s32[1]{0:T(128)} %bitcast.1.core_ref, f32[32,512]{1,0:T(8,128)S(1)} %collective-permute-done.below, f32[32,512]{1,0:T(8,128)S(1)} %collective-permute-done.1.above, ...), custom_call_target="tpu_custom_call" | custom-call | tf_op jit(solution)/shard_map/apply_operator/pallas_call | solution.py:100
  24.6 3.7 %collective-permute-start.4 = (f32[32,512]{1,0:T(8,128)S(1)}, f32[32,512]{1,0:T(8,128)S(1)}, u32[]{:S(2)}, u32[]{:S(2)}) collective-permute-start(f32[32,512]{1,0:T(8,128)S(1)} %get-tuple-element.66), channel_id=1, source_target_pairs={{0,8},{4,12},{8,16},{12,20},{16,24},{20,28},{24,32},{28,36},{32,40... | collective-permute-start | bytes 196616 | tf_op jit(solution)/shard_map/ppermute | solution.py:263
  29.6 3.8 %collective-permute-done.5 = f32[32,512]{1,0:T(8,128)S(1)} collective-permute-done((f32[32,512]{1,0:T(8,128)S(1)}, f32[32,512]{1,0:T(8,128)S(1)}, u32[]{:S(2)}, u32[]{:S(2)}) %collective-permute-start.5) | collective-permute-done | bytes 65568 | tf_op jit(solution)/shard_map/ppermute | solution.py:263
  33.5 9.3 %all_to_all.60 = f32[4,32,512]{2,1,0:T(8,128)S(1)} all-to-all(f32[4,32,512]{2,1,0:T(8,128)S(1)} %broadcast_in_dim.20), channel_id=1, replica_groups=mesh['y'=8,'z'=8,'core'=2,'x'=4] {'x'}, dimensions={0} | all-to-all | bytes 524288 | tf_op jit(solution)/shard_map/all_to_all | solution.py:273
  43.9 12.9 %all-to-all-start.1 = ((f32[16,8,128]{2,1,0:T(8,128)}), f32[16,8,128]{2,1,0:T(8,128)S(1)}, u32[]{:S(2)}, u32[]{:S(2)}) async-start(f32[16,8,128]{2,1,0:T(8,128)} %bitcast.7), calls=%async_computation.1 | async-start | bytes 131072 | tf_op jit(solution)/shard_map/all_to_all | solution.py:279
  56.8 3.2 %collective-permute-start.6 = (f32[32,512]{1,0:T(8,128)S(1)}, f32[32,512]{1,0:T(8,128)S(1)}, u32[]{:S(2)}, u32[]{:S(2)}) collective-permute-start(f32[32,512]{1,0:T(8,128)S(1)} %fusion.9.own), channel_id=1, source_target_pairs={{0,8},{4,12},{8,16},{12,20},{16,24},{20,28},{24,32},{28,36},{32,40... | collective-permute-start | bytes 196616 | tf_op jit(solution)/shard_map/ppermute | solution.py:263
  61.3 3.2 %all-to-all-done.1 = f32[16,8,128]{2,1,0:T(8,128)S(1)} async-done(((f32[16,8,128]{2,1,0:T(8,128)}), f32[16,8,128]{2,1,0:T(8,128)S(1)}, u32[]{:S(2)}, u32[]{:S(2)}) %all-to-all-start.1) | async-done | bytes 65568 | tf_op jit(solution)/shard_map/all_to_all | solution.py:279
  65.1 3.7 %collective-permute-start.8 = (f32[2,32,512]{2,1,0:T(8,128)S(1)}, f32[2,32,512]{2,1,0:T(8,128)S(1)}, u32[]{:S(2)}, u32[]{:S(2)}) collective-permute-start(f32[2,32,512]{2,1,0:T(8,128)S(1)} %pad_maximum_fusion.1), channel_id=1, source_target_pairs={{0,4},{4,0},{1,5},{5,1},{2,6},{6,2},{3,7},{7,3},{8,12},{12,8},{9,1... | collective-permute-start | bytes 393224 | tf_op jit(solution)/shard_map/ppermute | solution.py:267
  71.5 3.1 %apply_operator.4 = (f32[32,512]{1,0:T(8,128)}, f32[32,512]{1,0:T(8,128)S(1)}, f32[2,32,512]{2,1,0:T(8,128)S(1)}, f32[32,512]{1,0:T(8,128)S(1)}, f32[32,512]{1,0:T(8,128)S(1)}) custom-call(s32[1]{0:T(128)} %bitcast.1.core_ref, f32[32,512]{1,0:T(8,128)S(1)} %collective-permute-done.6.below, f32[32,512]{1,0:T(8,128)S(1)} %collective-permute-done.7.above, ...), custom_call_target="tpu_custom_call" | custom-call | tf_op jit(solution)/shard_map/apply_operator/pallas_call | solution.py:100
  82.3 19.4 %all_to_all.61 = f32[8,8,128]{2,1,0:T(8,128)S(1)} all-to-all(f32[8,8,128]{2,1,0:T(8,128)S(1)} %broadcast_in_dim.21), channel_id=1, replica_groups=mesh['y'=8,'z'=8,'core'=2,'x'=4] {'y'}, dimensions={0} | all-to-all | bytes 65536 | tf_op jit(solution)/shard_map/all_to_all | solution.py:273
  102.4 5.4 %all-to-all-start.3 = ((f32[16,8,128]{2,1,0:T(8,128)}), f32[16,8,128]{2,1,0:T(8,128)S(1)}, u32[]{:S(2)}, u32[]{:S(2)}) async-start(f32[16,8,128]{2,1,0:T(8,128)} %broadcast_in_dim.22), calls=%async_computation.3 | async-start | bytes 131072 | tf_op jit(solution)/shard_map/all_to_all | solution.py:273
  107.8 7.8 %all-to-all-done.3 = f32[16,8,128]{2,1,0:T(8,128)S(1)} async-done(((f32[16,8,128]{2,1,0:T(8,128)}), f32[16,8,128]{2,1,0:T(8,128)S(1)}, u32[]{:S(2)}, u32[]{:S(2)}) %all-to-all-start.3) | async-done | bytes 65568 | tf_op jit(solution)/shard_map/all_to_all | solution.py:273
  116.3 3.4 %all-to-all-start.4 = ((f32[4,1,32,512]{3,2,1,0:T(8,128)}), f32[4,1,32,512]{3,2,1,0:T(8,128)S(1)}, u32[]{:S(2)}, u32[]{:S(2)}) async-start(f32[4,1,32,512]{3,2,1,0:T(8,128)} %broadcast_in_dim.24), calls=%async_computation.4 | async-start | bytes 524288 | tf_op jit(solution)/shard_map/all_to_all | solution.py:273
  119.8 4.7 %cholesky_inverse.2.inverse_ref = f32[128,128]{1,0:T(8,128)S(1)} custom-call(f32[128,128]{1,0:T(8,128)S(1)} %bitcast.69), custom_call_target="tpu_custom_call" | custom-call | tf_op jit(solution)/shard_map/cholesky_inverse/pallas_call | solution.py:228
  127.8 4.3 %all-to-all-start.5 = ((f32[16,8,128]{2,1,0:T(8,128)}), f32[16,8,128]{2,1,0:T(8,128)S(1)}, u32[]{:S(2)}, u32[]{:S(2)}) async-start(f32[16,8,128]{2,1,0:T(8,128)} %bitcast.13), calls=%async_computation.5 | async-start | bytes 131072 | tf_op jit(solution)/shard_map/all_to_all | solution.py:279
  132.1 3.3 %collective-permute-start.12 = (f32[32,512]{1,0:T(8,128)S(1)}, f32[32,512]{1,0:T(8,128)S(1)}, u32[]{:S(2)}, u32[]{:S(2)}) collective-permute-start(f32[32,512]{1,0:T(8,128)S(1)} %get-tuple-element.49.own), channel_id=1, source_target_pairs={{0,8},{4,12},{8,16},{12,20},{16,24},{20,28},{24,32},{28,36},{32,40... | collective-permute-start | bytes 196616 | tf_op jit(solution)/shard_map/ppermute | solution.py:263
  136.7 3.3 %all-to-all-done.5 = f32[16,8,128]{2,1,0:T(8,128)S(1)} async-done(((f32[16,8,128]{2,1,0:T(8,128)}), f32[16,8,128]{2,1,0:T(8,128)S(1)}, u32[]{:S(2)}, u32[]{:S(2)}) %all-to-all-start.5) | async-done | bytes 65568 | tf_op jit(solution)/shard_map/all_to_all | solution.py:279
  140.4 3.9 %collective-permute-start.14 = (f32[2,32,512]{2,1,0:T(8,128)S(1)}, f32[2,32,512]{2,1,0:T(8,128)S(1)}, u32[]{:S(2)}, u32[]{:S(2)}) collective-permute-start(f32[2,32,512]{2,1,0:T(8,128)S(1)} %pad_maximum_fusion.2), channel_id=1, source_target_pairs={{0,4},{4,0},{1,5},{5,1},{2,6},{6,2},{3,7},{7,3},{8,12},{12,8},{9,1... | collective-permute-start | bytes 393224 | tf_op jit(solution)/shard_map/ppermute | solution.py:267
  152.8 3.1 %collective-permute-start.16 = (f32[32,512]{1,0:T(8,128)S(1)}, f32[32,512]{1,0:T(8,128)S(1)}, u32[]{:S(2)}, u32[]{:S(2)}) collective-permute-start(f32[32,512]{1,0:T(8,128)S(1)} %get-tuple-element.62), channel_id=1, source_target_pairs={{0,8},{4,12},{8,16},{12,20},{16,24},{20,28},{24,32},{28,36},{32,40... | collective-permute-start | bytes 196616 | tf_op jit(solution)/shard_map/ppermute | solution.py:263
  157.2 14.2 %all_to_all.62 = f32[8,8,128]{2,1,0:T(8,128)S(1)} all-to-all(f32[8,8,128]{2,1,0:T(8,128)S(1)} %broadcast_in_dim.25), channel_id=1, replica_groups=mesh['y'=8,'z'=8,'core'=2,'x'=4] {'y'}, dimensions={0} | all-to-all | bytes 65536 | tf_op jit(solution)/shard_map/all_to_all | solution.py:273
  172.0 5.7 %all-to-all-start.7 = ((f32[16,8,128]{2,1,0:T(8,128)}), f32[16,8,128]{2,1,0:T(8,128)S(1)}, u32[]{:S(2)}, u32[]{:S(2)}) async-start(f32[16,8,128]{2,1,0:T(8,128)} %broadcast_in_dim.26), calls=%async_computation.7 | async-start | bytes 131072 | tf_op jit(solution)/shard_map/all_to_all | solution.py:273
  177.8 7.7 %all-to-all-done.7 = f32[16,8,128]{2,1,0:T(8,128)S(1)} async-done(((f32[16,8,128]{2,1,0:T(8,128)}), f32[16,8,128]{2,1,0:T(8,128)S(1)}, u32[]{:S(2)}, u32[]{:S(2)}) %all-to-all-start.7) | async-done | bytes 65568 | tf_op jit(solution)/shard_map/all_to_all | solution.py:273
  186.4 3.5 %all-to-all-start.8 = ((f32[4,2,32,512]{3,2,1,0:T(8,128)}), f32[4,2,32,512]{3,2,1,0:T(8,128)S(1)}, u32[]{:S(2)}, u32[]{:S(2)}) async-start(f32[4,2,32,512]{3,2,1,0:T(8,128)} %broadcast_in_dim.27), calls=%async_computation.8 | async-start | bytes 1048576 | tf_op jit(solution)/shard_map/all_to_all | solution.py:273
  189.8 4.7 %cholesky_inverse.3.inverse_ref = f32[128,128]{1,0:T(8,128)S(1)} custom-call(f32[128,128]{1,0:T(8,128)S(1)} %bitcast.70), custom_call_target="tpu_custom_call" | custom-call | tf_op jit(solution)/shard_map/cholesky_inverse/pallas_call | solution.py:228
  194.5 4.7 %all-to-all-done.8.raw_ref = f32[4,2,32,512]{3,2,1,0:T(8,128)S(1)} async-done(((f32[4,2,32,512]{3,2,1,0:T(8,128)}), f32[4,2,32,512]{3,2,1,0:T(8,128)S(1)}, u32[]{:S(2)}, u32[]{:S(2)}) %all-to-all-start.8) | async-done | bytes 524320 | tf_op jit(solution)/shard_map/all_to_all | solution.py:273
  200.6 11.2 %all_to_all.63 = f32[16,8,128]{2,1,0:T(8,128)S(1)} all-to-all(f32[16,8,128]{2,1,0:T(8,128)S(1)} %bitcast.72), channel_id=1, replica_groups=mesh['y'=8,'z'=8,'core'=2,'x'=4] {'z','core'}, dimensions={0} | all-to-all | bytes 131072 | tf_op jit(solution)/shard_map/all_to_all | solution.py:279
  211.8 9.2 %all_to_all.64 = f32[8,8,128]{2,1,0:T(8,128)S(1)} all-to-all(f32[8,8,128]{2,1,0:T(8,128)S(1)} %broadcast_in_dim.28), channel_id=1, replica_groups=mesh['y'=8,'z'=8,'core'=2,'x'=4] {'y'}, dimensions={0} | all-to-all | bytes 65536 | tf_op jit(solution)/shard_map/all_to_all | solution.py:273
  221.0 11.5 %all_to_all.65 = f32[16,8,128]{2,1,0:T(8,128)S(1)} all-to-all(f32[16,8,128]{2,1,0:T(8,128)S(1)} %broadcast_in_dim.29), channel_id=1, replica_groups=mesh['y'=8,'z'=8,'core'=2,'x'=4] {'z','core'}, dimensions={0} | all-to-all | bytes 131072 | tf_op jit(solution)/shard_map/all_to_all | solution.py:273
  232.6 5.5 %whiten.1 = f32[32,512]{1,0:T(8,128)} custom-call(s32[1]{0:T(128)} %bitcast.place_ref, f32[128,128]{1,0:T(8,128)S(1)} %bitcast.71, f32[128,512]{1,0:T(8,128)S(1)} %get-tuple-element.60.all_ref), custom_call_target="tpu_custom_call" | custom-call | tf_op jit(solution)/shard_map/whiten/pallas_call | solution.py:249
  (72 shorter events, 40.5 us)
Async XLA Ops:
  0.6 10.8 %copy-start.3 = (f32[32,512]{1,0:T(8,128)S(1)}, f32[32,512]{1,0:T(8,128)}, u32[]{:S(2)}) copy-start(f32[32,512]{1,0:T(8,128)} %own.1) | copy-start | bytes 196612
  0.6 10.7 %collective-permute-start = (f32[32,512]{1,0:T(8,128)}, f32[32,512]{1,0:T(8,128)S(1)}, u32[]{:S(2)}, u32[]{:S(2)}) collective-permute-start(f32[32,512]{1,0:T(8,128)} %own.1), channel_id=1, source_target_pairs={{0,8},{4,12},{8,16},{12,20},{16,24},{20,28},{24,32},{28,36},{32,40... | collective-permute-start | bytes 196616 | tf_op jit(solution)/shard_map/ppermute | solution.py:263
  5.6 5.9 %collective-permute-start.1 = (f32[32,512]{1,0:T(8,128)}, f32[32,512]{1,0:T(8,128)S(1)}, u32[]{:S(2)}, u32[]{:S(2)}) collective-permute-start(f32[32,512]{1,0:T(8,128)} %own.1), channel_id=1, source_target_pairs={{8,0},{12,4},{16,8},{20,12},{24,16},{28,20},{32,24},{36,28},{40,32... | collective-permute-start | bytes 196616 | tf_op jit(solution)/shard_map/ppermute | solution.py:263
  6.9 0.7 copy-start.4
  7.6 0.7 copy-start.5
  11.3 10.0 %copy-start = (bf16[5,512,512]{2,1,0:T(8,128)(2,1)}, bf16[5,512,512]{2,1,0:T(8,128)(2,1)S(1)}, u32[]{:S(2)}) copy-start(bf16[5,512,512]{2,1,0:T(8,128)(2,1)S(1)} %get-tuple-element.44.low) | copy-start | bytes 7864324
  11.5 6.7 %collective-permute-start.2 = (f32[2,32,512]{2,1,0:T(8,128)S(1)}, f32[2,32,512]{2,1,0:T(8,128)S(1)}, u32[]{:S(2)}, u32[]{:S(2)}) collective-permute-start(f32[2,32,512]{2,1,0:T(8,128)S(1)} %pad_maximum_fusion), channel_id=1, source_target_pairs={{0,4},{4,0},{1,5},{5,1},{2,6},{6,2},{3,7},{7,3},{8,12},{12,8},{9,1... | collective-permute-start | bytes 393224 | tf_op jit(solution)/shard_map/ppermute | solution.py:267
  21.3 3.2 %collective-permute-start.3 = (f32[2,32,512]{2,1,0:T(8,128)S(1)}, f32[2,32,512]{2,1,0:T(8,128)S(1)}, u32[]{:S(2)}, u32[]{:S(2)}) collective-permute-start(f32[2,32,512]{2,1,0:T(8,128)S(1)} %get-tuple-element.37), channel_id=1, source_target_pairs={{0,4},{4,0},{1,5},{5,1},{2,6},{6,2},{3,7},{7,3},{8,12},{12,8},{9,1... | collective-permute-start | bytes 393224 | tf_op jit(solution)/shard_map/ppermute | solution.py:267
  24.6 5.0 %collective-permute-start.4 = (f32[32,512]{1,0:T(8,128)S(1)}, f32[32,512]{1,0:T(8,128)S(1)}, u32[]{:S(2)}, u32[]{:S(2)}) collective-permute-start(f32[32,512]{1,0:T(8,128)S(1)} %get-tuple-element.66), channel_id=1, source_target_pairs={{0,8},{4,12},{8,16},{12,20},{16,24},{20,28},{24,32},{28,36},{32,40... | collective-permute-start | bytes 196616 | tf_op jit(solution)/shard_map/ppermute | solution.py:263
  28.3 5.2 %collective-permute-start.5 = (f32[32,512]{1,0:T(8,128)S(1)}, f32[32,512]{1,0:T(8,128)S(1)}, u32[]{:S(2)}, u32[]{:S(2)}) collective-permute-start(f32[32,512]{1,0:T(8,128)S(1)} %get-tuple-element.67), channel_id=1, source_target_pairs={{8,0},{12,4},{16,8},{20,12},{24,16},{28,20},{32,24},{36,28},{40,32... | collective-permute-start | bytes 196616 | tf_op jit(solution)/shard_map/ppermute | solution.py:263
  43.9 20.7 %all-to-all-start.1 = ((f32[16,8,128]{2,1,0:T(8,128)}), f32[16,8,128]{2,1,0:T(8,128)S(1)}, u32[]{:S(2)}, u32[]{:S(2)}) async-start(f32[16,8,128]{2,1,0:T(8,128)} %bitcast.7), calls=%async_computation.1 | async-start | bytes 131072 | tf_op jit(solution)/shard_map/all_to_all | solution.py:279
  56.8 7.8 %collective-permute-start.6 = (f32[32,512]{1,0:T(8,128)S(1)}, f32[32,512]{1,0:T(8,128)S(1)}, u32[]{:S(2)}, u32[]{:S(2)}) collective-permute-start(f32[32,512]{1,0:T(8,128)S(1)} %fusion.9.own), channel_id=1, source_target_pairs={{0,8},{4,12},{8,16},{12,20},{16,24},{20,28},{24,32},{28,36},{32,40... | collective-permute-start | bytes 196616 | tf_op jit(solution)/shard_map/ppermute | solution.py:263
  60.0 5.0 %collective-permute-start.7 = (f32[32,512]{1,0:T(8,128)S(1)}, f32[32,512]{1,0:T(8,128)S(1)}, u32[]{:S(2)}, u32[]{:S(2)}) collective-permute-start(f32[32,512]{1,0:T(8,128)S(1)} %fusion.9.own), channel_id=1, source_target_pairs={{8,0},{12,4},{16,8},{20,12},{24,16},{28,20},{32,24},{36,28},{40,32... | collective-permute-start | bytes 196616 | tf_op jit(solution)/shard_map/ppermute | solution.py:263
  65.1 4.7 %collective-permute-start.8 = (f32[2,32,512]{2,1,0:T(8,128)S(1)}, f32[2,32,512]{2,1,0:T(8,128)S(1)}, u32[]{:S(2)}, u32[]{:S(2)}) collective-permute-start(f32[2,32,512]{2,1,0:T(8,128)S(1)} %pad_maximum_fusion.1), channel_id=1, source_target_pairs={{0,4},{4,0},{1,5},{5,1},{2,6},{6,2},{3,7},{7,3},{8,12},{12,8},{9,1... | collective-permute-start | bytes 393224 | tf_op jit(solution)/shard_map/ppermute | solution.py:267
  69.8 1.7 copy-start.1
  74.7 3.2 %collective-permute-start.9 = (f32[2,32,512]{2,1,0:T(8,128)S(1)}, f32[2,32,512]{2,1,0:T(8,128)S(1)}, u32[]{:S(2)}, u32[]{:S(2)}) collective-permute-start(f32[2,32,512]{2,1,0:T(8,128)S(1)} %get-tuple-element.46), channel_id=1, source_target_pairs={{0,4},{4,0},{1,5},{5,1},{2,6},{6,2},{3,7},{7,3},{8,12},{12,8},{9,1... | collective-permute-start | bytes 393224 | tf_op jit(solution)/shard_map/ppermute | solution.py:267
  77.9 29.9 %collective-permute-start.10 = (f32[32,512]{1,0:T(8,128)S(1)}, f32[32,512]{1,0:T(8,128)S(1)}, u32[]{:S(2)}, u32[]{:S(2)}) collective-permute-start(f32[32,512]{1,0:T(8,128)S(1)} %get-tuple-element.64), channel_id=1, source_target_pairs={{0,8},{4,12},{8,16},{12,20},{16,24},{20,28},{24,32},{28,36},{32,40... | collective-permute-start | bytes 196616 | tf_op jit(solution)/shard_map/ppermute | solution.py:263
  81.0 26.8 %collective-permute-start.11 = (f32[32,512]{1,0:T(8,128)S(1)}, f32[32,512]{1,0:T(8,128)S(1)}, u32[]{:S(2)}, u32[]{:S(2)}) collective-permute-start(f32[32,512]{1,0:T(8,128)S(1)} %get-tuple-element.65), channel_id=1, source_target_pairs={{8,0},{12,4},{16,8},{20,12},{24,16},{28,20},{32,24},{36,28},{40,32... | collective-permute-start | bytes 196616 | tf_op jit(solution)/shard_map/ppermute | solution.py:263
  102.4 13.2 %all-to-all-start.3 = ((f32[16,8,128]{2,1,0:T(8,128)}), f32[16,8,128]{2,1,0:T(8,128)S(1)}, u32[]{:S(2)}, u32[]{:S(2)}) async-start(f32[16,8,128]{2,1,0:T(8,128)} %broadcast_in_dim.22), calls=%async_computation.3 | async-start | bytes 131072 | tf_op jit(solution)/shard_map/all_to_all | solution.py:273
  116.3 10.0 %all-to-all-start.4 = ((f32[4,1,32,512]{3,2,1,0:T(8,128)}), f32[4,1,32,512]{3,2,1,0:T(8,128)S(1)}, u32[]{:S(2)}, u32[]{:S(2)}) async-start(f32[4,1,32,512]{3,2,1,0:T(8,128)} %broadcast_in_dim.24), calls=%async_computation.4 | async-start | bytes 524288 | tf_op jit(solution)/shard_map/all_to_all | solution.py:273
  127.8 12.2 %all-to-all-start.5 = ((f32[16,8,128]{2,1,0:T(8,128)}), f32[16,8,128]{2,1,0:T(8,128)S(1)}, u32[]{:S(2)}, u32[]{:S(2)}) async-start(f32[16,8,128]{2,1,0:T(8,128)} %bitcast.13), calls=%async_computation.5 | async-start | bytes 131072 | tf_op jit(solution)/shard_map/all_to_all | solution.py:279
  132.1 7.9 %collective-permute-start.12 = (f32[32,512]{1,0:T(8,128)S(1)}, f32[32,512]{1,0:T(8,128)S(1)}, u32[]{:S(2)}, u32[]{:S(2)}) collective-permute-start(f32[32,512]{1,0:T(8,128)S(1)} %get-tuple-element.49.own), channel_id=1, source_target_pairs={{0,8},{4,12},{8,16},{12,20},{16,24},{20,28},{24,32},{28,36},{32,40... | collective-permute-start | bytes 196616 | tf_op jit(solution)/shard_map/ppermute | solution.py:263
  135.4 5.0 %collective-permute-start.13 = (f32[32,512]{1,0:T(8,128)S(1)}, f32[32,512]{1,0:T(8,128)S(1)}, u32[]{:S(2)}, u32[]{:S(2)}) collective-permute-start(f32[32,512]{1,0:T(8,128)S(1)} %get-tuple-element.49.own), channel_id=1, source_target_pairs={{8,0},{12,4},{16,8},{20,12},{24,16},{28,20},{32,24},{36,28},{40,32... | collective-permute-start | bytes 196616 | tf_op jit(solution)/shard_map/ppermute | solution.py:263
  140.4 4.7 %collective-permute-start.14 = (f32[2,32,512]{2,1,0:T(8,128)S(1)}, f32[2,32,512]{2,1,0:T(8,128)S(1)}, u32[]{:S(2)}, u32[]{:S(2)}) collective-permute-start(f32[2,32,512]{2,1,0:T(8,128)S(1)} %pad_maximum_fusion.2), channel_id=1, source_target_pairs={{0,4},{4,0},{1,5},{5,1},{2,6},{6,2},{3,7},{7,3},{8,12},{12,8},{9,1... | collective-permute-start | bytes 393224 | tf_op jit(solution)/shard_map/ppermute | solution.py:267
  145.1 1.7 copy-start.2
  149.5 3.2 %collective-permute-start.15 = (f32[2,32,512]{2,1,0:T(8,128)S(1)}, f32[2,32,512]{2,1,0:T(8,128)S(1)}, u32[]{:S(2)}, u32[]{:S(2)}) collective-permute-start(f32[2,32,512]{2,1,0:T(8,128)S(1)} %get-tuple-element.55), channel_id=1, source_target_pairs={{0,4},{4,0},{1,5},{5,1},{2,6},{6,2},{3,7},{7,3},{8,12},{12,8},{9,1... | collective-permute-start | bytes 393224 | tf_op jit(solution)/shard_map/ppermute | solution.py:267
  152.8 25.0 %collective-permute-start.16 = (f32[32,512]{1,0:T(8,128)S(1)}, f32[32,512]{1,0:T(8,128)S(1)}, u32[]{:S(2)}, u32[]{:S(2)}) collective-permute-start(f32[32,512]{1,0:T(8,128)S(1)} %get-tuple-element.62), channel_id=1, source_target_pairs={{0,8},{4,12},{8,16},{12,20},{16,24},{20,28},{24,32},{28,36},{32,40... | collective-permute-start | bytes 196616 | tf_op jit(solution)/shard_map/ppermute | solution.py:263
  155.9 21.8 %collective-permute-start.17 = (f32[32,512]{1,0:T(8,128)S(1)}, f32[32,512]{1,0:T(8,128)S(1)}, u32[]{:S(2)}, u32[]{:S(2)}) collective-permute-start(f32[32,512]{1,0:T(8,128)S(1)} %get-tuple-element.63), channel_id=1, source_target_pairs={{8,0},{12,4},{16,8},{20,12},{24,16},{28,20},{32,24},{36,28},{40,32... | collective-permute-start | bytes 196616 | tf_op jit(solution)/shard_map/ppermute | solution.py:263
  172.0 13.4 %all-to-all-start.7 = ((f32[16,8,128]{2,1,0:T(8,128)}), f32[16,8,128]{2,1,0:T(8,128)S(1)}, u32[]{:S(2)}, u32[]{:S(2)}) async-start(f32[16,8,128]{2,1,0:T(8,128)} %broadcast_in_dim.26), calls=%async_computation.7 | async-start | bytes 131072 | tf_op jit(solution)/shard_map/all_to_all | solution.py:273
  186.4 12.9 %all-to-all-start.8 = ((f32[4,2,32,512]{3,2,1,0:T(8,128)}), f32[4,2,32,512]{3,2,1,0:T(8,128)S(1)}, u32[]{:S(2)}, u32[]{:S(2)}) async-start(f32[4,2,32,512]{3,2,1,0:T(8,128)} %broadcast_in_dim.27), calls=%async_computation.8 | async-start | bytes 1048576 | tf_op jit(solution)/shard_map/all_to_all | solution.py:273

commit v5 on v3

--- a/solution.py
+++ b/solution.py
@@ -275,13 +275,13 @@
 def scattered(whole):
     size = whole.shape[0]
     line = lax.axis_size(("z", "core"))
-    return lax.all_to_all(whole.reshape(line, size // line, size), ("z", "core"), 0, 0).sum(axis=0)
+    share = lax.all_to_all(whole.reshape(line, size // line, size), ("z", "core"), 0, 0).sum(axis=0)
+    return spread(share, "y").sum(axis=0)
 
 
 def gathered(share):
     size = share.shape[1]
-    run = spread(share, "y").sum(axis=0)
-    return spread(run, ("z", "core")).reshape(size, size)
+    return spread(share, ("z", "core")).reshape(size, size)
 
 
 def body(tile_values, tile_rows, tile_cols, start_vectors):

time: 240 us -> 235 us (0.979)
  blocking collectives: 75.3 us -> 65.2 us
  starting transfers between devices: 84.3 us -> 90.5 us
    all_to_all x5, blocking collectives: 64.1 us -> 54 us  [spread(): return lax.all_to_all(copies, axes, 0, 0)]
    all_to_all x4, starting transfers between devices: 17.9 us -> 27 us  [spread(): return lax.all_to_all(copies, axes, 0, 0)]
    ppermute x12, starting transfers between devices: 29.1 us -> 25.6 us  [shifted(): lax.ppermute(value, ROWS, [(source, source + steps) for source in range(l...]
  transfers between devices with their start and end apart: 24 -> 24, of which waited for: 16 -> 14; matrix products, arithmetic and copies ran while one was open for 1% -> 1% of each run, Pallas kernels for 5% -> 5%
where the time goes in v5:
time: 235 us; the launch traced here: 233 us
  starting transfers between devices  90.5 us (39%)
  blocking collectives  65.2 us (28%)
  waiting for transfers between devices  38.2 us (16%)
  Pallas kernels  30.6 us (13%)
  local copies, waits for them, and re-layouts  7.73 us (3%)
    all_to_all x5, blocking collectives, spread(): return lax.all_to_all(copies, axes, 0, 0)  54 us
    all_to_all x4, starting transfers between devices, spread(): return lax.all_to_all(copies, axes, 0, 0)  27 us
    ppermute x12, starting transfers between devices, shifted(): lax.ppermute(value, ROWS, [(source, source + steps) for source in range(l...  25.6 us
    all_to_all x4, waiting for transfers between devices, spread(): return lax.all_to_all(copies, axes, 0, 0)  22 us
    ppermute x6, starting transfers between devices, swapped(): return lax.ppermute(value, 'core', [(0, 1), (1, 0)])  20.8 us
    all_to_all x2, starting transfers between devices, scattered(): lax.all_to_all(whole.reshape(line, size // line, size), ('z', 'core'), 0, 0)  17.1 us
    all_to_all x1, blocking collectives, scattered(): lax.all_to_all(whole.reshape(line, size // line, size), ('z', 'core'), 0, 0)  11.2 us
    pallas_call x2, Pallas kernels, cholesky_inverse(): pl.pallas_call(functools.partial(inverse_kernel, panel=4), in_specs=[vmem...  9.4 us
  transfers between devices with their start and end apart: 24, of which 14 were waited for; matrix products, arithmetic and copies ran while one was open for 1% of the time, Pallas kernels for 5%

profile of v5, /device:TPU:1, one launch (start us, length us, event | category | flops | bytes accessed | tf_op | source)
XLA Modules:
  0.0 233.5 jit_solution(12477427795398917071)
XLA Ops:
  0.6 4.9 %collective-permute-start = (f32[32,512]{1,0:T(8,128)}, f32[32,512]{1,0:T(8,128)S(1)}, u32[]{:S(2)}, u32[]{:S(2)}) collective-permute-start(f32[32,512]{1,0:T(8,128)} %own.1), channel_id=1, source_target_pairs={{0,8},{4,12},{8,16},{12,20},{16,24},{20,28},{24,32},{28,36},{32,40... | collective-permute-start | bytes 196616 | tf_op jit(solution)/shard_map/ppermute | solution.py:262
  8.2 3.0 %operator_band.1 = (bf16[5,512,512]{2,1,0:T(8,128)(2,1)S(1)}, bf16[5,512,512]{2,1,0:T(8,128)(2,1)S(1)}) custom-call(s32[15]{0:T(128)S(1)} %copy-done.4, s32[15]{0:T(128)S(1)} %copy-done.5, f32[15,256,256]{2,1,0:T(8,128)} %tiles_hbm.1), custom_call_target="tpu_custom_call" | custom-call | tf_op jit(solution)/shard_map/operator_band/pallas_call | solution.py:55
  11.5 5.7 %collective-permute-start.2 = (f32[2,32,512]{2,1,0:T(8,128)S(1)}, f32[2,32,512]{2,1,0:T(8,128)S(1)}, u32[]{:S(2)}, u32[]{:S(2)}) collective-permute-start(f32[2,32,512]{2,1,0:T(8,128)S(1)} %pad_maximum_fusion), channel_id=1, source_target_pairs={{0,4},{4,0},{1,5},{5,1},{2,6},{6,2},{3,7},{7,3},{8,12},{12,8},{9,1... | collective-permute-start | bytes 393224 | tf_op jit(solution)/shard_map/ppermute | solution.py:266
  18.2 3.1 %apply_operator.3 = (f32[32,512]{1,0:T(8,128)}, f32[32,512]{1,0:T(8,128)S(1)}, f32[2,32,512]{2,1,0:T(8,128)S(1)}, f32[32,512]{1,0:T(8,128)S(1)}, f32[32,512]{1,0:T(8,128)S(1)}) custom-call(s32[1]{0:T(128)} %bitcast.1.core_ref, f32[32,512]{1,0:T(8,128)S(1)} %collective-permute-done.below, f32[32,512]{1,0:T(8,128)S(1)} %collective-permute-done.1.above, ...), custom_call_target="tpu_custom_call" | custom-call | tf_op jit(solution)/shard_map/apply_operator/pallas_call | solution.py:99
  24.6 3.8 %collective-permute-start.4 = (f32[32,512]{1,0:T(8,128)S(1)}, f32[32,512]{1,0:T(8,128)S(1)}, u32[]{:S(2)}, u32[]{:S(2)}) collective-permute-start(f32[32,512]{1,0:T(8,128)S(1)} %get-tuple-element.66), channel_id=1, source_target_pairs={{0,8},{4,12},{8,16},{12,20},{16,24},{20,28},{24,32},{28,36},{32,40... | collective-permute-start | bytes 196616 | tf_op jit(solution)/shard_map/ppermute | solution.py:262
  29.7 3.8 %collective-permute-done.5 = f32[32,512]{1,0:T(8,128)S(1)} collective-permute-done((f32[32,512]{1,0:T(8,128)S(1)}, f32[32,512]{1,0:T(8,128)S(1)}, u32[]{:S(2)}, u32[]{:S(2)}) %collective-permute-start.5) | collective-permute-done | bytes 65568 | tf_op jit(solution)/shard_map/ppermute | solution.py:262
  33.5 9.3 %all_to_all.60 = f32[4,32,512]{2,1,0:T(8,128)S(1)} all-to-all(f32[4,32,512]{2,1,0:T(8,128)S(1)} %broadcast_in_dim.20), channel_id=1, replica_groups=mesh['y'=8,'z'=8,'core'=2,'x'=4] {'x'}, dimensions={0} | all-to-all | bytes 524288 | tf_op jit(solution)/shard_map/all_to_all | solution.py:272
  43.9 12.8 %all-to-all-start.1 = ((f32[16,8,128]{2,1,0:T(8,128)}), f32[16,8,128]{2,1,0:T(8,128)S(1)}, u32[]{:S(2)}, u32[]{:S(2)}) async-start(f32[16,8,128]{2,1,0:T(8,128)} %bitcast.7), calls=%async_computation.1 | async-start | bytes 131072 | tf_op jit(solution)/shard_map/all_to_all | solution.py:278
  56.7 3.2 %collective-permute-start.6 = (f32[32,512]{1,0:T(8,128)S(1)}, f32[32,512]{1,0:T(8,128)S(1)}, u32[]{:S(2)}, u32[]{:S(2)}) collective-permute-start(f32[32,512]{1,0:T(8,128)S(1)} %fusion.9.own), channel_id=1, source_target_pairs={{0,8},{4,12},{8,16},{12,20},{16,24},{20,28},{24,32},{28,36},{32,40... | collective-permute-start | bytes 196616 | tf_op jit(solution)/shard_map/ppermute | solution.py:262
  61.3 3.2 %all-to-all-done.1 = f32[16,8,128]{2,1,0:T(8,128)S(1)} async-done(((f32[16,8,128]{2,1,0:T(8,128)}), f32[16,8,128]{2,1,0:T(8,128)S(1)}, u32[]{:S(2)}, u32[]{:S(2)}) %all-to-all-start.1) | async-done | bytes 65568 | tf_op jit(solution)/shard_map/all_to_all | solution.py:278
  64.5 14.6 %all_to_all.61 = f32[8,8,128]{2,1,0:T(8,128)S(1)} all-to-all(f32[8,8,128]{2,1,0:T(8,128)S(1)} %broadcast_in_dim.21), channel_id=1, replica_groups=mesh['y'=8,'z'=8,'core'=2,'x'=4] {'y'}, dimensions={0} | all-to-all | bytes 65536 | tf_op jit(solution)/shard_map/all_to_all | solution.py:272
  79.2 4.0 %collective-permute-start.8 = (f32[2,32,512]{2,1,0:T(8,128)S(1)}, f32[2,32,512]{2,1,0:T(8,128)S(1)}, u32[]{:S(2)}, u32[]{:S(2)}) collective-permute-start(f32[2,32,512]{2,1,0:T(8,128)S(1)} %pad_maximum_fusion.1), channel_id=1, source_target_pairs={{0,4},{4,0},{1,5},{5,1},{2,6},{6,2},{3,7},{7,3},{8,12},{12,8},{9,1... | collective-permute-start | bytes 393224 | tf_op jit(solution)/shard_map/ppermute | solution.py:266
  85.9 3.1 %apply_operator.4 = (f32[32,512]{1,0:T(8,128)}, f32[32,512]{1,0:T(8,128)S(1)}, f32[2,32,512]{2,1,0:T(8,128)S(1)}, f32[32,512]{1,0:T(8,128)S(1)}, f32[32,512]{1,0:T(8,128)S(1)}) custom-call(s32[1]{0:T(128)} %bitcast.1.core_ref, f32[32,512]{1,0:T(8,128)S(1)} %collective-permute-done.6.below, f32[32,512]{1,0:T(8,128)S(1)} %collective-permute-done.7.above, ...), custom_call_target="tpu_custom_call" | custom-call | tf_op jit(solution)/shard_map/apply_operator/pallas_call | solution.py:99
  95.5 9.9 %all-to-all-start.3 = ((f32[16,8,128]{2,1,0:T(8,128)}), f32[16,8,128]{2,1,0:T(8,128)S(1)}, u32[]{:S(2)}, u32[]{:S(2)}) async-start(f32[16,8,128]{2,1,0:T(8,128)} %broadcast_in_dim.22), calls=%async_computation.3 | async-start | bytes 131072 | tf_op jit(solution)/shard_map/all_to_all | solution.py:272
  105.5 7.7 %all-to-all-done.3 = f32[16,8,128]{2,1,0:T(8,128)S(1)} async-done(((f32[16,8,128]{2,1,0:T(8,128)}), f32[16,8,128]{2,1,0:T(8,128)S(1)}, u32[]{:S(2)}, u32[]{:S(2)}) %all-to-all-start.3) | async-done | bytes 65568 | tf_op jit(solution)/shard_map/all_to_all | solution.py:272
  114.0 3.4 %all-to-all-start.4 = ((f32[4,1,32,512]{3,2,1,0:T(8,128)}), f32[4,1,32,512]{3,2,1,0:T(8,128)S(1)}, u32[]{:S(2)}, u32[]{:S(2)}) async-start(f32[4,1,32,512]{3,2,1,0:T(8,128)} %broadcast_in_dim.24), calls=%async_computation.4 | async-start | bytes 524288 | tf_op jit(solution)/shard_map/all_to_all | solution.py:272
  117.4 4.7 %cholesky_inverse.2.inverse_ref = f32[128,128]{1,0:T(8,128)S(1)} custom-call(f32[128,128]{1,0:T(8,128)S(1)} %bitcast.69), custom_call_target="tpu_custom_call" | custom-call | tf_op jit(solution)/shard_map/cholesky_inverse/pallas_call | solution.py:227
  125.5 4.3 %all-to-all-start.5 = ((f32[16,8,128]{2,1,0:T(8,128)}), f32[16,8,128]{2,1,0:T(8,128)S(1)}, u32[]{:S(2)}, u32[]{:S(2)}) async-start(f32[16,8,128]{2,1,0:T(8,128)} %bitcast.13), calls=%async_computation.5 | async-start | bytes 131072 | tf_op jit(solution)/shard_map/all_to_all | solution.py:278
  129.7 3.3 %collective-permute-start.12 = (f32[32,512]{1,0:T(8,128)S(1)}, f32[32,512]{1,0:T(8,128)S(1)}, u32[]{:S(2)}, u32[]{:S(2)}) collective-permute-start(f32[32,512]{1,0:T(8,128)S(1)} %get-tuple-element.49.own), channel_id=1, source_target_pairs={{0,8},{4,12},{8,16},{12,20},{16,24},{20,28},{24,32},{28,36},{32,40... | collective-permute-start | bytes 196616 | tf_op jit(solution)/shard_map/ppermute | solution.py:262
  134.3 3.3 %all-to-all-done.5 = f32[16,8,128]{2,1,0:T(8,128)S(1)} async-done(((f32[16,8,128]{2,1,0:T(8,128)}), f32[16,8,128]{2,1,0:T(8,128)S(1)}, u32[]{:S(2)}, u32[]{:S(2)}) %all-to-all-start.5) | async-done | bytes 65568 | tf_op jit(solution)/shard_map/all_to_all | solution.py:278
  137.7 9.3 %all_to_all.62 = f32[8,8,128]{2,1,0:T(8,128)S(1)} all-to-all(f32[8,8,128]{2,1,0:T(8,128)S(1)} %broadcast_in_dim.25), channel_id=1, replica_groups=mesh['y'=8,'z'=8,'core'=2,'x'=4] {'y'}, dimensions={0} | all-to-all | bytes 65536 | tf_op jit(solution)/shard_map/all_to_all | solution.py:272
  147.0 4.3 %collective-permute-start.14 = (f32[2,32,512]{2,1,0:T(8,128)S(1)}, f32[2,32,512]{2,1,0:T(8,128)S(1)}, u32[]{:S(2)}, u32[]{:S(2)}) collective-permute-start(f32[2,32,512]{2,1,0:T(8,128)S(1)} %pad_maximum_fusion.2), channel_id=1, source_target_pairs={{0,4},{4,0},{1,5},{5,1},{2,6},{6,2},{3,7},{7,3},{8,12},{12,8},{9,1... | collective-permute-start | bytes 393224 | tf_op jit(solution)/shard_map/ppermute | solution.py:266
  153.8 2.6 %apply_operator.5 = (f32[32,512]{1,0:T(8,128)S(1)}, f32[32,512]{1,0:T(8,128)S(1)}, f32[2,32,512]{2,1,0:T(8,128)S(1)}, f32[32,512]{1,0:T(8,128)S(1)}, f32[32,512]{1,0:T(8,128)S(1)}) custom-call(s32[1]{0:T(128)} %bitcast.1.core_ref, f32[32,512]{1,0:T(8,128)S(1)} %collective-permute-done.12.below, f32[32,512]{1,0:T(8,128)S(1)} %collective-permute-done.13.above, ...), custom_call_target="tpu_custom_call" | custom-call | tf_op jit(solution)/shard_map/apply_operator/pallas_call | solution.py:99
  163.0 10.2 %all-to-all-start.7 = ((f32[16,8,128]{2,1,0:T(8,128)}), f32[16,8,128]{2,1,0:T(8,128)S(1)}, u32[]{:S(2)}, u32[]{:S(2)}) async-start(f32[16,8,128]{2,1,0:T(8,128)} %broadcast_in_dim.26), calls=%async_computation.7 | async-start | bytes 131072 | tf_op jit(solution)/shard_map/all_to_all | solution.py:272
  173.2 7.7 %all-to-all-done.7 = f32[16,8,128]{2,1,0:T(8,128)S(1)} async-done(((f32[16,8,128]{2,1,0:T(8,128)}), f32[16,8,128]{2,1,0:T(8,128)S(1)}, u32[]{:S(2)}, u32[]{:S(2)}) %all-to-all-start.7) | async-done | bytes 65568 | tf_op jit(solution)/shard_map/all_to_all | solution.py:272
  181.8 3.5 %all-to-all-start.8 = ((f32[4,2,32,512]{3,2,1,0:T(8,128)}), f32[4,2,32,512]{3,2,1,0:T(8,128)S(1)}, u32[]{:S(2)}, u32[]{:S(2)}) async-start(f32[4,2,32,512]{3,2,1,0:T(8,128)} %broadcast_in_dim.27), calls=%async_computation.8 | async-start | bytes 1048576 | tf_op jit(solution)/shard_map/all_to_all | solution.py:272
  185.3 4.7 %cholesky_inverse.3.inverse_ref = f32[128,128]{1,0:T(8,128)S(1)} custom-call(f32[128,128]{1,0:T(8,128)S(1)} %bitcast.70), custom_call_target="tpu_custom_call" | custom-call | tf_op jit(solution)/shard_map/cholesky_inverse/pallas_call | solution.py:227
  190.0 4.7 %all-to-all-done.8.raw_ref = f32[4,2,32,512]{3,2,1,0:T(8,128)S(1)} async-done(((f32[4,2,32,512]{3,2,1,0:T(8,128)}), f32[4,2,32,512]{3,2,1,0:T(8,128)S(1)}, u32[]{:S(2)}, u32[]{:S(2)}) %all-to-all-start.8) | async-done | bytes 524320 | tf_op jit(solution)/shard_map/all_to_all | solution.py:272
  196.0 11.2 %all_to_all.63 = f32[16,8,128]{2,1,0:T(8,128)S(1)} all-to-all(f32[16,8,128]{2,1,0:T(8,128)S(1)} %bitcast.72), channel_id=1, replica_groups=mesh['y'=8,'z'=8,'core'=2,'x'=4] {'z','core'}, dimensions={0} | all-to-all | bytes 131072 | tf_op jit(solution)/shard_map/all_to_all | solution.py:278
  207.2 9.2 %all_to_all.64 = f32[8,8,128]{2,1,0:T(8,128)S(1)} all-to-all(f32[8,8,128]{2,1,0:T(8,128)S(1)} %broadcast_in_dim.28), channel_id=1, replica_groups=mesh['y'=8,'z'=8,'core'=2,'x'=4] {'y'}, dimensions={0} | all-to-all | bytes 65536 | tf_op jit(solution)/shard_map/all_to_all | solution.py:272
  216.5 11.5 %all_to_all.65 = f32[16,8,128]{2,1,0:T(8,128)S(1)} all-to-all(f32[16,8,128]{2,1,0:T(8,128)S(1)} %broadcast_in_dim.29), channel_id=1, replica_groups=mesh['y'=8,'z'=8,'core'=2,'x'=4] {'z','core'}, dimensions={0} | all-to-all | bytes 131072 | tf_op jit(solution)/shard_map/all_to_all | solution.py:272
  228.0 5.5 %whiten.1 = f32[32,512]{1,0:T(8,128)} custom-call(s32[1]{0:T(128)} %bitcast.place_ref, f32[128,128]{1,0:T(8,128)S(1)} %bitcast.71, f32[128,512]{1,0:T(8,128)S(1)} %get-tuple-element.60.all_ref), custom_call_target="tpu_custom_call" | custom-call | tf_op jit(solution)/shard_map/whiten/pallas_call | solution.py:248
  (72 shorter events, 36.6 us)
Async XLA Ops:
  0.6 10.8 %copy-start.3 = (f32[32,512]{1,0:T(8,128)S(1)}, f32[32,512]{1,0:T(8,128)}, u32[]{:S(2)}) copy-start(f32[32,512]{1,0:T(8,128)} %own.1) | copy-start | bytes 196612
  0.6 10.6 %collective-permute-start = (f32[32,512]{1,0:T(8,128)}, f32[32,512]{1,0:T(8,128)S(1)}, u32[]{:S(2)}, u32[]{:S(2)}) collective-permute-start(f32[32,512]{1,0:T(8,128)} %own.1), channel_id=1, source_target_pairs={{0,8},{4,12},{8,16},{12,20},{16,24},{20,28},{24,32},{28,36},{32,40... | collective-permute-start | bytes 196616 | tf_op jit(solution)/shard_map/ppermute | solution.py:262
  5.6 5.9 %collective-permute-start.1 = (f32[32,512]{1,0:T(8,128)}, f32[32,512]{1,0:T(8,128)S(1)}, u32[]{:S(2)}, u32[]{:S(2)}) collective-permute-start(f32[32,512]{1,0:T(8,128)} %own.1), channel_id=1, source_target_pairs={{8,0},{12,4},{16,8},{20,12},{24,16},{28,20},{32,24},{36,28},{40,32... | collective-permute-start | bytes 196616 | tf_op jit(solution)/shard_map/ppermute | solution.py:262
  6.9 0.7 copy-start.4
  7.6 0.7 copy-start.5
  11.3 10.1 %copy-start = (bf16[5,512,512]{2,1,0:T(8,128)(2,1)}, bf16[5,512,512]{2,1,0:T(8,128)(2,1)S(1)}, u32[]{:S(2)}) copy-start(bf16[5,512,512]{2,1,0:T(8,128)(2,1)S(1)} %get-tuple-element.44.low) | copy-start | bytes 7864324
  11.5 6.7 %collective-permute-start.2 = (f32[2,32,512]{2,1,0:T(8,128)S(1)}, f32[2,32,512]{2,1,0:T(8,128)S(1)}, u32[]{:S(2)}, u32[]{:S(2)}) collective-permute-start(f32[2,32,512]{2,1,0:T(8,128)S(1)} %pad_maximum_fusion), channel_id=1, source_target_pairs={{0,4},{4,0},{1,5},{5,1},{2,6},{6,2},{3,7},{7,3},{8,12},{12,8},{9,1... | collective-permute-start | bytes 393224 | tf_op jit(solution)/shard_map/ppermute | solution.py:266
  21.3 3.2 %collective-permute-start.3 = (f32[2,32,512]{2,1,0:T(8,128)S(1)}, f32[2,32,512]{2,1,0:T(8,128)S(1)}, u32[]{:S(2)}, u32[]{:S(2)}) collective-permute-start(f32[2,32,512]{2,1,0:T(8,128)S(1)} %get-tuple-element.37), channel_id=1, source_target_pairs={{0,4},{4,0},{1,5},{5,1},{2,6},{6,2},{3,7},{7,3},{8,12},{12,8},{9,1... | collective-permute-start | bytes 393224 | tf_op jit(solution)/shard_map/ppermute | solution.py:266
  24.6 5.1 %collective-permute-start.4 = (f32[32,512]{1,0:T(8,128)S(1)}, f32[32,512]{1,0:T(8,128)S(1)}, u32[]{:S(2)}, u32[]{:S(2)}) collective-permute-start(f32[32,512]{1,0:T(8,128)S(1)} %get-tuple-element.66), channel_id=1, source_target_pairs={{0,8},{4,12},{8,16},{12,20},{16,24},{20,28},{24,32},{28,36},{32,40... | collective-permute-start | bytes 196616 | tf_op jit(solution)/shard_map/ppermute | solution.py:262
  28.4 5.1 %collective-permute-start.5 = (f32[32,512]{1,0:T(8,128)S(1)}, f32[32,512]{1,0:T(8,128)S(1)}, u32[]{:S(2)}, u32[]{:S(2)}) collective-permute-start(f32[32,512]{1,0:T(8,128)S(1)} %get-tuple-element.67), channel_id=1, source_target_pairs={{8,0},{12,4},{16,8},{20,12},{24,16},{28,20},{32,24},{36,28},{40,32... | collective-permute-start | bytes 196616 | tf_op jit(solution)/shard_map/ppermute | solution.py:262
  43.9 20.6 %all-to-all-start.1 = ((f32[16,8,128]{2,1,0:T(8,128)}), f32[16,8,128]{2,1,0:T(8,128)S(1)}, u32[]{:S(2)}, u32[]{:S(2)}) async-start(f32[16,8,128]{2,1,0:T(8,128)} %bitcast.7), calls=%async_computation.1 | async-start | bytes 131072 | tf_op jit(solution)/shard_map/all_to_all | solution.py:278
  56.7 22.4 %collective-permute-start.6 = (f32[32,512]{1,0:T(8,128)S(1)}, f32[32,512]{1,0:T(8,128)S(1)}, u32[]{:S(2)}, u32[]{:S(2)}) collective-permute-start(f32[32,512]{1,0:T(8,128)S(1)} %fusion.9.own), channel_id=1, source_target_pairs={{0,8},{4,12},{8,16},{12,20},{16,24},{20,28},{24,32},{28,36},{32,40... | collective-permute-start | bytes 196616 | tf_op jit(solution)/shard_map/ppermute | solution.py:262
  60.0 19.2 %collective-permute-start.7 = (f32[32,512]{1,0:T(8,128)S(1)}, f32[32,512]{1,0:T(8,128)S(1)}, u32[]{:S(2)}, u32[]{:S(2)}) collective-permute-start(f32[32,512]{1,0:T(8,128)S(1)} %fusion.9.own), channel_id=1, source_target_pairs={{8,0},{12,4},{16,8},{20,12},{24,16},{28,20},{32,24},{36,28},{40,32... | collective-permute-start | bytes 196616 | tf_op jit(solution)/shard_map/ppermute | solution.py:262
  79.2 5.0 %collective-permute-start.8 = (f32[2,32,512]{2,1,0:T(8,128)S(1)}, f32[2,32,512]{2,1,0:T(8,128)S(1)}, u32[]{:S(2)}, u32[]{:S(2)}) collective-permute-start(f32[2,32,512]{2,1,0:T(8,128)S(1)} %pad_maximum_fusion.1), channel_id=1, source_target_pairs={{0,4},{4,0},{1,5},{5,1},{2,6},{6,2},{3,7},{7,3},{8,12},{12,8},{9,1... | collective-permute-start | bytes 393224 | tf_op jit(solution)/shard_map/ppermute | solution.py:266
  84.2 1.7 copy-start.1
  89.0 3.2 %collective-permute-start.9 = (f32[2,32,512]{2,1,0:T(8,128)S(1)}, f32[2,32,512]{2,1,0:T(8,128)S(1)}, u32[]{:S(2)}, u32[]{:S(2)}) collective-permute-start(f32[2,32,512]{2,1,0:T(8,128)S(1)} %get-tuple-element.46), channel_id=1, source_target_pairs={{0,4},{4,0},{1,5},{5,1},{2,6},{6,2},{3,7},{7,3},{8,12},{12,8},{9,1... | collective-permute-start | bytes 393224 | tf_op jit(solution)/shard_map/ppermute | solution.py:266
  92.3 13.2 %collective-permute-start.10 = (f32[32,512]{1,0:T(8,128)S(1)}, f32[32,512]{1,0:T(8,128)S(1)}, u32[]{:S(2)}, u32[]{:S(2)}) collective-permute-start(f32[32,512]{1,0:T(8,128)S(1)} %get-tuple-element.64), channel_id=1, source_target_pairs={{0,8},{4,12},{8,16},{12,20},{16,24},{20,28},{24,32},{28,36},{32,40... | collective-permute-start | bytes 196616 | tf_op jit(solution)/shard_map/ppermute | solution.py:262
  93.6 11.9 %collective-permute-start.11 = (f32[32,512]{1,0:T(8,128)S(1)}, f32[32,512]{1,0:T(8,128)S(1)}, u32[]{:S(2)}, u32[]{:S(2)}) collective-permute-start(f32[32,512]{1,0:T(8,128)S(1)} %get-tuple-element.65), channel_id=1, source_target_pairs={{8,0},{12,4},{16,8},{20,12},{24,16},{28,20},{32,24},{36,28},{40,32... | collective-permute-start | bytes 196616 | tf_op jit(solution)/shard_map/ppermute | solution.py:262
  95.5 17.7 %all-to-all-start.3 = ((f32[16,8,128]{2,1,0:T(8,128)}), f32[16,8,128]{2,1,0:T(8,128)S(1)}, u32[]{:S(2)}, u32[]{:S(2)}) async-start(f32[16,8,128]{2,1,0:T(8,128)} %broadcast_in_dim.22), calls=%async_computation.3 | async-start | bytes 131072 | tf_op jit(solution)/shard_map/all_to_all | solution.py:272
  114.0 10.0 %all-to-all-start.4 = ((f32[4,1,32,512]{3,2,1,0:T(8,128)}), f32[4,1,32,512]{3,2,1,0:T(8,128)S(1)}, u32[]{:S(2)}, u32[]{:S(2)}) async-start(f32[4,1,32,512]{3,2,1,0:T(8,128)} %broadcast_in_dim.24), calls=%async_computation.4 | async-start | bytes 524288 | tf_op jit(solution)/shard_map/all_to_all | solution.py:272
  125.5 12.2 %all-to-all-start.5 = ((f32[16,8,128]{2,1,0:T(8,128)}), f32[16,8,128]{2,1,0:T(8,128)S(1)}, u32[]{:S(2)}, u32[]{:S(2)}) async-start(f32[16,8,128]{2,1,0:T(8,128)} %bitcast.13), calls=%async_computation.5 | async-start | bytes 131072 | tf_op jit(solution)/shard_map/all_to_all | solution.py:278
  129.7 17.2 %collective-permute-start.12 = (f32[32,512]{1,0:T(8,128)S(1)}, f32[32,512]{1,0:T(8,128)S(1)}, u32[]{:S(2)}, u32[]{:S(2)}) collective-permute-start(f32[32,512]{1,0:T(8,128)S(1)} %get-tuple-element.49.own), channel_id=1, source_target_pairs={{0,8},{4,12},{8,16},{12,20},{16,24},{20,28},{24,32},{28,36},{32,40... | collective-permute-start | bytes 196616 | tf_op jit(solution)/shard_map/ppermute | solution.py:262
  133.0 13.9 %collective-permute-start.13 = (f32[32,512]{1,0:T(8,128)S(1)}, f32[32,512]{1,0:T(8,128)S(1)}, u32[]{:S(2)}, u32[]{:S(2)}) collective-permute-start(f32[32,512]{1,0:T(8,128)S(1)} %get-tuple-element.49.own), channel_id=1, source_target_pairs={{8,0},{12,4},{16,8},{20,12},{24,16},{28,20},{32,24},{36,28},{40,32... | collective-permute-start | bytes 196616 | tf_op jit(solution)/shard_map/ppermute | solution.py:262
  147.0 5.1 %collective-permute-start.14 = (f32[2,32,512]{2,1,0:T(8,128)S(1)}, f32[2,32,512]{2,1,0:T(8,128)S(1)}, u32[]{:S(2)}, u32[]{:S(2)}) collective-permute-start(f32[2,32,512]{2,1,0:T(8,128)S(1)} %pad_maximum_fusion.2), channel_id=1, source_target_pairs={{0,4},{4,0},{1,5},{5,1},{2,6},{6,2},{3,7},{7,3},{8,12},{12,8},{9,1... | collective-permute-start | bytes 393224 | tf_op jit(solution)/shard_map/ppermute | solution.py:266
  152.1 1.7 copy-start.2
  156.5 3.2 %collective-permute-start.15 = (f32[2,32,512]{2,1,0:T(8,128)S(1)}, f32[2,32,512]{2,1,0:T(8,128)S(1)}, u32[]{:S(2)}, u32[]{:S(2)}) collective-permute-start(f32[2,32,512]{2,1,0:T(8,128)S(1)} %get-tuple-element.55), channel_id=1, source_target_pairs={{0,4},{4,0},{1,5},{5,1},{2,6},{6,2},{3,7},{7,3},{8,12},{12,8},{9,1... | collective-permute-start | bytes 393224 | tf_op jit(solution)/shard_map/ppermute | solution.py:266
  159.7 13.4 %collective-permute-start.16 = (f32[32,512]{1,0:T(8,128)S(1)}, f32[32,512]{1,0:T(8,128)S(1)}, u32[]{:S(2)}, u32[]{:S(2)}) collective-permute-start(f32[32,512]{1,0:T(8,128)S(1)} %get-tuple-element.62), channel_id=1, source_target_pairs={{0,8},{4,12},{8,16},{12,20},{16,24},{20,28},{24,32},{28,36},{32,40... | collective-permute-start | bytes 196616 | tf_op jit(solution)/shard_map/ppermute | solution.py:262
  161.0 12.1 %collective-permute-start.17 = (f32[32,512]{1,0:T(8,128)S(1)}, f32[32,512]{1,0:T(8,128)S(1)}, u32[]{:S(2)}, u32[]{:S(2)}) collective-permute-start(f32[32,512]{1,0:T(8,128)S(1)} %get-tuple-element.63), channel_id=1, source_target_pairs={{8,0},{12,4},{16,8},{20,12},{24,16},{28,20},{32,24},{36,28},{40,32... | collective-permute-start | bytes 196616 | tf_op jit(solution)/shard_map/ppermute | solution.py:262
  163.0 18.0 %all-to-all-start.7 = ((f32[16,8,128]{2,1,0:T(8,128)}), f32[16,8,128]{2,1,0:T(8,128)S(1)}, u32[]{:S(2)}, u32[]{:S(2)}) async-start(f32[16,8,128]{2,1,0:T(8,128)} %broadcast_in_dim.26), calls=%async_computation.7 | async-start | bytes 131072 | tf_op jit(solution)/shard_map/all_to_all | solution.py:272
  181.8 12.9 %all-to-all-start.8 = ((f32[4,2,32,512]{3,2,1,0:T(8,128)}), f32[4,2,32,512]{3,2,1,0:T(8,128)S(1)}, u32[]{:S(2)}, u32[]{:S(2)}) async-start(f32[4,2,32,512]{3,2,1,0:T(8,128)} %broadcast_in_dim.27), calls=%async_computation.8 | async-start | bytes 1048576 | tf_op jit(solution)/shard_map/all_to_all | solution.py:272
